TPU v7x, 256 devices: a whole 4x4x8 slice. The times are simulated.
256 devices in a mesh: batch: 64 (over z, x, core), chan: 4 (over y).
Axes of the slice: x: 4, y: 4, z: 8, core: 2. Of those that a mesh axis runs over, the one named last changes fastest.
Arguments:
- monomers: bfloat16 [65536, 1280], P('batch', 'chan'), may hold values from -8 to 8
- keep_mask: int32 [2, 65536], P(None, 'batch'), may hold values 0 or 1
- lengths: int32 [128], P('batch'), may hold values from 256 to 512
- norm_gain: float32 [1280], replicated, may hold values from 0.5 to 1.5
- weight_a: bfloat16 [5, 1280, 1280], P(None, 'batch', 'chan'), may hold values from -0.078125 to 0.078125
- weight_b: bfloat16 [5, 1280, 512], P(None, 'chan', 'batch'), may hold values from -0.078125 to 0.078125
Outputs:
- whitened: float32 [2, 65536, 512], P(None, ('batch', 'chan'))
- pair_gap: float32 [65536], P(('batch', 'chan'))
All inputs are finite; a program needn't handle non-finite values. No bound on the sum of `keep_mask` on one device may be relied on, other than what follows from the above.
Results may differ from a plain program's by a relative error of at most 0.0007.
The roundings to bfloat16 on the way count: a program that leaves them out, or rounds other values in their place, can miss the bound.
Values may be sent and summed in bfloat16 or wider, within the bound.
A program may use at most 128 MiB of HBM per device.

v0:
```python
import jax
import jax.numpy as jnp
from jax import lax
from jax.sharding import Mesh
from jax.sharding import PartitionSpec as P

BATCH = ("batch_0", "batch_1", "batch_2")
BATCH_CHAN = ("batch_0", "batch_1", "batch_2", "chan")


EPS_NORM = 1e-05
EPS_COV = 0.0001
FULL_PRECISION = lax.Precision.HIGHEST


def joined_along(pieces, dim):
    pieces = jnp.moveaxis(pieces, 0, dim)
    shape = pieces.shape
    return pieces.reshape(*shape[:dim], shape[dim] * shape[dim + 1], *shape[dim + 2 :])


def copy_for_each(array, axis):
    copies = jnp.broadcast_to(array, (lax.axis_size(axis), *array.shape))
    return lax.all_to_all(copies, axis, split_axis=0, concat_axis=0, tiled=True)


def gathered_copies(array, axis, dim):
    return joined_along(copy_for_each(array, axis), dim)


def in_blocks(array, dim, size):
    shape = array.shape
    pieces = array.reshape(*shape[:dim], size, shape[dim] // size, *shape[dim + 1 :])
    return jnp.moveaxis(pieces, dim, 0)


def summed_on_arrival(array, axis, dim):
    pieces = in_blocks(array, dim, lax.axis_size(axis))
    arrived = lax.all_to_all(pieces, axis, split_axis=0, concat_axis=0, tiled=True)
    return arrived.sum(axis=0)


def sum_in_two_steps(array, axes, dim):
    far, near = axes
    own = summed_on_arrival(in_blocks(array, dim, lax.axis_size(far)), near, dim + 1)
    return jnp.sum(lax.all_to_all(own, far, 0, 0, tiled=True), axis=0)


def padded_to(lines, size):
    spare = -lines.shape[0] % size
    if not spare:
        return lines
    return jnp.concatenate([lines, jnp.zeros((spare, *lines.shape[1:]), lines.dtype)])


def gathered_by_axis(array, axes, dim):
    far, near = axes
    pieces = copy_for_each(copy_for_each(array, far), near)
    return joined_along(pieces.swapaxes(0, 1).reshape(-1, *array.shape), dim)


def total_of(array, axes):
    own = sum_in_two_steps(
        padded_to(array, lax.axis_size(axes[0]) * lax.axis_size(axes[1])), axes, 0
    )
    whole = gathered_by_axis(own, axes, 0)
    return whole[: len(array)].reshape(array.shape)


def in_one(arrays, axis):
    ends = [0]
    for a in arrays:
        ends.append(ends[-1] + a.size)
    so_far = total_of(jnp.concatenate([a.ravel() for a in arrays]), axis)
    return tuple((so_far[b:e].reshape(a.shape) for a, b, e in zip(arrays, ends, ends[1:])))


def smooth_gate(values):
    return (
        0.5
        * values
        * (1.0 + jnp.tanh(0.7978845608 * (values + 0.044715 * values * values * values)))
    )


def pad_positions(inputs, dilation_step):
    return jnp.pad(inputs, ((0, 0), (0, 0), (2 * dilation_step, 2 * dilation_step), (0, 0)))


def conv_taps(padded, kernel_weight, dilation_step, length):
    running = None
    for kernel_tap in range(5):
        offset_input = lax.slice_in_dim(
            padded, kernel_tap * dilation_step, kernel_tap * dilation_step + length, axis=2
        )
        kernel_contribution = jnp.einsum(
            "vslc,co->vslo",
            offset_input,
            kernel_weight[kernel_tap],
            preferred_element_type=jnp.float32,
        )
        running = kernel_contribution if running is None else running + kernel_contribution
    return running


def whiten(factor, block_rows):
    return jax.scipy.linalg.solve_triangular(factor, block_rows.T, lower=True).T


def shards(monomers, keep_mask, lengths, norm_gain, weight_a, weight_b):
    sequences = lengths.shape[0]
    tokens_dev = monomers.shape[0]
    length = tokens_dev // sequences
    channel_count = norm_gain.shape[0]
    positions = lax.broadcasted_iota(jnp.int32, (sequences, length), 1)
    alive = (positions < lengths[:, None]).astype(jnp.float32).reshape(tokens_dev)
    kept_rows = keep_mask.astype(jnp.float32) * alive[None, :]
    gathered = gathered_copies(monomers, "chan", 1)
    viewed = gathered.astype(jnp.float32)[None] * kept_rows[:, :, None]
    square_mean = jnp.mean(viewed * viewed, axis=-1, keepdims=True)
    normed = (viewed * lax.rsqrt(square_mean + EPS_NORM) * norm_gain).astype(jnp.bfloat16)
    padded_in = pad_positions(normed.reshape(2, sequences, length, channel_count), 1)
    full_a, full_b = (
        lax.all_gather(weight_a, BATCH, axis=1, tiled=True),
        lax.all_gather(weight_b, BATCH, axis=2, tiled=True),
    )
    hidden_pre = conv_taps(padded_in, full_a, 1, length)
    hidden = smooth_gate(hidden_pre).astype(jnp.bfloat16)
    padded_hidden = pad_positions(hidden, 2)
    partial_embed = conv_taps(padded_hidden, full_b, 2, length)
    partial_embed = partial_embed.reshape(2, tokens_dev, partial_embed.shape[3])
    embedded = summed_on_arrival(partial_embed, "chan", 1)
    row_count = embedded.shape[1]
    embed_width = embedded.shape[2]
    own_alive = lax.dynamic_slice_in_dim(alive, lax.axis_index("chan") * row_count, row_count, 0)
    masked = embedded * own_alive[None, :, None]
    identity_block = jnp.eye(embed_width, dtype=jnp.float32)[None]
    local_raw = jnp.einsum("vtf,vtg->vfg", masked, masked, precision=FULL_PRECISION)
    row_sums, live_count, raw_gram = in_one(
        (jnp.sum(masked, axis=1), jnp.sum(own_alive), local_raw),
        (("batch_0", "batch_1"), ("batch_2", "chan")),
    )
    center = row_sums / live_count
    centered = (embedded - center[:, None, :]) * own_alive[None, :, None]
    covariance = (
        raw_gram / live_count - center[:, :, None] * center[:, None, :] + EPS_COV * identity_block
    )
    factor_low = jnp.linalg.cholesky(covariance)
    whitened = jax.vmap(whiten)(factor_low, centered)
    gap_rows = whitened[0] - whitened[1]
    pair_gap = jnp.sum(gap_rows * gap_rows, axis=-1) / embed_width
    return (whitened, pair_gap)


def solution(mesh):
    torus = Mesh(
        mesh.devices.reshape(8, 4, 2, mesh.shape["chan"]), ("batch_0", "batch_1", "batch_2", "chan")
    )
    in_specs = (
        P(BATCH, "chan"),
        P(None, BATCH),
        P(BATCH),
        P(),
        P(None, BATCH, "chan"),
        P(None, "chan", BATCH),
    )
    out_specs = (P(None, BATCH_CHAN, None), P(BATCH_CHAN))
    return jax.shard_map(
        shards, mesh=torus, in_specs=in_specs, out_specs=out_specs, check_vma=False
    )
```

profile of v0, /device:TPU:1, one launch (start us, length us, event | category | flops | bytes accessed | tf_op | source)
XLA Modules:
  0.0 669.1 jit_solution(10293636125830832461)
XLA Ops:
  8.8 3.0 broadcast_in_dim.10
  11.8 5.1 all-to-all-start
  17.8 29.4 %all-to-all-done = bf16[4,1024,320]{1,2,0:T(8,128)(2,1)S(1)} async-done(((bf16[4,1024,320]{1,2,0:T(8,128)(2,1)}), bf16[4,1024,320]{1,2,0:T(8,128)(2,1)S(1)}, u32[]{:S(2)}, u32[]{:S(2)}) %all-to-all-start) | async-done | bytes 2621472 | tf_op jit(solution)/shard_map/all_to_all | solution.py:24
  47.1 5.3 convert_bitcast_fusion
  52.4 5.9 copy.112
  58.3 3.7 multiply_reduce_fusion
  62.1 8.1 %reshape.184 = f32[2,512,1280]{1,0,2:T(2,128)} reshape(f32[1024,4,320]{0,2,1:T(8,128)} %get-tuple-element.41) | data formatting | bytes 10485760 | tf_op jit(solution)/shard_map/convert_element_type | solution.py:119
  70.2 8.9 %copy.111 = f32[2,512,1280]{2,1,0:T(8,128)} copy(f32[2,512,1280]{1,0,2:T(2,128)} %reshape.184) | data formatting | bytes 10485760 | tf_op jit(solution)/shard_map/convert_element_type | solution.py:119
  79.1 6.5 multiply_convert_fusion
  85.6 12.1 %all-gather.3.cloned.1.call-done = bf16[5,1280,320]{2,0,1:T(8,128)(2,1)} async-done(((bf16[5,20,320]{2,0,1:T(8,128)(2,1)}), bf16[5,1280,320]{2,0,1:T(8,128)(2,1)}) %all-gather.3.cloned.1.call-update) | async-done | bytes 4096016 | tf_op jit(solution)/shard_map/all_gather | solution.py:124
  97.7 23.9 %fusion.73 = (bf16[1,1280,320]{2,0,1:T(2,128)(2,1)S(1)}, bf16[1,1280,320]{2,0,1:T(2,128)(2,1)}, bf16[1,1280,320]{2,0,1:T(2,128)(2,1)}, bf16[1,1280,320]{2,0,1:T(2,128)(2,1)}, bf16[1,1280,320]{2,0,1:T(2,128)(2,1)}) fusion(bf16[5,1280,320]{2,0,1:T(8,128)(2,1)} %all-gather.3.cloned.1.call-done), kind=kLoop, calls=%fused_computation.137 | loop fusion | bytes 8192000 | tf_op jit(solution)/shard_map/slice | solution.py:99
  121.6 4.8 copy.171
  126.4 4.9 copy.170
  131.3 4.8 copy.168
  136.1 4.9 copy.167
  141.0 3.9 copy.169
  144.9 4.8 fusion
  155.6 2.7 fusion.16
  158.3 10.8 %all-gather.5.cloned.1.call-done = bf16[5,320,512]{1,2,0:T(8,128)(2,1)} async-done(((bf16[5,320,8]{1,2,0:T(8,128)(2,1)}), bf16[5,320,512]{1,2,0:T(8,128)(2,1)}) %all-gather.5.cloned.1.call-update) | async-done | bytes 1638416 | tf_op jit(solution)/shard_map/all_gather | solution.py:125
  169.1 3.3 fusion.18
  172.4 2.8 fusion.19
  183.5 4.9 all-to-all-start.1
  189.0 48.0 %all-to-all-done.1 = f32[4,2,256,512]{3,2,1,0:T(8,128)} async-done(((f32[4,2,256,512]{3,2,1,0:T(8,128)}), f32[4,2,256,512]{3,2,1,0:T(8,128)}, u32[]{:S(2)}, u32[]{:S(2)}) %all-to-all-start.1) | async-done | bytes 4194336 | tf_op jit(solution)/shard_map/all_to_all | solution.py:39
  237.0 2.8 reduce_sum.64
  242.9 15.8 %concatenate.14 = f32[525568]{0:T(1024)} concatenate(f32[1024]{0:T(1024)S(1)} %bitcast.176, f32[1]{0:T(128)} %bitcast.34, f32[524288]{0:T(1024)S(1)} %bitcast.166, f32[255]{0:T(256)S(1)} %broadcast_in_dim.11), dimensions={0} | concatenate | bytes 4204544 | tf_op jit(solution)/shard_map/concatenate | solution.py:53
  258.6 4.5 reshape_reshape.10
  265.2 31.9 %all_to_all.38 = f32[8,32,2053]{2,1,0:T(8,128)} all-to-all(f32[8,32,2053]{2,1,0:T(8,128)S(1)} %copy.128), channel_id=1, replica_groups=mesh['batch_0'=8,'batch_1'=4,'batch_2'=2,'chan'=4] {'batch_2','chan'}, dimensions={0} | all-to-all | bytes 4204544 | tf_op jit(solution)/shard_map/all_to_all | solution.py:39
  299.1 19.2 %all_to_all.39 = f32[32,1,2053]{2,1,0:T(1,128)S(1)} all-to-all(f32[32,1,2053]{2,1,0:T(1,128)S(1)} %all_to_all.27), channel_id=1, replica_groups=mesh['batch_0'=8,'batch_1'=4,'batch_2'=2,'chan'=4] {'batch_0','batch_1'}, dimensions={0} | all-to-all | bytes 525568 | tf_op jit(solution)/shard_map/all_to_all | solution.py:46
  318.6 15.1 %all_to_all.40 = f32[32,1,2053]{2,1,0:T(1,128)S(1)} all-to-all(f32[32,1,2053]{2,1,0:T(1,128)S(1)} %broadcast_in_dim.12), channel_id=1, replica_groups=mesh['batch_0'=8,'batch_1'=4,'batch_2'=2,'chan'=4] {'batch_0','batch_1'}, dimensions={0} | all-to-all | bytes 525568 | tf_op jit(solution)/shard_map/all_to_all | solution.py:24
  335.2 7.7 %all-to-all-start.5 = ((f32[8,32,2053]{2,1,0:T(8,128)}), f32[8,32,2053]{2,1,0:T(8,128)}, u32[]{:S(2)}, u32[]{:S(2)}) async-start(f32[8,32,2053]{2,1,0:T(8,128)} %broadcast_in_dim.13), calls=%async_computation.5 | async-start | bytes 4456448 | tf_op jit(solution)/shard_map/all_to_all | solution.py:24
  344.1 26.5 %all-to-all-done.5 = f32[8,32,2053]{2,1,0:T(8,128)} async-done(((f32[8,32,2053]{2,1,0:T(8,128)}), f32[8,32,2053]{2,1,0:T(8,128)}, u32[]{:S(2)}, u32[]{:S(2)}) %all-to-all-start.5) | async-done | bytes 2102304 | tf_op jit(solution)/shard_map/all_to_all | solution.py:24
  370.6 4.3 copy.129
  374.9 4.0 reshape_reshape.11
  380.1 2.8 slice_divide_fusion
  390.8 3.0 copy.131
  397.3 23.5 %custom-call.35 = f32[2,128,128]{2,1,0:T(8,128)S(1)} custom-call(f32[2,128,128]{2,1,0:T(8,128)S(1)} %cholesky.274), custom_call_target="Cholesky" | custom-call | tf_op jit(solution)/shard_map/jit(cholesky)/cholesky | solution.py:148
  421.0 19.9 %custom-call.36 = f32[2,1,128,128]{2,3,1,0:T(8,128)S(1)} custom-call(f32[2,1,128,128]{3,2,1,0:T(8,128)S(1)} %select_bitcast_fusion.2), custom_call_target="InvertDiagBlocksLowerTriangular" | custom-call | tf_op jit(solution)/shard_map/jit(cholesky)/cholesky | solution.py:148
  444.0 23.5 %custom-call.37 = f32[2,128,128]{2,1,0:T(8,128)S(1)} custom-call(f32[2,128,128]{2,1,0:T(8,128)S(1)} %cholesky.278), custom_call_target="Cholesky" | custom-call | tf_op jit(solution)/shard_map/jit(cholesky)/cholesky | solution.py:148
  467.4 19.7 %custom-call.38 = f32[2,1,128,128]{2,3,1,0:T(8,128)S(1)} custom-call(f32[2,1,128,128]{3,2,1,0:T(8,128)S(1)} %get-tuple-element.46), custom_call_target="InvertDiagBlocksLowerTriangular" | custom-call | tf_op jit(solution)/shard_map/jit(cholesky)/cholesky | solution.py:148
  489.1 23.5 %custom-call.39 = f32[2,128,128]{2,1,0:T(8,128)S(1)} custom-call(f32[2,128,128]{2,1,0:T(8,128)S(1)} %cholesky.283), custom_call_target="Cholesky" | custom-call | tf_op jit(solution)/shard_map/jit(cholesky)/cholesky | solution.py:148
  512.6 20.1 %custom-call.40 = f32[2,1,128,128]{2,3,1,0:T(8,128)S(1)} custom-call(f32[2,1,128,128]{3,2,1,0:T(8,128)S(1)} %get-tuple-element.44), custom_call_target="InvertDiagBlocksLowerTriangular" | custom-call | tf_op jit(solution)/shard_map/jit(cholesky)/cholesky | solution.py:148
  534.5 23.5 %custom-call.41 = f32[2,128,128]{2,1,0:T(8,128)S(1)} custom-call(f32[2,128,128]{2,1,0:T(8,128)S(1)} %convolution_subtract_fusion.5), custom_call_target="Cholesky" | custom-call | tf_op jit(solution)/shard_map/jit(cholesky)/cholesky | solution.py:148
  560.1 14.2 %while.1 = (s32[]{:T(128)}, f32[2,512,512]{2,1,0:T(8,128)}, s32[4,2]{0,1:T(2,128)S(1)}, f32[4,2,128,128]{3,2,0,1:T(8,128)}, s32[]{:T(128)}) while((s32[]{:T(128)}, f32[2,512,512]{2,1,0:T(8,128)}, s32[4,2]{0,1:T(2,128)S(1)}, f32[4,2,128,128]{3,2,0,1:T(8,128)}, s32[]{:T(128)}) %tuple.43), condition=%wide.while_cond, body=%wide.while_body.sunk | while | flops 2 | bytes 263777 | solution.py:107
  560.7 3.0 bitcast_dynamic-update-slice_fusion.2
  564.3 3.0 bitcast_dynamic-update-slice_fusion.2
  567.9 3.0 bitcast_dynamic-update-slice_fusion.2
  571.4 2.9 bitcast_dynamic-update-slice_fusion.2
  574.3 79.6 %custom-call.42 = f32[2,4,128,128]{2,3,1,0:T(8,128)S(1)} custom-call(f32[2,4,128,128]{3,2,1,0:T(8,128)} %bitcast.177), custom_call_target="InvertDiagBlocksLowerTriangular" | custom-call | tf_op jit(solution)/shard_map/vmap(jit(_solve_triangular))/triangular_solve | solution.py:107
  (118 shorter events, 59.5 us)
Async XLA Ops:
  7.2 90.6 %all-gather.3.cloned.1.call-start = ((), (), s32[]{:S(2)}) async-start(), calls=%async_computation.6 | async-start | bytes 7987200 | tf_op jit(solution)/shard_map/all_gather | solution.py:124
  11.8 5.9 copy-start.11
  11.8 6.0 copy-start.9
  11.8 35.4 %all-to-all-start = ((bf16[4,1024,320]{1,2,0:T(8,128)(2,1)}), bf16[4,1024,320]{1,2,0:T(8,128)(2,1)S(1)}, u32[]{:S(2)}, u32[]{:S(2)}) async-start(bf16[4,1024,320]{1,2,0:T(8,128)(2,1)} %broadcast_in_dim.10), calls=%async_computation | async-start | bytes 5242880 | tf_op jit(solution)/shard_map/all_to_all | solution.py:24
  16.9 152.1 %all-gather.5.cloned.1.call-start = ((), (), s32[]{:S(2)}) async-start(), calls=%async_computation.7 | async-start | bytes 1996800 | tf_op jit(solution)/shard_map/all_gather | solution.py:125
  70.2 8.9 %copy-start.10 = (f32[1280]{0:T(1024)S(1)}, f32[1280]{0:T(1024)}, u32[]{:S(2)}) copy-start(f32[1280]{0:T(1024)} %param.9) | copy-start | bytes 15364
  141.0 8.7 %slice-start = ((s8[5242880]{0:T(1024)(128)(4,1)}), s8[1048576]{0:T(1024)(128)(4,1)S(1)}, s32[]{:S(2)}) async-start(s8[5242880]{0:T(1024)(128)(4,1)} %bitcast.168), calls=%async_computation.8 | async-start | bytes 2097152
  144.9 4.8 slice-start.1
  144.9 4.8 copy-start.5
  149.7 2.0 copy-start.6
  151.7 1.9 copy-start.7
  151.7 3.9 slice-start.2
  153.6 2.0 slice-start.3
  153.6 2.0 copy-start.8
  169.1 3.3 copy-start.4
  183.5 53.6 %all-to-all-start.1 = ((f32[4,2,256,512]{3,2,1,0:T(8,128)}), f32[4,2,256,512]{3,2,1,0:T(8,128)}, u32[]{:S(2)}, u32[]{:S(2)}) async-start(f32[4,2,256,512]{3,2,1,0:T(8,128)} %bitcast.163), calls=%async_computation.1 | async-start | bytes 8388608 | tf_op jit(solution)/shard_map/all_to_all | solution.py:39
  335.2 35.4 %all-to-all-start.5 = ((f32[8,32,2053]{2,1,0:T(8,128)}), f32[8,32,2053]{2,1,0:T(8,128)}, u32[]{:S(2)}, u32[]{:S(2)}) async-start(f32[8,32,2053]{2,1,0:T(8,128)} %broadcast_in_dim.13), calls=%async_computation.5 | async-start | bytes 4456448 | tf_op jit(solution)/shard_map/all_to_all | solution.py:24
  387.8 1.4 copy-start
  390.8 3.0 copy-start.1
  395.9 1.4 copy-start.2
  558.3 95.6 %copy-start.3 = (f32[2,512,256]{2,1,0:T(8,128)S(1)}, f32[2,512,256]{2,1,0:T(8,128)}, u32[]{:S(2)}) copy-start(f32[2,512,256]{2,1,0:T(8,128)} %multiply_bitcast_fusion) | copy-start | bytes 3145732
Sparse Core Ops, SparseCore 0:
  11.3 86.4 all-gather.2
  100.4 68.6 all-gather.4
where the time goes:
time: 678 us; the launch traced here: 669 us
  other arithmetic  267 us (39%)
  local copies, waits for them, and re-layouts  136 us (20%)
  waiting for transfers between devices  128 us (19%)
  blocking collectives  66.2 us (10%)
  matrix products  39.8 us (6%)
  starting transfers between devices  17.7 us (3%)
  between operations  14.8 us (2%)
    another operation x16, other arithmetic, shards(): factor_low = jnp.linalg.cholesky(covariance)  154 us
    another operation x4, other arithmetic, whiten(): return jax.scipy.linalg.solve_triangular(factor, block_rows.T, lower=True).T  81.4 us
    all_to_all x2, waiting for transfers between devices, copy_for_each(): return lax.all_to_all(copies, axis, split_axis=0, concat_axis=0, tiled=True)  55.9 us
    all_to_all x1, waiting for transfers between devices, summed_on_arrival(): lax.all_to_all(pieces, axis, split_axis=0, concat_axis=0, tiled=True)  48 us
    all_to_all x1, blocking collectives, summed_on_arrival(): lax.all_to_all(pieces, axis, split_axis=0, concat_axis=0, tiled=True)  31.9 us
    unnamed x43, local copies, waits for them, and re-layouts  28.3 us
    dot_general x10, matrix products, conv_taps(): jnp.einsum('vslc,co->vslo', offset_input, kernel_weight[kernel_tap], pref...  25.2 us
    slice x1, local copies, waits for them, and re-layouts, conv_taps(): kernel_weight[kernel_tap]  23.9 us
  transfers between devices with their start and end apart: 5, of which 5 were waited for; matrix products, arithmetic and copies ran while one was open for 16% of the time, Pallas kernels for 0%

commit v1 on v0

--- a/solution.py
+++ b/solution.py
@@ -1,6 +1,8 @@
 import jax
 import jax.numpy as jnp
 from jax import lax
+from jax.experimental import pallas as pl
+from jax.experimental.pallas import tpu as pltpu
 from jax.sharding import Mesh
 from jax.sharding import PartitionSpec as P
 
@@ -105,6 +107,382 @@
 
 def whiten(factor, block_rows):
     return jax.scipy.linalg.solve_triangular(factor, block_rows.T, lower=True).T
+
+
+HI = lax.Precision.HIGHEST
+MESH_IDS = pl.DeviceIdType.MESH
+Z, X, CORE, Y = "batch_0", "batch_1", "batch_2", "chan"
+AXES = (Z, X, CORE, Y)
+BLOCK = 128
+GROUP = 8
+
+
+def dot_of(a, b, dims, precision=HI):
+    return lax.dot_general(
+        a, b, (dims, ((), ())), precision=precision, preferred_element_type=jnp.float32
+    )
+
+
+def in_vmem():
+    return pl.BlockSpec(memory_space=pltpu.VMEM)
+
+
+def block_pairs(width):
+    return [(i, k) for i in range(width // BLOCK) for k in range(i + 1)]
+
+
+def share_rows(width, planes):
+    rows = len(block_pairs(width)) * BLOCK + GROUP
+    return -(-rows // (planes * GROUP)) * GROUP
+
+
+def moments_kernel(emb_ref, alive_ref, out_ref):
+    views, tokens, width = emb_ref.shape
+    pairs = block_pairs(width)
+    at = len(pairs) * BLOCK
+    alive = alive_ref[...]
+    for v in range(views):
+        masked = emb_ref[v] * alive
+        for i in range(width // BLOCK):
+            wide = (i + 1) * BLOCK
+            strip = dot_of(
+                masked[:, i * BLOCK : wide], masked[:, :wide], ((0,), (0,))
+            )
+            for k in range(i + 1):
+                b = pairs.index((i, k))
+                out_ref[v, b * BLOCK : (b + 1) * BLOCK, :] = strip[:, k * BLOCK : (k + 1) * BLOCK]
+        out_ref[v, at:, :] = jnp.zeros((out_ref.shape[1] - at, BLOCK), jnp.float32)
+        sums = jnp.sum(masked, axis=0, keepdims=True)
+        for k in range(width // BLOCK):
+            out_ref[v, at + k : at + k + 1, :] = sums[:, k * BLOCK : (k + 1) * BLOCK]
+        count = jnp.sum(alive, axis=0, keepdims=True)
+        last = at + width // BLOCK
+        out_ref[v, last : last + 1, :] = jnp.broadcast_to(count, (1, BLOCK))
+
+
+def moments_of(embedded, alive, planes):
+    views, tokens, width = embedded.shape
+    rows = share_rows(width, planes) * planes
+    return pl.pallas_call(
+        moments_kernel,
+        out_shape=jax.ShapeDtypeStruct((views, rows, BLOCK), jnp.float32),
+        in_specs=[in_vmem()] * 2,
+        out_specs=in_vmem(),
+        compiler_params=pltpu.CompilerParams(vmem_limit_bytes=32 << 20),
+        name="moments",
+    )(embedded, alive[:, None])
+
+
+def total_kernel(sizes, part_ref, out_ref, pair_in, mine, plane_in, share, line_in, total, sems):
+    depth, across, down = sizes
+    planes = across * down
+    rows = share.shape[0]
+    z, x = lax.axis_index(Z), lax.axis_index(X)
+    core, y = lax.axis_index(CORE), lax.axis_index(Y)
+    me = x * down + y
+    partner = 1 - core
+    pair_send, pair_recv, plane_send, plane_recv, line_send, line_recv, back_send, back_recv = sems
+
+    def in_plane(step):
+        other = lax.rem(me + step, planes)
+        return other, (z, other // down, core, lax.rem(other, down))
+
+    def in_line(step):
+        other = lax.rem(z + step, depth)
+        return other, (other, x, core, y)
+
+    barrier = pltpu.get_barrier_semaphore()
+    pl.semaphore_signal(barrier, inc=1, device_id=(z, x, partner, y), device_id_type=MESH_IDS)
+    for step in range(1, planes):
+        pl.semaphore_signal(barrier, inc=1, device_id=in_plane(step)[1], device_id_type=MESH_IDS)
+    for step in range(1, depth):
+        pl.semaphore_signal(barrier, inc=1, device_id=in_line(step)[1], device_id_type=MESH_IDS)
+    pl.semaphore_wait(barrier, 1 + planes - 1 + depth - 1)
+
+    def sent(src, dst, send, recv, device):
+        return pltpu.make_async_remote_copy(
+            src_ref=src, dst_ref=dst, send_sem=send, recv_sem=recv,
+            device_id=device, device_id_type=MESH_IDS,
+        )
+
+    swap = sent(part_ref.at[partner], pair_in, pair_send, pair_recv, (z, x, partner, y))
+    swap.start()
+    swap.wait()
+    mine[...] = part_ref[core] + pair_in[...]
+
+    def rows_of(index):
+        return pl.ds(pl.multiple_of(index * rows, GROUP), rows)
+
+    copies = []
+    for step in range(1, planes):
+        other, device = in_plane(step)
+        copy = sent(
+            mine.at[rows_of(other)], plane_in.at[step], plane_send.at[step], plane_recv.at[step], device
+        )
+        copy.start()
+        copies.append(copy)
+    for copy in copies:
+        copy.wait()
+    plane_in[0] = mine[rows_of(me)]
+    acc = None
+    for source in range(planes):
+        piece = plane_in[lax.rem(me - source + planes, planes)]
+        acc = piece if acc is None else acc + piece
+    share[...] = acc
+
+    copies = []
+    for step in range(1, depth):
+        _, device = in_line(step)
+        copy = sent(share, line_in.at[step], line_send.at[step], line_recv.at[step], device)
+        copy.start()
+        copies.append(copy)
+    for copy in copies:
+        copy.wait()
+    line_in[0] = share[...]
+    acc = None
+    for source in range(depth):
+        piece = line_in[lax.rem(z - source + depth, depth)]
+        acc = piece if acc is None else acc + piece
+    total[...] = acc
+
+    copies = []
+    for step in range(1, planes):
+        _, device = in_plane(step)
+        copy = sent(
+            total, out_ref.at[rows_of(me)], back_send.at[step], back_recv.at[step], device
+        )
+        copy.start()
+        copies.append(copy)
+    out_ref[rows_of(me)] = total[...]
+    for copy in copies:
+        copy.wait()
+
+
+def total_moments(parts, mesh_sizes):
+    depth, across, down = mesh_sizes
+    planes = across * down
+    _, all_rows, lanes = parts.shape
+    rows = all_rows // planes
+    dma = pltpu.SemaphoreType.DMA
+
+    def kernel(part_ref, out_ref, pair_in, mine, plane_in, share, line_in, total, *sems):
+        total_kernel(mesh_sizes, part_ref, out_ref, pair_in, mine, plane_in, share, line_in, total, sems)
+
+    return pl.pallas_call(
+        kernel,
+        out_shape=jax.ShapeDtypeStruct((all_rows, lanes), jnp.float32),
+        in_specs=[in_vmem()],
+        out_specs=in_vmem(),
+        scratch_shapes=[
+            pltpu.VMEM((all_rows, lanes), jnp.float32),
+            pltpu.VMEM((all_rows, lanes), jnp.float32),
+            pltpu.VMEM((planes, rows, lanes), jnp.float32),
+            pltpu.VMEM((rows, lanes), jnp.float32),
+            pltpu.VMEM((depth, rows, lanes), jnp.float32),
+            pltpu.VMEM((rows, lanes), jnp.float32),
+            dma, dma,
+            dma((planes,)), dma((planes,)),
+            dma((depth,)), dma((depth,)),
+            dma((planes,)), dma((planes,)),
+        ],
+        compiler_params=pltpu.CompilerParams(
+            collective_id=1, has_side_effects=True, vmem_limit_bytes=32 << 20
+        ),
+        name="total_moments",
+    )(parts)
+
+
+def splat_row(v, a):
+    return jnp.broadcast_to(v[a : a + 1, :], (GROUP, BLOCK))
+
+
+def splat_lane(v, j):
+    return jnp.broadcast_to(v[:, j : j + 1], (GROUP, BLOCK))
+
+
+def base_inverse(load, store):
+    count = BLOCK // GROUP
+    groups = [load(g) for g in range(count)]
+    lane = lax.broadcasted_iota(jnp.int32, (GROUP, BLOCK), 1)
+    sub = lax.broadcasted_iota(jnp.int32, (GROUP, BLOCK), 0)
+    steps = range(GROUP)
+    for p in range(count):
+        j = GROUP * p
+        v = groups[p]
+        cols = [splat_lane(v, j + a) for a in steps]
+        e = [[splat_row(cols[a], b) if b >= a else None for a in steps] for b in steps]
+        low = [[None] * GROUP for _ in steps]
+        rec = []
+        for a in steps:
+            rec.append(1.0 / e[a][a])
+            for b in range(a + 1, GROUP):
+                low[b][a] = e[b][a] * rec[a]
+            for b in range(a + 1, GROUP):
+                for c in range(a + 1, b + 1):
+                    e[b][c] = e[b][c] - low[b][a] * e[c][a]
+        panel = (lane >= j) & (lane < j + GROUP)
+        rows = []
+        for a in steps:
+            r = jnp.where(panel, jnp.where(lane == j + a, 1.0, 0.0), splat_row(v, a))
+            for b in range(a):
+                r = r - low[a][b] * rows[b]
+            rows.append(r)
+        out = None
+        for a in steps:
+            r = rows[a] * lax.rsqrt(e[a][a])
+            out = r if out is None else jnp.where(sub == a, r, out)
+        store(p, jnp.where(lane < j + GROUP, out, 0.0))
+        for g in range(p + 1, count):
+            x = groups[g]
+            w = []
+            acc = jnp.where(panel, 0.0, x)
+            for a in steps:
+                t = splat_lane(x, j + a)
+                for b in range(a):
+                    t = t - low[a][b] * w[b]
+                w.append(t)
+                acc = acc - (t * rec[a]) * rows[a]
+            groups[g] = acc
+
+
+def factor_kernel(total_ref, out_ref, work, m_ref):
+    width = work.shape[1]
+    blocks = width // BLOCK
+    pairs = block_pairs(width)
+    at = len(pairs) * BLOCK
+    tail = total_ref[at : at + GROUP, :]
+    count = tail[blocks : blocks + 1, 0:1]
+    center = jnp.concatenate([tail[k : k + 1, :] for k in range(blocks)], axis=1) / count
+    first = lax.broadcasted_iota(jnp.int32, (GROUP, width), 0) == 0
+    center8 = jnp.where(first, jnp.broadcast_to(center, (GROUP, width)), 0.0)
+    eye = lax.broadcasted_iota(jnp.int32, (BLOCK, BLOCK), 0) == lax.broadcasted_iota(
+        jnp.int32, (BLOCK, BLOCK), 1
+    )
+    for b, (i, k) in enumerate(pairs):
+        outer = dot_of(
+            center8[:, i * BLOCK : (i + 1) * BLOCK], center8[:, k * BLOCK : (k + 1) * BLOCK], ((0,), (0,))
+        )
+        block = total_ref[b * BLOCK : (b + 1) * BLOCK, :] / count - outer
+        if i == k:
+            block = block + jnp.where(eye, EPS_COV, 0.0)
+        work[i * BLOCK : (i + 1) * BLOCK, k * BLOCK : (k + 1) * BLOCK] = block
+        if i != k:
+            work[k * BLOCK : (k + 1) * BLOCK, i * BLOCK : (i + 1) * BLOCK] = block.T
+    row_block = lax.broadcasted_iota(jnp.int32, (width, BLOCK), 0) // BLOCK
+    col_block = lax.broadcasted_iota(jnp.int32, (width, width), 1) // BLOCK
+    strip_block = lax.broadcasted_iota(jnp.int32, (BLOCK, width), 1) // BLOCK
+    strip_eye = jnp.where(
+        lax.broadcasted_iota(jnp.int32, (BLOCK, width), 1) % BLOCK
+        == lax.broadcasted_iota(jnp.int32, (BLOCK, width), 0),
+        1.0,
+        0.0,
+    )
+
+    def step(k, _):
+        here = pl.multiple_of(k * BLOCK, BLOCK)
+
+        def load(g):
+            return work[pl.ds(pl.multiple_of(here + GROUP * g, GROUP), GROUP), pl.ds(here, BLOCK)]
+
+        def store(g, val):
+            m_ref[GROUP * g : GROUP * (g + 1), :] = val
+
+        base_inverse(load, store)
+        m = m_ref[...]
+        col = jnp.where(row_block > k, work[:, pl.ds(here, BLOCK)], 0.0)
+        left = dot_of(col, m, ((1,), (1,)))
+        row = jnp.where(strip_block == k, strip_eye, work[pl.ds(here, BLOCK), :])
+        across = dot_of(m, row, ((1,), (0,)))
+        work[...] = jnp.where(col_block == k, 0.0, work[...]) - dot_of(left, across, ((1,), (0,)))
+        work[pl.ds(here, BLOCK), :] = jnp.where(strip_block <= k, across, 0.0)
+        return 0
+
+    lax.fori_loop(0, blocks, step, 0)
+    out_ref[:width, :] = work[...]
+    out_ref[width:, :] = center8
+
+
+def inverse_factor(total, width):
+    return pl.pallas_call(
+        factor_kernel,
+        out_shape=jax.ShapeDtypeStruct((width + GROUP, width), jnp.float32),
+        in_specs=[in_vmem()],
+        out_specs=in_vmem(),
+        scratch_shapes=[
+            pltpu.VMEM((width, width), jnp.float32),
+            pltpu.VMEM((BLOCK, BLOCK), jnp.float32),
+        ],
+        compiler_params=pltpu.CompilerParams(vmem_limit_bytes=32 << 20),
+        name="inverse_factor",
+    )(total)
+
+
+def swap_kernel(own_ref, out_ref, send, recv):
+    z, x = lax.axis_index(Z), lax.axis_index(X)
+    core, y = lax.axis_index(CORE), lax.axis_index(Y)
+    other = (z, x, 1 - core, y)
+    barrier = pltpu.get_barrier_semaphore()
+    pl.semaphore_signal(barrier, inc=1, device_id=other, device_id_type=MESH_IDS)
+    pl.semaphore_wait(barrier, 1)
+    copy = pltpu.make_async_remote_copy(
+        src_ref=own_ref, dst_ref=out_ref, send_sem=send, recv_sem=recv,
+        device_id=other, device_id_type=MESH_IDS,
+    )
+    copy.start()
+    copy.wait()
+
+
+def from_partner(own):
+    return pl.pallas_call(
+        swap_kernel,
+        out_shape=jax.ShapeDtypeStruct(own.shape, own.dtype),
+        in_specs=[in_vmem()],
+        out_specs=in_vmem(),
+        scratch_shapes=[pltpu.SemaphoreType.DMA, pltpu.SemaphoreType.DMA],
+        compiler_params=pltpu.CompilerParams(
+            collective_id=2, has_side_effects=True, vmem_limit_bytes=16 << 20
+        ),
+        name="from_partner",
+    )(own)
+
+
+def whiten_kernel(emb_ref, alive_ref, own_ref, other_ref, out_ref, gap_ref):
+    views, tokens, width = emb_ref.shape
+    core = lax.axis_index(CORE)
+    alive = alive_ref[...]
+    for ref, v in ((own_ref, core), (other_ref, 1 - core)):
+        centered = (emb_ref[v] - ref[width : width + 1, :]) * alive
+        out_ref[v] = dot_of(centered, ref[:width, :], ((1,), (1,)))
+    gap = out_ref[0] - out_ref[1]
+    ones = jnp.ones((GROUP, width), jnp.float32)
+    sums = dot_of(ones, gap * gap, ((1,), (1,))) / width
+    for k in range(tokens // BLOCK):
+        gap_ref[k : k + 1, :] = sums[0:1, k * BLOCK : (k + 1) * BLOCK]
+
+
+def whitened_rows(embedded, alive, own, other):
+    views, tokens, width = embedded.shape
+    whitened, gap = pl.pallas_call(
+        whiten_kernel,
+        out_shape=(
+            jax.ShapeDtypeStruct(embedded.shape, jnp.float32),
+            jax.ShapeDtypeStruct((tokens // BLOCK, BLOCK), jnp.float32),
+        ),
+        in_specs=[in_vmem()] * 4,
+        out_specs=(in_vmem(), in_vmem()),
+        compiler_params=pltpu.CompilerParams(vmem_limit_bytes=32 << 20),
+        name="whitened_rows",
+    )(embedded, alive[:, None], own, other)
+    return whitened, gap.reshape(tokens)
+
+
+def whitening(embedded, alive, sizes):
+    width = embedded.shape[2]
+    parts = moments_of(embedded, alive, sizes[1] * sizes[2])
+    total = total_moments(parts, sizes)
+    own = inverse_factor(total, width)
+    other = from_partner(own)
+    return whitened_rows(embedded, alive, own, other)
 
 
 def shards(monomers, keep_mask, lengths, norm_gain, weight_a, weight_b):
@@ -133,23 +511,8 @@
     row_count = embedded.shape[1]
     embed_width = embedded.shape[2]
     own_alive = lax.dynamic_slice_in_dim(alive, lax.axis_index("chan") * row_count, row_count, 0)
-    masked = embedded * own_alive[None, :, None]
-    identity_block = jnp.eye(embed_width, dtype=jnp.float32)[None]
-    local_raw = jnp.einsum("vtf,vtg->vfg", masked, masked, precision=FULL_PRECISION)
-    row_sums, live_count, raw_gram = in_one(
-        (jnp.sum(masked, axis=1), jnp.sum(own_alive), local_raw),
-        (("batch_0", "batch_1"), ("batch_2", "chan")),
-    )
-    center = row_sums / live_count
-    centered = (embedded - center[:, None, :]) * own_alive[None, :, None]
-    covariance = (
-        raw_gram / live_count - center[:, :, None] * center[:, None, :] + EPS_COV * identity_block
-    )
-    factor_low = jnp.linalg.cholesky(covariance)
-    whitened = jax.vmap(whiten)(factor_low, centered)
-    gap_rows = whitened[0] - whitened[1]
-    pair_gap = jnp.sum(gap_rows * gap_rows, axis=-1) / embed_width
-    return (whitened, pair_gap)
+    sizes = (lax.axis_size(Z), lax.axis_size(X), lax.axis_size(Y))
+    return whitening(embedded, own_alive, sizes)
 
 
 def solution(mesh):

time: 678 us -> 334 us (0.49); the launches traced: 669 us -> 333 us
  other arithmetic: 267 us -> 18.6 us
  Pallas kernels: 0 us -> 74.3 us
  blocking collectives: 66.2 us -> 0 us
  local copies, waits for them, and re-layouts: 136 us -> 77.1 us
  waiting for transfers between devices: 128 us -> 101 us
  starting transfers between devices: 17.7 us -> 10 us
    another operation x20 -> x0, other arithmetic: 235 us -> none  [the longest x16 154 us: shards(): factor_low = jnp.linalg.cholesky(covariance)]
    pallas_call x0 -> x5, Pallas kernels: none -> 74.3 us  [the longest x1 39.9 us: total_moments(): pl.pallas_call(kernel, out_shape=jax.ShapeDtypeStruct((all_rows, lanes),...]
    all_to_all x3 -> x0, blocking collectives: 66.2 us -> none  [the longest x1 31.9 us: summed_on_arrival(): lax.all_to_all(pieces, axis, split_axis=0, concat_axis=0, tiled=True)]
    all_to_all x2 -> x1, waiting for transfers between devices: 55.9 us -> 29.4 us  [copy_for_each(): return lax.all_to_all(copies, axis, split_axis=0, concat_axis=0, tiled=True)]
    another operation x18 -> x0, local copies, waits for them, and re-layouts: 18.5 us -> none
    concatenate x1 -> x0, local copies, waits for them, and re-layouts: 15.8 us -> none  [padded_to(): jnp.concatenate([lines, jnp.zeros((spare, *lines.shape[1:]), lines.dtype)])]
    another operation x13 -> x0, matrix products: 12.8 us -> none  [the longest x6 6.73 us: shards(): factor_low = jnp.linalg.cholesky(covariance)]
    dot_general x10, matrix products: 25.2 us -> 37.1 us  [conv_taps(): jnp.einsum('vslc,co->vslo', offset_input, kernel_weight[kernel_tap], pref...]
  transfers between devices with their start and end apart: 5 -> 4, of which waited for: 5 -> 4; matrix products, arithmetic and copies ran while one was open for 16% -> 31% of each run, Pallas kernels for 0% -> 0%
where the time goes in v1:
time: 334 us; the launch traced here: 333 us
  waiting for transfers between devices  101 us (30%)
  local copies, waits for them, and re-layouts  77.1 us (23%)
  Pallas kernels  74.3 us (22%)
  matrix products  37.1 us (11%)
  other arithmetic  18.6 us (6%)
  between operations  14.5 us (4%)
  starting transfers between devices  10 us (3%)
    all_to_all x1, waiting for transfers between devices, summed_on_arrival(): lax.all_to_all(pieces, axis, split_axis=0, concat_axis=0, tiled=True)  48.5 us
    pallas_call x1, Pallas kernels, total_moments(): pl.pallas_call(kernel, out_shape=jax.ShapeDtypeStruct((all_rows, lanes),...  39.9 us
    dot_general x10, matrix products, conv_taps(): jnp.einsum('vslc,co->vslo', offset_input, kernel_weight[kernel_tap], pref...  37.1 us
    all_to_all x1, waiting for transfers between devices, copy_for_each(): return lax.all_to_all(copies, axis, split_axis=0, concat_axis=0, tiled=True)  29.4 us
    pallas_call x1, Pallas kernels, inverse_factor(): pl.pallas_call(factor_kernel, out_shape=jax.ShapeDtypeStruct((width + GRO...  25.5 us
    unnamed x31, local copies, waits for them, and re-layouts  24.8 us
    slice x1, local copies, waits for them, and re-layouts, conv_taps(): kernel_weight[kernel_tap]  23.4 us
    convert_element_type x3, local copies, waits for them, and re-layouts, shards(): viewed = gathered.astype(jnp.float32)[None] * kept_rows[:, :, None]  23.1 us
  transfers between devices with their start and end apart: 4, of which 4 were waited for; matrix products, arithmetic and copies ran while one was open for 31% of the time, Pallas kernels for 0%

profile of v1, /device:TPU:1, one launch (start us, length us, event | category | flops | bytes accessed | tf_op | source)
XLA Modules:
  0.0 333.2 jit_solution(7489894843250917847)
XLA Ops:
  7.2 0.0 all-gather.3.cloned.1.call-start
  7.2 1.6 copy.35
  8.8 0.0 all-gather.3.cloned.1.call-update
  8.8 3.0 broadcast_in_dim.4
  11.8 5.1 %all-to-all-start = ((bf16[4,1024,320]{1,2,0:T(8,128)(2,1)}), bf16[4,1024,320]{1,2,0:T(8,128)(2,1)S(1)}, u32[]{:S(2)}, u32[]{:S(2)}) async-start(bf16[4,1024,320]{1,2,0:T(8,128)(2,1)} %broadcast_in_dim.4), calls=%async_computation | async-start | bytes 5242880 | tf_op jit(solution)/shard_map/all_to_all | solution.py:26
  16.9 0.7 all-gather.5.cloned.1.call-update
  17.7 0.0 copy-done.7
  17.7 0.1 fusion.26
  17.8 29.4 %all-to-all-done = bf16[4,1024,320]{1,2,0:T(8,128)(2,1)S(1)} async-done(((bf16[4,1024,320]{1,2,0:T(8,128)(2,1)}), bf16[4,1024,320]{1,2,0:T(8,128)(2,1)S(1)}, u32[]{:S(2)}, u32[]{:S(2)}) %all-to-all-start) | async-done | bytes 2621472 | tf_op jit(solution)/shard_map/all_to_all | solution.py:26
  47.2 5.4 %convert_bitcast_fusion = (f32[1024,4,320]{0,2,1:T(8,128)}, f32[4,1024,320]{1,2,0:T(8,128)}) fusion(bf16[4,1024,320]{1,2,0:T(8,128)(2,1)S(1)} %all-to-all-done), kind=kLoop, calls=%fused_computation.29 | loop fusion | flops 1310720 | bytes 13107200 | tf_op jit(solution)/shard_map/convert_element_type | solution.py:497
  52.5 8.1 %reshape.63 = f32[2,512,1280]{1,0,2:T(2,128)} reshape(f32[1024,4,320]{0,2,1:T(8,128)} %get-tuple-element.11) | data formatting | bytes 10485760 | tf_op jit(solution)/shard_map/convert_element_type | solution.py:497
  60.6 8.9 %copy.33 = f32[2,512,1280]{2,1,0:T(8,128)} copy(f32[2,512,1280]{1,0,2:T(2,128)} %reshape.63) | data formatting | bytes 10485760 | tf_op jit(solution)/shard_map/convert_element_type | solution.py:497
  69.6 6.0 %copy.34 = f32[1024,1280]{1,0:T(8,128)} copy(f32[1024,1280]{0,1:T(8,128)} %bitcast.92) | data formatting | bytes 10485760 | tf_op jit(solution)/shard_map/convert_element_type | solution.py:497
  75.6 3.8 %multiply_reduce_fusion = f32[2,1024]{1,0:T(2,128)S(1)} fusion(f32[2,1024]{1,0:T(2,128)S(1)} %convert_multiply_fusion, f32[1024,1280]{1,0:T(8,128)} %copy.34), kind=kLoop, calls=%fused_computation.1 | loop fusion | flops 7862272 | bytes 5259264 | tf_op jit(solution)/shard_map/reduce_sum | solution.py:498
  79.4 6.6 %multiply_convert_fusion = bf16[2,2,512,1280]{3,2,1,0:T(8,128)(2,1)} fusion(f32[1280]{0:T(1024)S(1)} %copy-done.6, f32[2,2,512]{2,1,0:T(2,128)S(1)} %rsqrt.12, f32[2,2,512]{2,1,0:T(2,128)S(1)} %mul.84, f32[2,512,1280]{2,1,0:T(8,128)} %copy.33), kind=kLoop, calls=%fused_computation | loop fusion | flops 10485760 | bytes 10507264 | tf_op jit(solution)/shard_map/convert_element_type | solution.py:499
  86.1 11.6 %all-gather.3.cloned.1.call-done = bf16[5,1280,320]{2,0,1:T(8,128)(2,1)} async-done(((bf16[5,20,320]{2,0,1:T(8,128)(2,1)}), bf16[5,1280,320]{2,0,1:T(8,128)(2,1)}) %all-gather.3.cloned.1.call-update) | async-done | bytes 4096016 | tf_op jit(solution)/shard_map/all_gather | solution.py:502
  97.7 23.4 %fusion.35 = (bf16[1,1280,320]{2,0,1:T(2,128)(2,1)}, bf16[1,1280,320]{2,0,1:T(2,128)(2,1)}, bf16[1,1280,320]{2,0,1:T(2,128)(2,1)}, bf16[1,1280,320]{2,0,1:T(2,128)(2,1)}, bf16[1,1280,320]{2,0,1:T(2,128)(2,1)S(1)}) fusion(bf16[5,1280,320]{2,0,1:T(8,128)(2,1)} %all-gather.3.cloned.1.call-done), kind=kLoop, calls=%fused_computation.53 | loop fusion | bytes 8192000 | tf_op jit(solution)/shard_map/slice | solution.py:101
  121.1 4.9 %copy.61 = bf16[1,1280,320]{1,2,0:T(8,128)(2,1)} copy(bf16[1,1280,320]{2,0,1:T(2,128)(2,1)} %get-tuple-element.6) | data formatting | bytes 1638400
  126.0 4.8 %copy.62 = bf16[1,1280,320]{1,2,0:T(8,128)(2,1)} copy(bf16[1,1280,320]{2,0,1:T(2,128)(2,1)} %get-tuple-element.7) | data formatting | bytes 1638400
  130.8 4.9 %copy.60 = bf16[1,1280,320]{1,2,0:T(8,128)(2,1)} copy(bf16[1,1280,320]{2,0,1:T(2,128)(2,1)} %get-tuple-element.8) | data formatting | bytes 1638400
  135.7 4.9 %copy.59 = bf16[1,1280,320]{1,2,0:T(8,128)(2,1)} copy(bf16[1,1280,320]{2,0,1:T(2,128)(2,1)} %get-tuple-element.9) | data formatting | bytes 1638400
  140.6 3.8 %copy.63 = bf16[1,1280,320]{1,2,0:T(8,128)(2,1)} copy(bf16[1,1280,320]{2,0,1:T(2,128)(2,1)S(1)} %get-tuple-element.10) | data formatting | bytes 1638400
  144.4 0.0 slice-start.1
  144.4 4.8 %fusion.4 = f32[2,2,512,320]{2,3,1,0:T(8,128)S(1)} fusion(bf16[2,2,512,1280]{3,2,1,0:T(8,128)(2,1)} %multiply_convert_fusion, bf16[1,1280,320]{1,2,0:T(8,128)(2,1)} %copy.60), kind=kOutput, calls=%fused_computation.6 | convolution fusion | flops 1677721600 | bytes 8683520 | tf_op jit(solution)/shard_map/vslc,co->vslo/dot_general | solution.py:98
  149.2 0.0 copy-start.4
  149.2 1.9 fusion.2
  151.2 0.0 slice-start.2
  151.2 1.9 fusion
  153.1 0.0 slice-start.3
  153.1 1.9 fusion.6
  155.1 2.7 fusion.16
  157.8 11.3 %all-gather.5.cloned.1.call-done = bf16[5,320,512]{1,2,0:T(8,128)(2,1)} async-done(((bf16[5,320,8]{1,2,0:T(8,128)(2,1)}), bf16[5,320,512]{1,2,0:T(8,128)(2,1)}) %all-gather.5.cloned.1.call-update) | async-done | bytes 1638416 | tf_op jit(solution)/shard_map/all_gather | solution.py:503
  169.0 3.3 fusion.18
  172.4 14.7 %fusion.19 = f32[2,2,512,512]{3,2,1,0:T(8,128)S(1)} fusion(bf16[2,2,512,320]{2,3,1,0:T(8,128)(2,1)S(1)} %fusion.16, bf16[5,320,512]{1,2,0:T(8,128)(2,1)S(1)} %copy-done), kind=kOutput, calls=%fused_computation.28 | convolution fusion | flops 671088640 | bytes 5898240 | tf_op jit(solution)/shard_map/vslc,co->vslo/dot_general | solution.py:98
  187.1 1.3 fusion.25
  188.4 2.2 fusion.17
  190.6 2.4 add_add_fusion
  193.0 2.4 copy.71
  195.5 4.9 %all-to-all-start.1 = ((f32[4,2,256,512]{3,2,1,0:T(8,128)}), f32[4,2,256,512]{3,2,1,0:T(8,128)}, u32[]{:S(2)}, u32[]{:S(2)}) async-start(f32[4,2,256,512]{3,2,1,0:T(8,128)} %bitcast.93), calls=%async_computation.1 | async-start | bytes 8388608 | tf_op jit(solution)/shard_map/all_to_all | solution.py:41
  200.3 0.1 dynamic_slice.3
  200.4 0.1 copy.48.alive_ref
  200.5 48.5 %all-to-all-done.1 = f32[4,2,256,512]{3,2,1,0:T(8,128)} async-done(((f32[4,2,256,512]{3,2,1,0:T(8,128)}), f32[4,2,256,512]{3,2,1,0:T(8,128)}, u32[]{:S(2)}, u32[]{:S(2)}) %all-to-all-start.1) | async-done | bytes 4194336 | tf_op jit(solution)/shard_map/all_to_all | solution.py:41
  249.0 2.8 reduce_sum.19.emb_ref
  251.8 1.7 moments.1.part_ref
  253.5 39.9 %total_moments.1.total_ref = f32[1408,128]{1,0:T(8,128)S(1)} custom-call(f32[2,1408,128]{2,1,0:T(8,128)S(1)} %moments.1.part_ref), custom_call_target="tpu_custom_call" | custom-call | tf_op jit(solution)/shard_map/total_moments/pallas_call | solution.py:271
  293.3 25.5 %inverse_factor.1.own_ref = f32[520,512]{1,0:T(8,128)S(1)} custom-call(f32[1408,128]{1,0:T(8,128)S(1)} %total_moments.1.total_ref), custom_call_target="tpu_custom_call" | custom-call | tf_op jit(solution)/shard_map/inverse_factor/pallas_call | solution.py:406
  318.8 3.7 %from_partner.1.other_ref = f32[520,512]{1,0:T(8,128)S(1)} custom-call(f32[520,512]{1,0:T(8,128)S(1)} %inverse_factor.1.own_ref), custom_call_target="tpu_custom_call" | custom-call | tf_op jit(solution)/shard_map/from_partner/pallas_call | solution.py:436
  322.5 3.7 %whitened_rows.1 = (f32[2,256,512]{2,1,0:T(8,128)}, f32[2,128]{1,0:T(2,128)}) custom-call(f32[2,256,512]{2,1,0:T(8,128)S(1)} %reduce_sum.19.emb_ref, f32[256,1]{1,0:T(8,128)S(1)} %copy.48.alive_ref, f32[520,512]{1,0:T(8,128)S(1)} %inverse_factor.1.own_ref, f32[520,512]{1,0:T(8,128)S(1)} %from_partner.1.other_ref), custom_call_target="tpu_custom_call" | custom-call | tf_op jit(solution)/shard_map/whitened_rows/pallas_call | solution.py:465
  (27 shorter events, 0.1 us)
Async XLA Ops:
  7.2 90.6 %all-gather.3.cloned.1.call-start = ((), (), s32[]{:S(2)}) async-start(), calls=%async_computation.2 | async-start | bytes 7987200 | tf_op jit(solution)/shard_map/all_gather | solution.py:502
  11.8 5.9 %copy-start.7 = (s32[2]{0:T(128)S(1)}, s32[2]{0:T(128)}, u32[]{:S(2)}) copy-start(s32[2]{0:T(128)} %param.8) | copy-start | bytes 28
  11.8 6.0 %copy-start.5 = (s32[2,1024]{1,0:T(2,128)S(1)}, s32[2,1024]{1,0:T(2,128)}, u32[]{:S(2)}) copy-start(s32[2,1024]{1,0:T(2,128)} %param.7) | copy-start | bytes 24580
  11.8 35.4 %all-to-all-start = ((bf16[4,1024,320]{1,2,0:T(8,128)(2,1)}), bf16[4,1024,320]{1,2,0:T(8,128)(2,1)S(1)}, u32[]{:S(2)}, u32[]{:S(2)}) async-start(bf16[4,1024,320]{1,2,0:T(8,128)(2,1)} %broadcast_in_dim.4), calls=%async_computation | async-start | bytes 5242880 | tf_op jit(solution)/shard_map/all_to_all | solution.py:26
  16.9 152.1 %all-gather.5.cloned.1.call-start = ((), (), s32[]{:S(2)}) async-start(), calls=%async_computation.3 | async-start | bytes 1996800 | tf_op jit(solution)/shard_map/all_gather | solution.py:503
  75.6 3.8 %copy-start.6 = (f32[1280]{0:T(1024)S(1)}, f32[1280]{0:T(1024)}, u32[]{:S(2)}) copy-start(f32[1280]{0:T(1024)} %param.9) | copy-start | bytes 15364
  140.6 8.6 %slice-start = ((s8[5242880]{0:T(1024)(128)(4,1)}), s8[1048576]{0:T(1024)(128)(4,1)S(1)}, s32[]{:S(2)}) async-start(s8[5242880]{0:T(1024)(128)(4,1)} %bitcast.95), calls=%async_computation.4 | async-start | bytes 2097152
  144.4 4.8 %slice-start.1 = ((s8[5242880]{0:T(1024)(128)(4,1)}), s8[4194304]{0:T(1024)(128)(4,1)S(1)}, s32[]{:S(2)}) async-start(s8[5242880]{0:T(1024)(128)(4,1)} %bitcast.95), calls=%async_computation.5 | async-start | bytes 8388608
  144.4 4.8 %copy-start.2 = (bf16[1,1280,320]{1,2,0:T(8,128)(2,1)S(1)}, bf16[1,1280,320]{1,2,0:T(8,128)(2,1)}, u32[]{:S(2)}) copy-start(bf16[1,1280,320]{1,2,0:T(8,128)(2,1)} %copy.62) | copy-start | bytes 2457604
  149.2 2.0 copy-start.4
  151.2 2.0 copy-start.3
  151.2 3.9 %slice-start.2 = ((s8[5242880]{0:T(1024)(128)(4,1)}), s8[4194304]{0:T(1024)(128)(4,1)S(1)}, s32[]{:S(2)}) async-start(s8[5242880]{0:T(1024)(128)(4,1)} %bitcast.97), calls=%async_computation.6 | async-start | bytes 8388608
  153.1 2.0 slice-start.3
  153.1 2.0 copy-start.1
  169.0 3.3 copy-start
  195.5 53.5 %all-to-all-start.1 = ((f32[4,2,256,512]{3,2,1,0:T(8,128)}), f32[4,2,256,512]{3,2,1,0:T(8,128)}, u32[]{:S(2)}, u32[]{:S(2)}) async-start(f32[4,2,256,512]{3,2,1,0:T(8,128)} %bitcast.93), calls=%async_computation.1 | async-start | bytes 8388608 | tf_op jit(solution)/shard_map/all_to_all | solution.py:41
Sparse Core Ops, SparseCore 0:
  11.3 86.3 all-gather.2
  100.4 68.6 all-gather.4

commit v2 on v1

--- a/solution.py
+++ b/solution.py
@@ -12,103 +12,6 @@
 
 EPS_NORM = 1e-05
 EPS_COV = 0.0001
-FULL_PRECISION = lax.Precision.HIGHEST
-
-
-def joined_along(pieces, dim):
-    pieces = jnp.moveaxis(pieces, 0, dim)
-    shape = pieces.shape
-    return pieces.reshape(*shape[:dim], shape[dim] * shape[dim + 1], *shape[dim + 2 :])
-
-
-def copy_for_each(array, axis):
-    copies = jnp.broadcast_to(array, (lax.axis_size(axis), *array.shape))
-    return lax.all_to_all(copies, axis, split_axis=0, concat_axis=0, tiled=True)
-
-
-def gathered_copies(array, axis, dim):
-    return joined_along(copy_for_each(array, axis), dim)
-
-
-def in_blocks(array, dim, size):
-    shape = array.shape
-    pieces = array.reshape(*shape[:dim], size, shape[dim] // size, *shape[dim + 1 :])
-    return jnp.moveaxis(pieces, dim, 0)
-
-
-def summed_on_arrival(array, axis, dim):
-    pieces = in_blocks(array, dim, lax.axis_size(axis))
-    arrived = lax.all_to_all(pieces, axis, split_axis=0, concat_axis=0, tiled=True)
-    return arrived.sum(axis=0)
-
-
-def sum_in_two_steps(array, axes, dim):
-    far, near = axes
-    own = summed_on_arrival(in_blocks(array, dim, lax.axis_size(far)), near, dim + 1)
-    return jnp.sum(lax.all_to_all(own, far, 0, 0, tiled=True), axis=0)
-
-
-def padded_to(lines, size):
-    spare = -lines.shape[0] % size
-    if not spare:
-        return lines
-    return jnp.concatenate([lines, jnp.zeros((spare, *lines.shape[1:]), lines.dtype)])
-
-
-def gathered_by_axis(array, axes, dim):
-    far, near = axes
-    pieces = copy_for_each(copy_for_each(array, far), near)
-    return joined_along(pieces.swapaxes(0, 1).reshape(-1, *array.shape), dim)
-
-
-def total_of(array, axes):
-    own = sum_in_two_steps(
-        padded_to(array, lax.axis_size(axes[0]) * lax.axis_size(axes[1])), axes, 0
-    )
-    whole = gathered_by_axis(own, axes, 0)
-    return whole[: len(array)].reshape(array.shape)
-
-
-def in_one(arrays, axis):
-    ends = [0]
-    for a in arrays:
-        ends.append(ends[-1] + a.size)
-    so_far = total_of(jnp.concatenate([a.ravel() for a in arrays]), axis)
-    return tuple((so_far[b:e].reshape(a.shape) for a, b, e in zip(arrays, ends, ends[1:])))
-
-
-def smooth_gate(values):
-    return (
-        0.5
-        * values
-        * (1.0 + jnp.tanh(0.7978845608 * (values + 0.044715 * values * values * values)))
-    )
-
-
-def pad_positions(inputs, dilation_step):
-    return jnp.pad(inputs, ((0, 0), (0, 0), (2 * dilation_step, 2 * dilation_step), (0, 0)))
-
-
-def conv_taps(padded, kernel_weight, dilation_step, length):
-    running = None
-    for kernel_tap in range(5):
-        offset_input = lax.slice_in_dim(
-            padded, kernel_tap * dilation_step, kernel_tap * dilation_step + length, axis=2
-        )
-        kernel_contribution = jnp.einsum(
-            "vslc,co->vslo",
-            offset_input,
-            kernel_weight[kernel_tap],
-            preferred_element_type=jnp.float32,
-        )
-        running = kernel_contribution if running is None else running + kernel_contribution
-    return running
-
-
-def whiten(factor, block_rows):
-    return jax.scipy.linalg.solve_triangular(factor, block_rows.T, lower=True).T
-
-
 HI = lax.Precision.HIGHEST
 MESH_IDS = pl.DeviceIdType.MESH
 Z, X, CORE, Y = "batch_0", "batch_1", "batch_2", "chan"
@@ -485,33 +388,299 @@
     return whitened_rows(embedded, alive, own, other)
 
 
+def gather_kernel(sizes, xt_ref, wa_ref, wb_ref, xt_out, wa_out, wb_out, sems):
+    depth, across, down = sizes
+    z, x = lax.axis_index(Z), lax.axis_index(X)
+    core, y = lax.axis_index(CORE), lax.axis_index(Y)
+    (xs, xr, zs, zr, ps, pr, cs, cr, local) = sems
+
+    barrier = pltpu.get_barrier_semaphore()
+    peers = [(lax.rem(z + s, depth), x, core, y) for s in range(1, depth)]
+    peers += [(z, lax.rem(x + s, across), core, y) for s in range(1, across)]
+    peers += [(z, x, core, lax.rem(y + s, down)) for s in range(1, down)]
+    peers += [(z, x, 1 - core, y)]
+    for peer in peers:
+        pl.semaphore_signal(barrier, inc=1, device_id=peer, device_id_type=MESH_IDS)
+    pl.semaphore_wait(barrier, len(peers))
+
+    started = []
+
+    def send(src, dst, send_sem, recv_sem, device):
+        copy = pltpu.make_async_remote_copy(
+            src_ref=src, dst_ref=dst, send_sem=send_sem, recv_sem=recv_sem,
+            device_id=device, device_id_type=MESH_IDS,
+        )
+        copy.start()
+        started.append(copy)
+        return copy
+
+    weights = ((wa_ref, wa_out), (wb_ref, wb_out))
+    own = []
+    for i, (src, dst) in enumerate(((xt_ref, xt_out.at[y]), (wa_ref, wa_out.at[z, x, core]), (wb_ref, wb_out.at[z, x, core]))):
+        copy = pltpu.make_async_copy(src, dst, local.at[i])
+        copy.start()
+        own.append(copy)
+    from_y = []
+    for s in (2, 1, 3):
+        from_y.append(send(xt_ref, xt_out.at[y], xs.at[s], xr.at[s], (z, x, core, lax.rem(y + s, down))))
+    along_z = {}
+    order = sorted(range(1, depth), key=lambda s: (min(s, depth - s), s))
+    for i, (src, dst) in enumerate(weights):
+        for s in order:
+            along_z[i, s] = send(
+                src, dst.at[z, x, core], zs.at[i, s], zr.at[i, s], (lax.rem(z + s, depth), x, core, y)
+            )
+    along_x, to_core = {}, {}
+
+    def to_partner(i, s, t):
+        zz = lax.rem(z + depth - s, depth)
+        xx = lax.rem(x + across - t, across)
+        src, dst = weights[i]
+        here = src if s == 0 and t == 0 else dst.at[zz, xx, core]
+        to_core[i, s, t] = send(
+            here, dst.at[zz, xx, core], cs.at[i, s, t], cr.at[i, s, t], (z, x, 1 - core, y)
+        )
+
+    for i, (src, dst) in enumerate(weights):
+        for s in [0] + order:
+            zz = lax.rem(z + depth - s, depth)
+            if s:
+                along_z[i, s].wait_recv()
+            here = dst.at[zz, x, core] if s else src
+            for t in range(1, across):
+                along_x[i, s, t] = send(
+                    here, dst.at[zz, x, core], ps.at[i, s, t], pr.at[i, s, t],
+                    (z, lax.rem(x + t, across), core, y),
+                )
+            to_partner(i, s, 0)
+    for i in range(2):
+        for s in [0] + order:
+            for t in range(1, across):
+                along_x[i, s, t].wait_recv()
+                to_partner(i, s, t)
+    for copy in to_core.values():
+        copy.wait_recv()
+    for copy in from_y:
+        copy.wait_recv()
+    for copy in started:
+        copy.wait_send()
+    for copy in own:
+        copy.wait()
+
+
+def gathered_inputs(xt, wa, wb, sizes):
+    depth, across, down = sizes
+    dma = pltpu.SemaphoreType.DMA
+    anywhere = pl.BlockSpec(memory_space=pl.ANY)
+
+    def kernel(xt_ref, wa_ref, wb_ref, xt_out, wa_out, wb_out, *sems):
+        gather_kernel(sizes, xt_ref, wa_ref, wb_ref, xt_out, wa_out, wb_out, sems)
+
+    return pl.pallas_call(
+        kernel,
+        out_shape=(
+            jax.ShapeDtypeStruct((down, *xt.shape), xt.dtype),
+            jax.ShapeDtypeStruct((depth, across, 2, *wa.shape), wa.dtype),
+            jax.ShapeDtypeStruct((depth, across, 2, *wb.shape), wb.dtype),
+        ),
+        in_specs=[anywhere] * 3,
+        out_specs=(anywhere,) * 3,
+        scratch_shapes=[
+            dma((down,)), dma((down,)),
+            dma((2, depth)), dma((2, depth)),
+            dma((2, depth, across)), dma((2, depth, across)),
+            dma((2, depth, across)), dma((2, depth, across)),
+            dma((3,)),
+        ],
+        compiler_params=pltpu.CompilerParams(collective_id=3, has_side_effects=True),
+        name="gathered_inputs",
+    )(xt, wa, wb)
+
+
+def gate(values):
+    return 0.5 * values * (1.0 + jnp.tanh(0.7978845608 * (values + 0.044715 * values * values * values)))
+
+
+PAD = 8
+ROWS = 128
+
+
+def conv_kernel(
+    sizes, xt_ref, wa_ref, wb_ref, gain_ref, kept_ref, out_ref, n_ref, w_ref, stage, p_ref, h_ref, q_ref, cols
+):
+    sequences, length, out_width, taps = sizes
+    channels, tokens = xt_ref.shape
+    chunks, chunk_rows, lanes = wa_ref.shape
+    eye = lax.broadcasted_iota(jnp.int32, (BLOCK, BLOCK), 0) == lax.broadcasted_iota(
+        jnp.int32, (BLOCK, BLOCK), 1
+    )
+    squares = jnp.zeros((1, tokens), jnp.float32)
+    for i in range(channels // BLOCK):
+        part = xt_ref[i * BLOCK : (i + 1) * BLOCK, :].astype(jnp.float32)
+        squares = squares + jnp.sum(part * part, axis=0, keepdims=True)
+    scale = lax.rsqrt(squares / channels + EPS_NORM)
+    for i in range(channels // BLOCK):
+        part = xt_ref[i * BLOCK : (i + 1) * BLOCK, :].astype(jnp.float32)
+        gain = jnp.sum(
+            jnp.where(eye, jnp.broadcast_to(gain_ref[i : i + 1, :], (BLOCK, BLOCK)), 0.0), axis=1, keepdims=True
+        )
+        normed = (part * scale * gain).astype(jnp.bfloat16)
+        n_ref[:, i * BLOCK : (i + 1) * BLOCK] = normed.T
+
+    position = lax.broadcasted_iota(jnp.int32, (GROUP, tokens), 1) % length
+    for k in range(taps):
+        move = k - taps // 2
+        rolled = kept_ref[...] if move == 0 else pltpu.roll(kept_ref[...], (-move) % tokens, 1)
+        inside = (position + move >= 0) & (position + move < length)
+        cols[k] = jnp.where(inside, rolled, 0.0).T
+
+    group = 4
+    def relay(q, _):
+        for i in range(group):
+            stage[i * chunk_rows : (i + 1) * chunk_rows, :] = wa_ref[q * group + i].astype(jnp.float32)
+        at = pl.multiple_of(q * group * chunk_rows, group * chunk_rows)
+        w_ref[pl.ds(at, group * chunk_rows), :] = stage[...].astype(jnp.bfloat16)
+        return 0
+
+    lax.fori_loop(0, chunks // group, relay, 0)
+
+    width = lanes // taps
+    for pad in (p_ref, q_ref):
+        pad[0:PAD, :] = jnp.zeros((PAD, pad.shape[1]), jnp.float32)
+        pad[PAD + length :, :] = jnp.zeros((PAD, pad.shape[1]), jnp.float32)
+
+    def sequence(s, _):
+        start = pl.multiple_of(s * length, length)
+        for r in range(length // ROWS):
+            p_ref[PAD + r * ROWS : PAD + (r + 1) * ROWS, :] = jnp.dot(
+                n_ref[pl.ds(start + r * ROWS, ROWS), :], w_ref[...], preferred_element_type=jnp.float32
+            )
+        for r in range(length // ROWS):
+            for v in range(2):
+                acc = None
+                for k in range(taps):
+                    first = PAD + r * ROWS + k - taps // 2
+                    piece = p_ref[first : first + ROWS, k * width : (k + 1) * width]
+                    piece = piece * cols[k, pl.ds(start + r * ROWS, ROWS), v : v + 1]
+                    acc = piece if acc is None else acc + piece
+                h_ref[v, r * ROWS : (r + 1) * ROWS, :] = gate(acc).astype(jnp.bfloat16)
+        for v in range(2):
+            for k in range(taps):
+                taps_b = wb_ref[:, k].astype(jnp.float32).reshape(out_width, width).astype(jnp.bfloat16)
+                q_ref[PAD : PAD + length, :] = lax.dot_general(
+                    h_ref[v], taps_b, (((1,), (1,)), ((), ())), preferred_element_type=jnp.float32
+                )
+                first = PAD + 2 * (k - taps // 2)
+                piece = q_ref[first : first + length, :]
+                if k == 0:
+                    out_ref[v, pl.ds(start, length), :] = piece
+                else:
+                    out_ref[v, pl.ds(start, length), :] += piece
+        return 0
+
+    lax.fori_loop(0, sequences, sequence, 0)
+
+
+def conv_block(xt, wa, wb, gain, kept, sequences):
+    channels, tokens = xt.shape
+    chunks, chunk_rows, lanes = wa.shape
+    taps, rows, width = wb.shape[1:]
+    out_width = wb.shape[0] * rows
+    length = tokens // sequences
+    sizes = (sequences, length, out_width, taps)
+    bf, f32 = jnp.bfloat16, jnp.float32
+
+    def kernel(*refs):
+        conv_kernel(sizes, *refs)
+
+    return pl.pallas_call(
+        kernel,
+        out_shape=jax.ShapeDtypeStruct((2, tokens, out_width), f32),
+        in_specs=[in_vmem()] * 5,
+        out_specs=in_vmem(),
+        scratch_shapes=[
+            pltpu.VMEM((tokens, channels), bf),
+            pltpu.VMEM((channels, lanes), bf),
+            pltpu.VMEM((4 * chunk_rows, lanes), f32),
+            pltpu.VMEM((length + 2 * PAD, lanes), f32),
+            pltpu.VMEM((2, length, width), bf),
+            pltpu.VMEM((length + 2 * PAD, out_width), f32),
+            pltpu.VMEM((taps, tokens, GROUP), f32),
+        ],
+        compiler_params=pltpu.CompilerParams(vmem_limit_bytes=60 << 20),
+        name="conv_block",
+    )(xt, wa, wb, gain, kept)
+
+
+def spread_sum_kernel(down, part_ref, out_ref, inbox, send, recv):
+    z, x = lax.axis_index(Z), lax.axis_index(X)
+    core, y = lax.axis_index(CORE), lax.axis_index(Y)
+    rows = out_ref.shape[1]
+    barrier = pltpu.get_barrier_semaphore()
+    for s in range(1, down):
+        pl.semaphore_signal(
+            barrier, inc=1, device_id=(z, x, core, lax.rem(y + s, down)), device_id_type=MESH_IDS
+        )
+    pl.semaphore_wait(barrier, down - 1)
+    copies = []
+    for s in (2, 1, 3):
+        other = lax.rem(y + s, down)
+        copy = pltpu.make_async_remote_copy(
+            src_ref=part_ref.at[:, pl.ds(pl.multiple_of(other * rows, rows), rows), :],
+            dst_ref=inbox.at[s],
+            send_sem=send.at[s], recv_sem=recv.at[s],
+            device_id=(z, x, core, other), device_id_type=MESH_IDS,
+        )
+        copy.start()
+        copies.append(copy)
+    for copy in copies:
+        copy.wait()
+    mine = part_ref[:, pl.ds(pl.multiple_of(y * rows, rows), rows), :]
+    out_ref[...] = ((mine + inbox[1]) + inbox[2]) + inbox[3]
+
+
+def spread_sum(part, down):
+    views, tokens, width = part.shape
+    rows = tokens // down
+    dma = pltpu.SemaphoreType.DMA
+    return pl.pallas_call(
+        lambda *refs: spread_sum_kernel(down, *refs),
+        out_shape=jax.ShapeDtypeStruct((views, rows, width), jnp.float32),
+        in_specs=[in_vmem()],
+        out_specs=in_vmem(),
+        scratch_shapes=[
+            pltpu.VMEM((down, views, rows, width), jnp.float32), dma((down,)), dma((down,)),
+        ],
+        compiler_params=pltpu.CompilerParams(
+            collective_id=4, has_side_effects=True, vmem_limit_bytes=32 << 20
+        ),
+        name="spread_sum",
+    )(part)
+
+
 def shards(monomers, keep_mask, lengths, norm_gain, weight_a, weight_b):
     sequences = lengths.shape[0]
-    tokens_dev = monomers.shape[0]
-    length = tokens_dev // sequences
-    channel_count = norm_gain.shape[0]
+    tokens = monomers.shape[0]
+    length = tokens // sequences
+    taps, rows, width = weight_a.shape
+    sizes = (lax.axis_size(Z), lax.axis_size(X), lax.axis_size(Y))
     positions = lax.broadcasted_iota(jnp.int32, (sequences, length), 1)
-    alive = (positions < lengths[:, None]).astype(jnp.float32).reshape(tokens_dev)
-    kept_rows = keep_mask.astype(jnp.float32) * alive[None, :]
-    gathered = gathered_copies(monomers, "chan", 1)
-    viewed = gathered.astype(jnp.float32)[None] * kept_rows[:, :, None]
-    square_mean = jnp.mean(viewed * viewed, axis=-1, keepdims=True)
-    normed = (viewed * lax.rsqrt(square_mean + EPS_NORM) * norm_gain).astype(jnp.bfloat16)
-    padded_in = pad_positions(normed.reshape(2, sequences, length, channel_count), 1)
-    full_a, full_b = (
-        lax.all_gather(weight_a, BATCH, axis=1, tiled=True),
-        lax.all_gather(weight_b, BATCH, axis=2, tiled=True),
-    )
-    hidden_pre = conv_taps(padded_in, full_a, 1, length)
-    hidden = smooth_gate(hidden_pre).astype(jnp.bfloat16)
-    padded_hidden = pad_positions(hidden, 2)
-    partial_embed = conv_taps(padded_hidden, full_b, 2, length)
-    partial_embed = partial_embed.reshape(2, tokens_dev, partial_embed.shape[3])
-    embedded = summed_on_arrival(partial_embed, "chan", 1)
-    row_count = embedded.shape[1]
-    embed_width = embedded.shape[2]
-    own_alive = lax.dynamic_slice_in_dim(alive, lax.axis_index("chan") * row_count, row_count, 0)
-    sizes = (lax.axis_size(Z), lax.axis_size(X), lax.axis_size(Y))
+    alive = (positions < lengths[:, None]).astype(jnp.float32).reshape(tokens)
+    kept = keep_mask.astype(jnp.float32) * alive[None, :]
+    kept = jnp.pad(kept, ((0, GROUP - 2), (0, 0)))
+    wa = weight_a.transpose(1, 0, 2).reshape(rows, taps * width)
+    xt, wa, wb = gathered_inputs(monomers.T, wa, weight_b.transpose(0, 2, 1), sizes)
+    part = conv_block(
+        xt.reshape(-1, tokens),
+        wa.reshape(-1, *wa.shape[3:]),
+        wb.reshape(-1, *wb.shape[3:]),
+        norm_gain.reshape(-1, BLOCK),
+        kept,
+        sequences,
+    )
+    embedded = spread_sum(part, sizes[2])
+    own = embedded.shape[1]
+    own_alive = lax.dynamic_slice_in_dim(alive, lax.axis_index(Y) * own, own, 0)
     return whitening(embedded, own_alive, sizes)
 
 

time: 334 us -> 208 us (0.62)
  Pallas kernels: 74.3 us -> 201 us
  waiting for transfers between devices: 101 us -> 0 us
  local copies, waits for them, and re-layouts: 77.1 us -> 4.69 us
  matrix products: 37.1 us -> 0 us
  other arithmetic: 18.6 us -> 1.43 us
  between operations: 14.5 us -> 0.7 us
  starting transfers between devices: 10 us -> 0 us
    pallas_call x0 -> x3, Pallas kernels: none -> 126 us  [the longest x1 54.7 us: gathered_inputs(): pl.pallas_call(kernel, out_shape=(jax.ShapeDtypeStruct((down, *xt.shape),...]
    all_to_all x2 -> x0, waiting for transfers between devices: 77.8 us -> none  [the longest x1 48.5 us: summed_on_arrival(): lax.all_to_all(pieces, axis, split_axis=0, concat_axis=0, tiled=True)]
    dot_general x10 -> x0, matrix products: 37.1 us -> none  [conv_taps(): jnp.einsum('vslc,co->vslo', offset_input, kernel_weight[kernel_tap], pref...]
    slice x1 -> x0, local copies, waits for them, and re-layouts: 23.4 us -> none  [conv_taps(): kernel_weight[kernel_tap]]
    convert_element_type x3 -> x0, local copies, waits for them, and re-layouts: 23.1 us -> none  [shards(): viewed = gathered.astype(jnp.float32)[None] * kept_rows[:, :, None]]
    all_gather x2 -> x0, waiting for transfers between devices: 22.9 us -> none  [the longest x1 11.6 us: shards(): lax.all_gather(weight_a, BATCH, axis=1, tiled=True)]
    unnamed x31 -> x3, local copies, waits for them, and re-layouts: 24.8 us -> 2.19 us
    convert_element_type x2 -> x0, other arithmetic: 12 us -> none  [the longest x1 6.63 us: shards(): (viewed * lax.rsqrt(square_mean + EPS_NORM) * norm_gain).astype(jnp.bfloa...]
  transfers between devices with their start and end apart: 4 -> 0, of which waited for: 4 -> 0; matrix products, arithmetic and copies ran while one was open for 31% -> 0% of each run, Pallas kernels for 0% -> 0%
where the time goes in v2:
time: 208 us
  Pallas kernels  201 us (97%)
  local copies, waits for them, and re-layouts  4.69 us (2%)
    pallas_call x1, Pallas kernels, gathered_inputs(): pl.pallas_call(kernel, out_shape=(jax.ShapeDtypeStruct((down, *xt.shape),...  54.7 us
    pallas_call x1, Pallas kernels, spread_sum(): pl.pallas_call(lambda *refs: spread_sum_kernel(down, *refs), out_shape=ja...  49.7 us
    pallas_call x1, Pallas kernels, total_moments(): pl.pallas_call(kernel, out_shape=jax.ShapeDtypeStruct((all_rows, lanes),...  37.8 us
    pallas_call x1, Pallas kernels, inverse_factor(): pl.pallas_call(factor_kernel, out_shape=jax.ShapeDtypeStruct((width + GRO...  25.7 us
    pallas_call x1, Pallas kernels, conv_block(): pl.pallas_call(kernel, out_shape=jax.ShapeDtypeStruct((2, tokens, out_wid...  22.1 us
    pallas_call x1, Pallas kernels, from_partner(): pl.pallas_call(swap_kernel, out_shape=jax.ShapeDtypeStruct(own.shape, own...  6.12 us

profile of v2, /device:TPU:1, one launch (start us, length us, event | category | flops | bytes accessed | tf_op | source)
XLA Modules:
  0.0 208.2 jit_solution(5583664880989119940)
XLA Ops:
  0.6 0.9 copy.9
  1.5 0.8 reshape.43.wa_ref
  2.3 54.7 %gathered_inputs.1 = (bf16[4,320,1024]{2,1,0:T(8,128)(2,1)}, bf16[8,4,2,20,1600]{4,3,2,1,0:T(8,128)(2,1)}, bf16[8,4,2,5,8,320]{5,4,3,2,1,0:T(8,128)(2,1)}) custom-call(bf16[320,1024]{1,0:T(8,128)(2,1)} %bitcast.15, bf16[20,1600]{1,0:T(8,128)(2,1)} %reshape.43.wa_ref, bf16[5,8,320]{2,1,0:T(8,128)(2,1)} %bitcast.17), custom_call_target="tpu_custom_call" | custom-call | tf_op jit(solution)/shard_map/gathered_inputs/pallas_call | solution.py:479
  57.0 0.7 fusion
  57.7 0.7 convert_multiply_fusion
  58.4 0.6 pad.4.refs_4_
  59.0 22.1 %conv_block.1.refs_0_ = f32[2,1024,512]{2,1,0:T(8,128)} custom-call(bf16[1280,1024]{1,0:T(8,128)(2,1)} %bitcast.13, bf16[64,20,1600]{2,1,0:T(8,128)(2,1)} %bitcast.12, bf16[64,5,8,320]{3,2,1,0:T(8,128)(2,1)} %bitcast.14, f32[10,128]{1,0:T(8,128)} %bitcast.20, f32[8,1024]{1,0:T(8,128)} %pad.4.refs_4_), custom_call_target="tpu_custom_call" | custom-call | tf_op jit(solution)/shard_map/conv_block/pallas_call | solution.py:596
  81.1 0.0 copy-start
  81.1 2.2 %copy-done = f32[2,1024,512]{2,1,0:T(8,128)S(1)} copy-done((f32[2,1024,512]{2,1,0:T(8,128)S(1)}, f32[2,1024,512]{2,1,0:T(8,128)}, u32[]{:S(2)}) %copy-start) | copy-done | bytes 4194328
  83.3 49.7 %spread_sum.1.emb_ref = f32[2,256,512]{2,1,0:T(8,128)S(1)} custom-call(f32[2,1024,512]{2,1,0:T(8,128)S(1)} %copy-done), custom_call_target="tpu_custom_call" | custom-call | tf_op jit(solution)/shard_map/spread_sum/pallas_call | solution.py:646
  133.0 0.1 dynamic_slice.3
  133.1 0.1 copy.11.alive_ref
  133.3 1.7 moments.1.part_ref
  134.9 37.8 %total_moments.1.total_ref = f32[1408,128]{1,0:T(8,128)S(1)} custom-call(f32[2,1408,128]{2,1,0:T(8,128)S(1)} %moments.1.part_ref), custom_call_target="tpu_custom_call" | custom-call | tf_op jit(solution)/shard_map/total_moments/pallas_call | solution.py:174
  172.7 25.7 %inverse_factor.1.own_ref = f32[520,512]{1,0:T(8,128)S(1)} custom-call(f32[1408,128]{1,0:T(8,128)S(1)} %total_moments.1.total_ref), custom_call_target="tpu_custom_call" | custom-call | tf_op jit(solution)/shard_map/inverse_factor/pallas_call | solution.py:309
  198.4 6.1 %from_partner.1.other_ref = f32[520,512]{1,0:T(8,128)S(1)} custom-call(f32[520,512]{1,0:T(8,128)S(1)} %inverse_factor.1.own_ref), custom_call_target="tpu_custom_call" | custom-call | tf_op jit(solution)/shard_map/from_partner/pallas_call | solution.py:339
  204.5 3.7 %whitened_rows.1 = (f32[2,256,512]{2,1,0:T(8,128)}, f32[2,128]{1,0:T(2,128)}) custom-call(f32[2,256,512]{2,1,0:T(8,128)S(1)} %spread_sum.1.emb_ref, f32[256,1]{1,0:T(8,128)S(1)} %copy.11.alive_ref, f32[520,512]{1,0:T(8,128)S(1)} %inverse_factor.1.own_ref, f32[520,512]{1,0:T(8,128)S(1)} %from_partner.1.other_ref), custom_call_target="tpu_custom_call" | custom-call | tf_op jit(solution)/shard_map/whitened_rows/pallas_call | solution.py:368
  (1 shorter events, 0.0 us)
Async XLA Ops:
  81.1 2.2 %copy-start = (f32[2,1024,512]{2,1,0:T(8,128)S(1)}, f32[2,1024,512]{2,1,0:T(8,128)}, u32[]{:S(2)}) copy-start(f32[2,1024,512]{2,1,0:T(8,128)} %conv_block.1.refs_0_) | copy-start | bytes 12582916

commit v3 on v2

v3 whole, which is shorter than its diff:
```python
import jax
import jax.numpy as jnp
from jax import lax
from jax.experimental import pallas as pl
from jax.experimental.pallas import tpu as pltpu
from jax.sharding import Mesh
from jax.sharding import PartitionSpec as P

BATCH = ("batch_0", "batch_1", "batch_2")
BATCH_CHAN = ("batch_0", "batch_1", "batch_2", "chan")


EPS_NORM = 1e-05
EPS_COV = 0.0001
HI = lax.Precision.HIGHEST
MESH_IDS = pl.DeviceIdType.MESH
Z, X, CORE, Y = "batch_0", "batch_1", "batch_2", "chan"
AXES = (Z, X, CORE, Y)
BLOCK = 128
GROUP = 8


def dot_of(a, b, dims, precision=HI):
    return lax.dot_general(
        a, b, (dims, ((), ())), precision=precision, preferred_element_type=jnp.float32
    )


def in_vmem():
    return pl.BlockSpec(memory_space=pltpu.VMEM)


def block_pairs(width):
    return [(i, k) for i in range(width // BLOCK) for k in range(i + 1)]


def share_rows(width, planes):
    rows = len(block_pairs(width)) * BLOCK + GROUP
    return -(-rows // (planes * GROUP)) * GROUP


def alive_column(lengths_ref, tokens, length):
    start = lax.axis_index(Y) * tokens
    limit = lengths_ref[start // length] - lax.rem(start, length)
    return jnp.where(lax.broadcasted_iota(jnp.int32, (tokens, 1), 0) < limit, 1.0, 0.0)


def in_smem():
    return pl.BlockSpec(memory_space=pltpu.SMEM)


def moments_into(emb_ref, alive, out_ref):
    views, tokens, width = emb_ref.shape
    pairs = block_pairs(width)
    at = len(pairs) * BLOCK
    for v in range(views):
        masked = emb_ref[v] * alive
        for i in range(width // BLOCK):
            wide = (i + 1) * BLOCK
            strip = dot_of(
                masked[:, i * BLOCK : wide], masked[:, :wide], ((0,), (0,))
            )
            for k in range(i + 1):
                b = pairs.index((i, k))
                out_ref[v, b * BLOCK : (b + 1) * BLOCK, :] = strip[:, k * BLOCK : (k + 1) * BLOCK]
        out_ref[v, at:, :] = jnp.zeros((out_ref.shape[1] - at, BLOCK), jnp.float32)
        sums = jnp.sum(masked, axis=0, keepdims=True)
        for k in range(width // BLOCK):
            out_ref[v, at + k : at + k + 1, :] = sums[:, k * BLOCK : (k + 1) * BLOCK]
        count = jnp.sum(alive, axis=0, keepdims=True)
        last = at + width // BLOCK
        out_ref[v, last : last + 1, :] = jnp.broadcast_to(count, (1, BLOCK))


def total_kernel(sizes, parts, part_ref, out_ref, pair_in, mine, plane_in, share, line_in, total, *sems):
    depth, across, down = sizes
    planes = across * down
    rows = share.shape[0]
    z, x = lax.axis_index(Z), lax.axis_index(X)
    core, y = lax.axis_index(CORE), lax.axis_index(Y)
    me = x * down + y
    partner = 1 - core
    pair_send, pair_recv, plane_send, plane_recv, line_send, line_recv, back_send, back_recv = sems

    def in_plane(step):
        other = lax.rem(me + step, planes)
        return other, (z, other // down, core, lax.rem(other, down))

    def in_line(step):
        other = lax.rem(z + step, depth)
        return other, (other, x, core, y)

    barrier = pltpu.get_barrier_semaphore()
    pl.semaphore_signal(barrier, inc=1, device_id=(z, x, partner, y), device_id_type=MESH_IDS)
    for step in range(1, planes):
        pl.semaphore_signal(barrier, inc=1, device_id=in_plane(step)[1], device_id_type=MESH_IDS)
    for step in range(1, depth):
        pl.semaphore_signal(barrier, inc=1, device_id=in_line(step)[1], device_id_type=MESH_IDS)
    pl.semaphore_wait(barrier, 1 + planes - 1 + depth - 1)

    def sent(src, dst, send, recv, device):
        copy = pltpu.make_async_remote_copy(
            src_ref=src, dst_ref=dst, send_sem=send, recv_sem=recv,
            device_id=device, device_id_type=MESH_IDS,
        )
        copy.start()
        return copy

    sent(part_ref.at[partner], pair_in, pair_send, pair_recv, (z, x, partner, y)).wait()
    mine[...] = part_ref[core] + pair_in[...]

    starts = [sum(parts[:i]) for i in range(len(parts))]

    def rows_of(index, i):
        return pl.ds(pl.multiple_of(index * rows + starts[i], GROUP), parts[i])

    def within(i):
        return pl.ds(starts[i], parts[i])

    def summed(buffer, own, count, i):
        acc = None
        for source in range(count):
            piece = buffer[lax.rem(own - source + count, count), within(i)]
            acc = piece if acc is None else acc + piece
        return acc

    spread, lines, back = {}, {}, {}
    for i in range(len(parts)):
        for step in range(1, planes):
            other, device = in_plane(step)
            spread[i, step] = sent(
                mine.at[rows_of(other, i)], plane_in.at[step, within(i)],
                plane_send.at[i, step], plane_recv.at[i, step], device,
            )

    def to_line(i):
        for step in range(1, planes):
            spread[i, step].wait_recv()
        plane_in[0, within(i)] = mine[rows_of(me, i)]
        share[within(i)] = summed(plane_in, me, planes, i)
        for step in range(1, depth):
            lines[i, step] = sent(
                share.at[within(i)], line_in.at[step, within(i)],
                line_send.at[i, step], line_recv.at[i, step], in_line(step)[1],
            )

    def to_plane(i):
        for step in range(1, depth):
            lines[i, step].wait_recv()
        line_in[0, within(i)] = share[within(i)]
        total[within(i)] = summed(line_in, z, depth, i)
        for step in range(1, planes):
            back[i, step] = sent(
                total.at[within(i)], out_ref.at[rows_of(me, i)],
                back_send.at[i, step], back_recv.at[i, step], in_plane(step)[1],
            )
        out_ref[rows_of(me, i)] = total[within(i)]

    lag = 2
    for i in range(len(parts) + lag):
        if i < len(parts):
            to_line(i)
        if i >= lag:
            to_plane(i - lag)
    for copy in back.values():
        copy.wait_recv()
    for group in (spread, lines, back):
        for copy in group.values():
            copy.wait_send()


def total_moments(parts, mesh_sizes):
    depth, across, down = mesh_sizes
    planes = across * down
    _, all_rows, lanes = parts.shape
    rows = all_rows // planes
    tiles = rows // GROUP
    pieces = tuple(GROUP * (tiles // 4 + (1 if i < tiles % 4 else 0)) for i in range(4))
    dma = pltpu.SemaphoreType.DMA
    vm = lambda *shape: pltpu.VMEM(shape, jnp.float32)
    return pl.pallas_call(
        lambda *refs: total_kernel(mesh_sizes, pieces, *refs),
        out_shape=jax.ShapeDtypeStruct((all_rows, lanes), jnp.float32),
        in_specs=[in_vmem()],
        out_specs=in_vmem(),
        scratch_shapes=[
            vm(all_rows, lanes),
            vm(all_rows, lanes),
            vm(planes, rows, lanes),
            vm(rows, lanes),
            vm(depth, rows, lanes),
            vm(rows, lanes),
            dma, dma,
            dma((4, planes)), dma((4, planes)),
            dma((4, depth)), dma((4, depth)),
            dma((4, planes)), dma((4, planes)),
        ],
        compiler_params=pltpu.CompilerParams(
            collective_id=1, has_side_effects=True, vmem_limit_bytes=32 << 20
        ),
        name="total_moments",
    )(parts)


def splat_row(v, a):
    return jnp.broadcast_to(v[a : a + 1, :], (GROUP, BLOCK))


def splat_lane(v, j):
    return jnp.broadcast_to(v[:, j : j + 1], (GROUP, BLOCK))


def base_inverse(load, store):
    count = BLOCK // GROUP
    groups = [load(g) for g in range(count)]
    lane = lax.broadcasted_iota(jnp.int32, (GROUP, BLOCK), 1)
    sub = lax.broadcasted_iota(jnp.int32, (GROUP, BLOCK), 0)
    steps = range(GROUP)
    for p in range(count):
        j = GROUP * p
        v = groups[p]
        cols = [splat_lane(v, j + a) for a in steps]
        e = [[splat_row(cols[a], b) if b >= a else None for a in steps] for b in steps]
        low = [[None] * GROUP for _ in steps]
        rec = []
        for a in steps:
            rec.append(1.0 / e[a][a])
            for b in range(a + 1, GROUP):
                low[b][a] = e[b][a] * rec[a]
            for b in range(a + 1, GROUP):
                for c in range(a + 1, b + 1):
                    e[b][c] = e[b][c] - low[b][a] * e[c][a]
        panel = (lane >= j) & (lane < j + GROUP)
        rows = []
        for a in steps:
            r = jnp.where(panel, jnp.where(lane == j + a, 1.0, 0.0), splat_row(v, a))
            for b in range(a):
                r = r - low[a][b] * rows[b]
            rows.append(r)
        out = None
        for a in steps:
            r = rows[a] * lax.rsqrt(e[a][a])
            out = r if out is None else jnp.where(sub == a, r, out)
        store(p, jnp.where(lane < j + GROUP, out, 0.0))
        for g in range(p + 1, count):
            x = groups[g]
            w = []
            acc = jnp.where(panel, 0.0, x)
            for a in steps:
                t = splat_lane(x, j + a)
                for b in range(a):
                    t = t - low[a][b] * w[b]
                w.append(t)
                acc = acc - (t * rec[a]) * rows[a]
            groups[g] = acc


def factor_kernel(total_ref, out_ref, work, m_ref):
    width = work.shape[1]
    blocks = width // BLOCK
    pairs = block_pairs(width)
    at = len(pairs) * BLOCK
    tail = total_ref[at : at + GROUP, :]
    count = tail[blocks : blocks + 1, 0:1]
    center = jnp.concatenate([tail[k : k + 1, :] for k in range(blocks)], axis=1) / count
    first = lax.broadcasted_iota(jnp.int32, (GROUP, width), 0) == 0
    center8 = jnp.where(first, jnp.broadcast_to(center, (GROUP, width)), 0.0)
    eye = lax.broadcasted_iota(jnp.int32, (BLOCK, BLOCK), 0) == lax.broadcasted_iota(
        jnp.int32, (BLOCK, BLOCK), 1
    )
    for b, (i, k) in enumerate(pairs):
        outer = dot_of(
            center8[:, i * BLOCK : (i + 1) * BLOCK], center8[:, k * BLOCK : (k + 1) * BLOCK], ((0,), (0,))
        )
        block = total_ref[b * BLOCK : (b + 1) * BLOCK, :] / count - outer
        if i == k:
            block = block + jnp.where(eye, EPS_COV, 0.0)
        work[i * BLOCK : (i + 1) * BLOCK, k * BLOCK : (k + 1) * BLOCK] = block
        if i != k:
            work[k * BLOCK : (k + 1) * BLOCK, i * BLOCK : (i + 1) * BLOCK] = block.T
    row_block = lax.broadcasted_iota(jnp.int32, (width, BLOCK), 0) // BLOCK
    col_block = lax.broadcasted_iota(jnp.int32, (width, width), 1) // BLOCK
    strip_block = lax.broadcasted_iota(jnp.int32, (BLOCK, width), 1) // BLOCK
    strip_eye = jnp.where(
        lax.broadcasted_iota(jnp.int32, (BLOCK, width), 1) % BLOCK
        == lax.broadcasted_iota(jnp.int32, (BLOCK, width), 0),
        1.0,
        0.0,
    )

    def step(k, _):
        here = pl.multiple_of(k * BLOCK, BLOCK)

        def load(g):
            return work[pl.ds(pl.multiple_of(here + GROUP * g, GROUP), GROUP), pl.ds(here, BLOCK)]

        def store(g, val):
            m_ref[GROUP * g : GROUP * (g + 1), :] = val

        base_inverse(load, store)
        m = m_ref[...]
        col = jnp.where(row_block > k, work[:, pl.ds(here, BLOCK)], 0.0)
        left = dot_of(col, m, ((1,), (1,)))
        row = jnp.where(strip_block == k, strip_eye, work[pl.ds(here, BLOCK), :])
        across = dot_of(m, row, ((1,), (0,)))
        work[...] = jnp.where(col_block == k, 0.0, work[...]) - dot_of(left, across, ((1,), (0,)))
        work[pl.ds(here, BLOCK), :] = jnp.where(strip_block <= k, across, 0.0)
        return 0

    lax.fori_loop(0, blocks, step, 0)
    out_ref[:width, :] = work[...]
    out_ref[width:, :] = center8


def inverse_factor(total, width):
    return pl.pallas_call(
        factor_kernel,
        out_shape=jax.ShapeDtypeStruct((width + GROUP, width), jnp.float32),
        in_specs=[in_vmem()],
        out_specs=in_vmem(),
        scratch_shapes=[
            pltpu.VMEM((width, width), jnp.float32),
            pltpu.VMEM((BLOCK, BLOCK), jnp.float32),
        ],
        compiler_params=pltpu.CompilerParams(vmem_limit_bytes=32 << 20),
        name="inverse_factor",
    )(total)


def swap_kernel(own_ref, out_ref, send, recv):
    z, x = lax.axis_index(Z), lax.axis_index(X)
    core, y = lax.axis_index(CORE), lax.axis_index(Y)
    other = (z, x, 1 - core, y)
    barrier = pltpu.get_barrier_semaphore()
    pl.semaphore_signal(barrier, inc=1, device_id=other, device_id_type=MESH_IDS)
    pl.semaphore_wait(barrier, 1)
    copy = pltpu.make_async_remote_copy(
        src_ref=own_ref, dst_ref=out_ref, send_sem=send, recv_sem=recv,
        device_id=other, device_id_type=MESH_IDS,
    )
    copy.start()
    copy.wait()


def from_partner(own):
    return pl.pallas_call(
        swap_kernel,
        out_shape=jax.ShapeDtypeStruct(own.shape, own.dtype),
        in_specs=[in_vmem()],
        out_specs=in_vmem(),
        scratch_shapes=[pltpu.SemaphoreType.DMA, pltpu.SemaphoreType.DMA],
        compiler_params=pltpu.CompilerParams(
            collective_id=2, has_side_effects=True, vmem_limit_bytes=16 << 20
        ),
        name="from_partner",
    )(own)


def whiten_kernel(length, lengths_ref, emb_ref, own_ref, other_ref, out_ref, gap_ref):
    views, tokens, width = emb_ref.shape
    core = lax.axis_index(CORE)
    alive = alive_column(lengths_ref, tokens, length)
    for ref, v in ((own_ref, core), (other_ref, 1 - core)):
        centered = (emb_ref[v] - ref[width : width + 1, :]) * alive
        out_ref[v] = dot_of(centered, ref[:width, :], ((1,), (1,)))
    gap = out_ref[0] - out_ref[1]
    ones = jnp.ones((GROUP, width), jnp.float32)
    sums = dot_of(ones, gap * gap, ((1,), (1,))) / width
    for k in range(tokens // BLOCK):
        gap_ref[k : k + 1, :] = sums[0:1, k * BLOCK : (k + 1) * BLOCK]


def whitened_rows(lengths, embedded, own, other, length):
    views, tokens, width = embedded.shape
    whitened, gap = pl.pallas_call(
        lambda *refs: whiten_kernel(length, *refs),
        out_shape=(
            jax.ShapeDtypeStruct(embedded.shape, jnp.float32),
            jax.ShapeDtypeStruct((tokens // BLOCK, BLOCK), jnp.float32),
        ),
        in_specs=[in_smem()] + [in_vmem()] * 3,
        out_specs=(in_vmem(), in_vmem()),
        compiler_params=pltpu.CompilerParams(vmem_limit_bytes=32 << 20),
        name="whitened_rows",
    )(lengths, embedded, own, other)
    return whitened, gap.reshape(tokens)


class Sender:
    def __init__(self, send_sems, recv_sems):
        self.send_sems, self.recv_sems = send_sems, recv_sems
        self.started, self.used = [], 0

    def site(self):
        self.used += 1
        return self.used - 1

    def copy(self, site, src, dst, device):
        return pltpu.make_async_remote_copy(
            src_ref=src, dst_ref=dst,
            send_sem=self.send_sems.at[site], recv_sem=self.recv_sems.at[site],
            device_id=device, device_id_type=MESH_IDS,
        )

    def send(self, site, src, dst, device):
        made = self.copy(site, src, dst, device)
        made.start()
        self.started.append(made)

    def arrived(self, site, dst, device):
        self.copy(site, dst, dst, device).wait_recv()

    def finish(self):
        for made in self.started:
            made.wait_send()


class Ring:
    def __init__(self, sender, size, pos, device_at, slot_at, hops, own=None):
        self.sender, self.size, self.pos = sender, size, pos
        self.device_at, self.slot_at = device_at, slot_at
        self.hops = {1: hops[0], -1: hops[1]}
        self.own = own
        self.sites = {
            (sign, h): sender.site() for sign in (1, -1) for h in range(1, self.hops[sign] + 1)
        }

    def at(self, offset):
        return lax.rem(self.pos + offset + 2 * self.size, self.size)

    def pass_on(self, sign, h):
        source = self.at(-sign * (h - 1))
        slot = self.slot_at(source)
        src = self.own if h == 1 and self.own is not None else slot
        self.sender.send(self.sites[sign, h], src, slot, self.device_at(self.at(sign)))

    def launch(self):
        for sign in (1, -1):
            self.pass_on(sign, 1)

    def has(self, sign, h):
        return h <= self.hops[sign]

    def take(self, sign, h):
        slot = self.slot_at(self.at(-sign * h))
        self.sender.arrived(self.sites[sign, h], slot, self.device_at(self.at(-sign)))
        if h < self.hops[sign]:
            self.pass_on(sign, h + 1)
        return (sign * h) % self.size


class Place:
    def __init__(self, sizes):
        self.depth, self.across, self.down = sizes
        self.z, self.x = lax.axis_index(Z), lax.axis_index(X)
        self.core, self.y = lax.axis_index(CORE), lax.axis_index(Y)
        self.partner = (self.z, self.x, 1 - self.core, self.y)

    def z_at(self, s):
        return lax.rem(self.z - s + 2 * self.depth, self.depth)

    def x_at(self, t):
        return lax.rem(self.x - t + 2 * self.across, self.across)

    def y_at(self, s):
        return lax.rem(self.y + s + 2 * self.down, self.down)

    def along_z(self, zz):
        return (zz, self.x, self.core, self.y)

    def along_x(self, xx):
        return (self.z, xx, self.core, self.y)

    def along_y(self, yy):
        return (self.z, self.x, self.core, yy)

    def greet(self):
        peers = [self.along_z(self.z_at(s)) for s in (1, -1)]
        peers += [self.along_x(self.x_at(s)) for s in (1, -1)]
        peers += [self.along_y(self.y_at(s)) for s in range(1, self.down)]
        peers += [self.partner]
        barrier = pltpu.get_barrier_semaphore()
        for peer in peers:
            pl.semaphore_signal(barrier, inc=1, device_id=peer, device_id_type=MESH_IDS)
        pl.semaphore_wait(barrier, len(peers))


SITES = 64


def rows_of_slab(zz, xx, core, across):
    return pl.ds(pl.multiple_of(((zz * across + xx) * 2 + core) * GROUP, GROUP), GROUP)


def gather_kernel(
    sizes, xt_ref, raw_a, raw_b, xt_out, wa_out, wb_out, wa_ref, wb_ref,
    ring_send, ring_recv, pair_send, pair_recv, y_send, y_recv, local,
):
    here = Place(sizes)
    depth, across, down = sizes
    z, x, core, y = here.z, here.x, here.core, here.y
    wa_ref[...] = jnp.concatenate([raw_a[k] for k in range(raw_a.shape[0])], axis=1)
    wb_ref[...] = jnp.concatenate([raw_b[k] for k in range(raw_b.shape[0])], axis=1)
    here.greet()
    half = xt_ref.shape[0] // 2

    def slab(zz, xx, cc):
        return wb_out.at[:, rows_of_slab(zz, xx, cc, across), :]

    def own_part(yy):
        return wb_out.at[yy, rows_of_slab(z, x, core, across), :]

    own = [
        pltpu.make_async_copy(wb_ref, own_part(y), local.at[0]),
        pltpu.make_async_copy(wa_ref, wa_out.at[z, x, core], local.at[1]),
        pltpu.make_async_copy(xt_ref, xt_out.at[y], local.at[2]),
    ]
    for copy in own:
        copy.start()

    ys = Sender(y_send, y_recv)
    wb_sites = {s: ys.site() for s in range(1, down)}
    for s in range(1, down):
        ys.send(wb_sites[s], wb_ref, own_part(y), here.along_y(here.y_at(s)))

    def piece(yy, p):
        return xt_out.at[yy, p * half : (p + 1) * half, :]

    xt_sites = {(sign, p, h): ys.site() for sign in (1, -1) for p in (0, 1) for h in (1, 2)}
    for first in (0, 1):
        for sign in (1, -1):
            p = first if sign == 1 else 1 - first
            ys.send(
                xt_sites[sign, p, 1], xt_ref.at[p * half : (p + 1) * half, :], piece(y, p),
                here.along_y(here.y_at(sign)),
            )

    def first_pieces():
        for sign, p in ((1, 0), (-1, 1)):
            source = here.y_at(-sign)
            ys.arrived(xt_sites[sign, p, 1], piece(source, p), here.along_y(source))
            ys.send(xt_sites[sign, p, 2], piece(source, p), piece(source, p), here.along_y(here.y_at(sign)))

    def last_pieces():
        for sign, p in ((1, 1), (-1, 0)):
            source = here.y_at(-sign)
            ys.arrived(xt_sites[sign, p, 1], piece(source, p), here.along_y(source))
        for sign, p in ((1, 0), (-1, 1)):
            ys.arrived(xt_sites[sign, p, 2], piece(here.y_at(2), p), here.along_y(here.y_at(-sign)))

    def slabs_ready():
        for s in range(1, down):
            source = here.y_at(-s)
            ys.arrived(wb_sites[s], own_part(source), here.along_y(source))
        own[0].wait()

    pairs = Sender(pair_send, pair_recv)

    def to_partner(s, t):
        slot = wa_out.at[here.z_at(s), here.x_at(t), core]
        src = wa_ref if s == 0 and t == 0 else slot
        pairs.send(s * across + t, src, slot, here.partner)

    @pl.when(core == 0)
    def _():
        rings = Sender(ring_send, ring_recv)
        down_z = Ring(rings, depth, z, here.along_z, lambda zz: wa_out.at[zz, x, core], (4, 3), wa_ref)
        slabs_z = Ring(rings, depth, z, here.along_z, lambda zz: slab(zz, x, core), (3, 4))
        on_x = [
            Ring(
                rings, across, x, here.along_x,
                lambda xx, s=s: wa_out.at[here.z_at(s), xx, core],
                (2, 1) if s % 2 == 0 else (1, 2),
                wa_ref if s == 0 else None,
            )
            for s in range(depth)
        ]
        down_z.launch()
        on_x[0].launch()
        to_partner(0, 0)
        slabs_ready()
        slabs_z.launch()
        waiting = [0]
        for h in range(1, 5):
            arrived = []
            for sign in (1, -1):
                if down_z.has(sign, h):
                    s = down_z.take(sign, h)
                    on_x[s].launch()
                    to_partner(s, 0)
                    arrived.append(s)
            for sign in (1, -1):
                if slabs_z.has(sign, h):
                    slabs_z.take(sign, h)
            for s in waiting:
                for sign in (1, -1):
                    to_partner(s, on_x[s].take(sign, 1))
            waiting = arrived
            if h == 3:
                first_pieces()
        for s in waiting:
            for sign in (1, -1):
                to_partner(s, on_x[s].take(sign, 1))
        for s in [0, 1, 7, 2, 6, 3, 5, 4]:
            to_partner(s, on_x[s].take(1 if s % 2 == 0 else -1, 2))
        rings.finish()

    @pl.when(core == 1)
    def _():
        rings = Sender(ring_send, ring_recv)
        own_x = Ring(rings, across, x, here.along_x, lambda xx: wa_out.at[z, xx, core], (2, 1), wa_ref)
        slabs_x = Ring(rings, across, x, here.along_x, lambda xx: slab(z, xx, core), (1, 2))
        on_z = [
            Ring(
                rings, depth, z, here.along_z,
                lambda zz, t=t: wa_out.at[zz, here.x_at(t), core],
                (4, 3) if t % 2 == 0 else (3, 4),
                wa_ref if t == 0 else None,
            )
            for t in range(across)
        ]
        own_x.launch()
        on_z[0].launch()
        to_partner(0, 0)
        slabs_ready()
        slabs_x.launch()
        for sign, h in ((1, 1), (-1, 1), (1, 2)):
            t = own_x.take(sign, h)
            on_z[t].launch()
            to_partner(0, t)
        for sign, h in ((1, 1), (-1, 1), (-1, 2)):
            slabs_x.take(sign, h)
        for h in range(1, 5):
            for t in (0, 1, 3, 2):
                for sign in (1, -1):
                    if on_z[t].has(sign, h):
                        to_partner(on_z[t].take(sign, h), t)
            if h == 1:
                first_pieces()
        rings.finish()

    last_pieces()
    for s in range(depth):
        for t in range(across):
            slot = wa_out.at[here.z_at(s), here.x_at(t), 1 - core]
            made = pairs.copy(s * across + t, slot, slot, here.partner)
            made.wait_recv()
            made.wait_send()
    ys_wait = ys.started
    for made in ys_wait[: down - 1 + 4]:
        made.wait_send()
    for sign, p in ((1, 0), (-1, 1)):
        ys.copy(
            xt_sites[sign, p, 2], piece(here.y_at(-sign), p), piece(here.y_at(-sign), p),
            here.along_y(here.y_at(sign)),
        ).wait_send()
    own[1].wait()
    own[2].wait()


def gathered_inputs(xt, wa, wb, sizes):
    depth, across, down = sizes
    dma = pltpu.SemaphoreType.DMA
    anywhere = pl.BlockSpec(memory_space=pl.ANY)
    taps, rows_a, width = wa.shape
    rows_b = wb.shape[1]
    return pl.pallas_call(
        lambda *refs: gather_kernel(sizes, *refs),
        out_shape=(
            jax.ShapeDtypeStruct((down, *xt.shape), xt.dtype),
            jax.ShapeDtypeStruct((depth, across, 2, rows_a, taps * width), wa.dtype),
            jax.ShapeDtypeStruct((down, depth * across * 2 * rows_b, taps * width), wb.dtype),
        ),
        in_specs=[anywhere, in_vmem(), in_vmem()],
        out_specs=(in_vmem(), anywhere, anywhere),
        scratch_shapes=[
            pltpu.VMEM((rows_a, taps * width), wa.dtype),
            pltpu.VMEM((rows_b, taps * width), wb.dtype),
            dma((SITES,)), dma((SITES,)),
            dma((depth * across,)), dma((depth * across,)),
            dma((16,)), dma((16,)),
            dma((3,)),
        ],
        compiler_params=pltpu.CompilerParams(
            collective_id=3, has_side_effects=True, vmem_limit_bytes=16 << 20
        ),
        name="gathered_inputs",
    )(xt, wa, wb)


def gate(values):
    return 0.5 * values * (1.0 + jnp.tanh(0.7978845608 * (values + 0.044715 * values * values * values)))


PAD = 8
ROWS = 128
EDGE = 16


def conv_kernel(
    sizes, lengths_ref, xt_ref, wa_hbm, gain_ref, keep_ref, out_ref, wa_ref, n_ref, w_ref, stage, p_ref, cols, sems
):
    sequences, length, taps = sizes
    channels, tokens = xt_ref.shape
    chunks, chunk_rows, lanes = wa_ref.shape
    loads = 4
    each = chunks // loads
    arriving = [
        pltpu.make_async_copy(wa_hbm.at[pl.ds(i * each, each)], wa_ref.at[pl.ds(i * each, each)], sems.at[i])
        for i in range(loads)
    ]
    for copy in arriving:
        copy.start()
    eye = lax.broadcasted_iota(jnp.int32, (BLOCK, BLOCK), 0) == lax.broadcasted_iota(
        jnp.int32, (BLOCK, BLOCK), 1
    )
    squares = jnp.zeros((1, tokens), jnp.float32)
    for i in range(channels // BLOCK):
        part = xt_ref[i * BLOCK : (i + 1) * BLOCK, :].astype(jnp.float32)
        squares = squares + jnp.sum(part * part, axis=0, keepdims=True)
    scale = lax.rsqrt(squares / channels + EPS_NORM)
    for i in range(channels // BLOCK):
        part = xt_ref[i * BLOCK : (i + 1) * BLOCK, :].astype(jnp.float32)
        gain = jnp.sum(
            jnp.where(eye, jnp.broadcast_to(gain_ref[i : i + 1, :], (BLOCK, BLOCK)), 0.0), axis=1, keepdims=True
        )
        normed = (part * scale * gain).astype(jnp.bfloat16)
        n_ref[:, i * BLOCK : (i + 1) * BLOCK] = normed.T

    token = lax.broadcasted_iota(jnp.int32, (GROUP, tokens), 1)
    position = token % length
    limit = jnp.zeros((GROUP, tokens), jnp.int32)
    for s in range(sequences):
        limit = jnp.where(token // length == s, lengths_ref[s], limit)
    view = lax.broadcasted_iota(jnp.int32, (GROUP, tokens), 0)
    keep = jnp.where(view == 0, keep_ref[0:1, :], jnp.where(view == 1, keep_ref[1:2, :], 0))
    kept = jnp.where(position < limit, keep, 0).astype(jnp.float32)
    for k in range(taps):
        move = k - taps // 2
        rolled = kept if move == 0 else pltpu.roll(kept, (-move) % tokens, 1)
        inside = (position + move >= 0) & (position + move < length)
        cols[k] = jnp.where(inside, rolled, 0.0).T

    group = 4

    def relay(q, _):
        for i in range(group):
            stage[i * chunk_rows : (i + 1) * chunk_rows, :] = wa_ref[q * group + i].astype(jnp.float32)
        at = pl.multiple_of(q * group * chunk_rows, group * chunk_rows)
        w_ref[pl.ds(at, group * chunk_rows), :] = stage[...].astype(jnp.bfloat16)
        return 0

    for i in range(loads):
        arriving[i].wait()
        lax.fori_loop(i * each // group, (i + 1) * each // group, relay, 0)

    width = lanes // taps
    p_ref[0:PAD, :] = jnp.zeros((PAD, lanes), jnp.float32)
    p_ref[PAD + length :, :] = jnp.zeros((PAD, lanes), jnp.float32)

    def sequence(s, _):
        start = pl.multiple_of(s * length, length)
        for r in range(length // ROWS):
            p_ref[PAD + r * ROWS : PAD + (r + 1) * ROWS, :] = jnp.dot(
                n_ref[pl.ds(start + r * ROWS, ROWS), :], w_ref[...], preferred_element_type=jnp.float32
            )
        for r in range(length // ROWS):
            hidden = []
            for v in range(2):
                acc = None
                for k in range(taps):
                    first = PAD + r * ROWS + k - taps // 2
                    piece = p_ref[first : first + ROWS, k * width : (k + 1) * width]
                    piece = piece * cols[k, pl.ds(start + r * ROWS, ROWS), v : v + 1]
                    acc = piece if acc is None else acc + piece
                hidden.append(gate(acc))
            out_ref[pl.ds(start + r * ROWS, ROWS), :] = jnp.concatenate(hidden, axis=1).astype(jnp.bfloat16)
        return 0

    lax.fori_loop(0, sequences, sequence, 0)


def first_conv(lengths, xt, wa, gain, keep, taps):
    channels, tokens = xt.shape
    chunks, chunk_rows, lanes = wa.shape
    sequences = lengths.shape[0]
    length = tokens // sequences
    bf, f32 = jnp.bfloat16, jnp.float32
    return pl.pallas_call(
        lambda *refs: conv_kernel((sequences, length, taps), *refs),
        out_shape=jax.ShapeDtypeStruct((tokens, 2 * lanes // taps), bf),
        in_specs=[in_smem(), in_vmem(), pl.BlockSpec(memory_space=pl.ANY), in_vmem(), in_vmem()],
        out_specs=in_vmem(),
        scratch_shapes=[
            pltpu.VMEM(wa.shape, bf),
            pltpu.VMEM((tokens, channels), bf),
            pltpu.VMEM((channels, lanes), bf),
            pltpu.VMEM((4 * chunk_rows, lanes), f32),
            pltpu.VMEM((length + 2 * PAD, lanes), f32),
            pltpu.VMEM((taps, tokens, GROUP), f32),
            pltpu.SemaphoreType.DMA((4,)),
        ],
        compiler_params=pltpu.CompilerParams(vmem_limit_bytes=40 << 20),
        name="first_conv",
    )(lengths, xt, wa, gain, keep)


def spread_kernel(
    sizes, h_ref, wb_in, hx_out, wb_out, ring_send, ring_recv, pair_send, pair_recv, y_send, y_recv, local
):
    here = Place(sizes)
    depth, across, down = sizes
    z, x, core, y = here.z, here.x, here.core, here.y
    here.greet()
    rows = h_ref.shape[0] // down
    window = rows + EDGE

    def source_rows(yy):
        return pl.ds(pl.multiple_of(yy * rows - EDGE * lax.rem(yy, 2), EDGE), window)

    def target_rows(yy):
        return pl.ds(pl.multiple_of(EDGE - EDGE * lax.rem(yy, 2), EDGE), window)

    ys = Sender(y_send, y_recv)
    for s in (2, 1, 3):
        other = here.y_at(s)
        ys.send(s, h_ref.at[source_rows(other), :], hx_out.at[y, target_rows(other), :], here.along_y(other))
    own = pltpu.make_async_copy(h_ref.at[source_rows(y), :], hx_out.at[y, target_rows(y), :], local.at[0])
    own.start()

    def slab(zz, xx, cc):
        return wb_out.at[:, rows_of_slab(zz, xx, cc, across), :]

    pairs = Sender(pair_send, pair_recv)

    def to_partner(s, t):
        slot = slab(here.z_at(s), here.x_at(t), core)
        pairs.send(s * across + t, slot, slot, here.partner)

    @pl.when(core == 0)
    def _():
        rings = Sender(ring_send, ring_recv)
        on_x = [
            Ring(
                rings, across, x, here.along_x,
                lambda xx, s=s: slab(here.z_at(s), xx, core),
                (2, 1) if s % 2 == 0 else (1, 2),
            )
            for s in range(depth)
        ]
        for s in range(depth):
            on_x[s].launch()
        for s in range(depth):
            to_partner(s, 0)
        for s in range(depth):
            for sign in (1, -1):
                to_partner(s, on_x[s].take(sign, 1))
        for s in range(depth):
            to_partner(s, on_x[s].take(1 if s % 2 == 0 else -1, 2))
        rings.finish()

    @pl.when(core == 1)
    def _():
        rings = Sender(ring_send, ring_recv)
        on_z = [
            Ring(
                rings, depth, z, here.along_z,
                lambda zz, t=t: slab(zz, here.x_at(t), core),
                (4, 3) if t % 2 == 0 else (3, 4),
            )
            for t in range(across)
        ]
        for t in range(across):
            on_z[t].launch()
        for t in range(across):
            to_partner(0, t)
        for h in range(1, 5):
            for t in range(across):
                for sign in (1, -1):
                    if on_z[t].has(sign, h):
                        to_partner(on_z[t].take(sign, h), t)
        rings.finish()

    for s in range(depth):
        for t in range(across):
            slot = slab(here.z_at(s), here.x_at(t), 1 - core)
            made = pairs.copy(s * across + t, slot, slot, here.partner)
            made.wait_recv()
            made.wait_send()
    for s in (2, 1, 3):
        source = here.y_at(-s)
        ys.arrived(s, hx_out.at[source, target_rows(y), :], here.along_y(source))
    ys.finish()
    own.wait()


def spread_hidden(hidden, wb, sizes):
    depth, across, down = sizes
    tokens, lanes = hidden.shape
    dma = pltpu.SemaphoreType.DMA
    anywhere = pl.BlockSpec(memory_space=pl.ANY)
    return pl.pallas_call(
        lambda *refs: spread_kernel(sizes, *refs),
        out_shape=(
            jax.ShapeDtypeStruct((down, tokens // down + 2 * EDGE, lanes), hidden.dtype),
            jax.ShapeDtypeStruct(wb.shape, wb.dtype),
        ),
        in_specs=[in_vmem(), anywhere],
        out_specs=(in_vmem(), anywhere),
        input_output_aliases={1: 1},
        scratch_shapes=[
            dma((SITES,)), dma((SITES,)),
            dma((depth * across,)), dma((depth * across,)),
            dma((4,)), dma((4,)),
            dma((1,)),
        ],
        compiler_params=pltpu.CompilerParams(
            collective_id=4, has_side_effects=True, vmem_limit_bytes=16 << 20
        ),
        name="spread_hidden",
    )(hidden, wb)


def embed_kernel(taps, length, lengths_ref, hx_ref, wb_hbm, emb_ref, out_ref, wb_ref, wide, cols, sems):
    down, rows, lanes = hx_ref.shape
    arriving = [pltpu.make_async_copy(wb_hbm.at[c], wb_ref.at[c], sems.at[c]) for c in range(down)]
    for copy in arriving:
        copy.start()
    views, tokens, width = emb_ref.shape
    odd = lax.rem(lax.axis_index(Y), 2)
    row = lax.broadcasted_iota(jnp.int32, (rows, lanes), 0)
    inside = (row >= EDGE * (1 - odd)) & (row < rows - EDGE * odd)
    per = lanes // views
    for c in range(down):
        wide[...] = jnp.where(inside, hx_ref[c].astype(jnp.float32), 0.0)
        arriving[c].wait()
        for v in range(views):
            pieces = []
            for k in range(taps):
                first = EDGE + 2 * (k - taps // 2)
                pieces.append(wide[first : first + tokens, v * per : (v + 1) * per])
            cols[...] = jnp.concatenate(pieces, axis=1).astype(jnp.bfloat16)
            part = lax.dot_general(
                cols[...], wb_ref[c], (((1,), (1,)), ((), ())), preferred_element_type=jnp.float32
            )
            if c == 0:
                emb_ref[v] = part
            else:
                emb_ref[v] += part
    moments_into(emb_ref, alive_column(lengths_ref, tokens, length), out_ref)


def embedding(lengths, hx, wb, planes, taps, length):
    down, rows, lanes = hx.shape
    width = wb.shape[1]
    tokens = rows - 2 * EDGE
    parts = share_rows(width, planes) * planes
    return pl.pallas_call(
        lambda *refs: embed_kernel(taps, length, *refs),
        out_shape=(
            jax.ShapeDtypeStruct((2, tokens, width), jnp.float32),
            jax.ShapeDtypeStruct((2, parts, BLOCK), jnp.float32),
        ),
        in_specs=[in_smem(), in_vmem(), pl.BlockSpec(memory_space=pl.ANY)],
        out_specs=(in_vmem(), in_vmem()),
        scratch_shapes=[
            pltpu.VMEM(wb.shape, wb.dtype),
            pltpu.VMEM((rows, lanes), jnp.float32),
            pltpu.VMEM((tokens, wb.shape[2]), jnp.bfloat16),
            pltpu.SemaphoreType.DMA((down,)),
        ],
        compiler_params=pltpu.CompilerParams(vmem_limit_bytes=40 << 20),
        name="embedding",
    )(lengths, hx, wb)


def shards(monomers, keep_mask, lengths, norm_gain, weight_a, weight_b):
    tokens = monomers.shape[0]
    length = tokens // lengths.shape[0]
    taps = weight_a.shape[0]
    sizes = (lax.axis_size(Z), lax.axis_size(X), lax.axis_size(Y))
    xt, wa, wb = gathered_inputs(monomers.T, weight_a, weight_b.transpose(0, 2, 1), sizes)
    hidden = first_conv(
        lengths,
        xt.reshape(-1, tokens),
        wa.reshape(-1, *wa.shape[3:]),
        norm_gain.reshape(-1, BLOCK),
        keep_mask,
        taps,
    )
    hx, wb = spread_hidden(hidden, wb, sizes)
    embedded, parts = embedding(lengths, hx, wb, sizes[1] * sizes[2], taps, length)
    total = total_moments(parts, sizes)
    inverse = inverse_factor(total, embedded.shape[2])
    other = from_partner(inverse)
    return whitened_rows(lengths, embedded, inverse, other, length)


def solution(mesh):
    torus = Mesh(
        mesh.devices.reshape(8, 4, 2, mesh.shape["chan"]), ("batch_0", "batch_1", "batch_2", "chan")
    )
    in_specs = (
        P(BATCH, "chan"),
        P(None, BATCH),
        P(BATCH),
        P(),
        P(None, BATCH, "chan"),
        P(None, "chan", BATCH),
    )
    out_specs = (P(None, BATCH_CHAN, None), P(BATCH_CHAN))
    return jax.shard_map(
        shards, mesh=torus, in_specs=in_specs, out_specs=out_specs, check_vma=False
    )
```

time: 208 us -> 156 us (0.75)
  Pallas kernels: 201 us -> 150 us
    pallas_call x6, Pallas kernels: 170 us -> 120 us  [the longest x1 40.1 us: gathered_inputs(): pl.pallas_call(lambda *refs: gather_kernel(sizes, *refs), out_shape=(jax....]
    unnamed x3 -> x14, local copies, waits for them, and re-layouts: 2.19 us -> 4.77 us
where the time goes in v3:
time: 156 us; the launch traced here: 155 us
  Pallas kernels  150 us (96%)
  local copies, waits for them, and re-layouts  4.77 us (3%)
    pallas_call x1, Pallas kernels, gathered_inputs(): pl.pallas_call(lambda *refs: gather_kernel(sizes, *refs), out_shape=(jax....  40.1 us
    pallas_call x1, Pallas kernels, total_moments(): pl.pallas_call(lambda *refs: total_kernel(mesh_sizes, pieces, *refs), out...  29.8 us
    pallas_call x1, Pallas kernels, inverse_factor(): pl.pallas_call(factor_kernel, out_shape=jax.ShapeDtypeStruct((width + GRO...  25.7 us
    pallas_call x1, Pallas kernels, spread_hidden(): pl.pallas_call(lambda *refs: spread_kernel(sizes, *refs), out_shape=(jax....  24.1 us
    pallas_call x1, Pallas kernels, first_conv(): pl.pallas_call(lambda *refs: conv_kernel((sequences, length, taps), *refs...  12.1 us
    pallas_call x1, Pallas kernels, embedding(): pl.pallas_call(lambda *refs: embed_kernel(taps, length, *refs), out_shape...  9.17 us
    unnamed x14, local copies, waits for them, and re-layouts  4.77 us
    pallas_call x1, Pallas kernels, from_partner(): pl.pallas_call(swap_kernel, out_shape=jax.ShapeDtypeStruct(own.shape, own...  4.65 us

profile of v3, /device:TPU:1, one launch (start us, length us, event | category | flops | bytes accessed | tf_op | source)
XLA Modules:
  0.0 155.4 jit_solution(9408957151594593698)
XLA Ops:
  0.6 0.0 copy-start
  0.6 1.1 copy-done
  1.7 0.0 copy-start.1
  1.7 0.9 copy-done.1
  2.6 0.0 copy-start.2
  2.6 0.8 copy-done.2
  3.4 40.1 %gathered_inputs.1 = (bf16[4,320,1024]{2,1,0:T(8,128)(2,1)S(1)}, bf16[8,4,2,20,1600]{4,3,2,1,0:T(8,128)(2,1)S(1)}, bf16[4,512,1600]{2,1,0:T(8,128)(2,1)S(1)}) custom-call(bf16[320,1024]{1,0:T(8,128)(2,1)S(1)} %bitcast.8, bf16[5,20,320]{2,1,0:T(8,128)(2,1)S(1)} %copy-done.1, bf16[5,8,320]{2,1,0:T(8,128)(2,1)S(1)} %bitcast.9), custom_call_target="tpu_custom_call" | custom-call | tf_op jit(solution)/shard_map/gathered_inputs/pallas_call | solution.py:667
  43.5 0.0 copy-start.3
  43.5 0.7 copy-done.3
  44.2 0.0 copy-start.4
  44.2 0.7 copy-done.4
  44.9 0.0 copy-start.5
  44.9 0.7 copy-done.5
  45.5 12.1 %first_conv.1.refs_0_ = bf16[1024,640]{1,0:T(8,128)(2,1)S(1)} custom-call(s32[2]{0:T(128)S(1)} %copy-done.5, bf16[1280,1024]{1,0:T(8,128)(2,1)S(1)} %bitcast.7, bf16[64,20,1600]{2,1,0:T(8,128)(2,1)S(1)} %bitcast.6, f32[10,128]{1,0:T(8,128)S(1)} %bitcast.10, s32[2,1024]{1,0:T(2,128)S(1)} %copy-done.4), custom_call_target="tpu_custom_call" | custom-call | tf_op jit(solution)/shard_map/first_conv/pallas_call | solution.py:789
  57.6 0.0 copy-start.6
  57.6 24.1 %spread_hidden.1 = (bf16[4,288,640]{2,1,0:T(8,128)(2,1)S(1)}, bf16[4,512,1600]{2,1,0:T(8,128)(2,1)S(1)}) custom-call(bf16[1024,640]{1,0:T(8,128)(2,1)S(1)} %first_conv.1.refs_0_, bf16[4,512,1600]{2,1,0:T(8,128)(2,1)S(1)} %get-tuple-element.13.refs_1_), custom_call_target="tpu_custom_call", output_to_operand_aliasing={{1}: (1, {})} | custom-call | tf_op jit(solution)/shard_map/spread_hidden/pallas_call | solution.py:902
  81.8 0.0 copy-done.6
  81.8 9.2 %embedding.1 = (f32[2,256,512]{2,1,0:T(8,128)S(1)}, f32[2,1408,128]{2,1,0:T(8,128)S(1)}) custom-call(s32[2]{0:T(128)S(1)} %copy-done.6, bf16[4,288,640]{2,1,0:T(8,128)(2,1)S(1)} %get-tuple-element.14.refs_1_, bf16[4,512,1600]{2,1,0:T(8,128)(2,1)S(1)} %get-tuple-element.15.refs_2_), custom_call_target="tpu_custom_call" | custom-call | tf_op jit(solution)/shard_map/embedding/pallas_call | solution.py:958
  90.9 29.8 %total_moments.1.total_ref = f32[1408,128]{1,0:T(8,128)S(1)} custom-call(f32[2,1408,128]{2,1,0:T(8,128)S(1)} %get-tuple-element.17.refs_0_), custom_call_target="tpu_custom_call" | custom-call | tf_op jit(solution)/shard_map/total_moments/pallas_call | solution.py:181
  120.8 25.7 %inverse_factor.1.own_ref.refs_2_ = f32[520,512]{1,0:T(8,128)S(1)} custom-call(f32[1408,128]{1,0:T(8,128)S(1)} %total_moments.1.total_ref), custom_call_target="tpu_custom_call" | custom-call | tf_op jit(solution)/shard_map/inverse_factor/pallas_call | solution.py:316
  146.4 4.7 %from_partner.1.refs_3_ = f32[520,512]{1,0:T(8,128)S(1)} custom-call(f32[520,512]{1,0:T(8,128)S(1)} %inverse_factor.1.own_ref.refs_2_), custom_call_target="tpu_custom_call" | custom-call | tf_op jit(solution)/shard_map/from_partner/pallas_call | solution.py:346
  151.1 4.3 %whitened_rows.1 = (f32[2,256,512]{2,1,0:T(8,128)}, f32[2,128]{1,0:T(2,128)}) custom-call(s32[2]{0:T(128)S(1)} %copy-done.6, f32[2,256,512]{2,1,0:T(8,128)S(1)} %get-tuple-element.16.refs_1_, f32[520,512]{1,0:T(8,128)S(1)} %inverse_factor.1.own_ref.refs_2_, f32[520,512]{1,0:T(8,128)S(1)} %from_partner.1.refs_3_), custom_call_target="tpu_custom_call" | custom-call | tf_op jit(solution)/shard_map/whitened_rows/pallas_call | solution.py:375
Async XLA Ops:
  0.6 1.1 copy-start
  1.7 0.9 copy-start.1
  2.6 0.8 copy-start.2
  43.5 0.7 copy-start.3
  44.2 0.7 copy-start.4
  44.9 0.7 copy-start.5
  57.6 24.2 %copy-start.6 = (s32[2]{0:T(128)S(1)}, s32[2]{0:T(128)}, u32[]{:S(2)}) copy-start(s32[2]{0:T(128)} %refs_0_.5) | copy-start | bytes 28

commit v4 on v3

--- a/solution.py
+++ b/solution.py
@@ -35,7 +35,7 @@
 
 
 def share_rows(width, planes):
-    rows = len(block_pairs(width)) * BLOCK + GROUP
+    rows = len(block_pairs(width)) * BLOCK
     return -(-rows // (planes * GROUP)) * GROUP
 
 
@@ -53,6 +53,7 @@
     views, tokens, width = emb_ref.shape
     pairs = block_pairs(width)
     at = len(pairs) * BLOCK
+    half = BLOCK // 2
     for v in range(views):
         masked = emb_ref[v] * alive
         for i in range(width // BLOCK):
@@ -63,13 +64,12 @@
             for k in range(i + 1):
                 b = pairs.index((i, k))
                 out_ref[v, b * BLOCK : (b + 1) * BLOCK, :] = strip[:, k * BLOCK : (k + 1) * BLOCK]
-        out_ref[v, at:, :] = jnp.zeros((out_ref.shape[1] - at, BLOCK), jnp.float32)
+        if out_ref.shape[1] > at:
+            out_ref[v, at:, :] = jnp.zeros((out_ref.shape[1] - at, BLOCK), jnp.float32)
         sums = jnp.sum(masked, axis=0, keepdims=True)
-        for k in range(width // BLOCK):
-            out_ref[v, at + k : at + k + 1, :] = sums[:, k * BLOCK : (k + 1) * BLOCK]
-        count = jnp.sum(alive, axis=0, keepdims=True)
-        last = at + width // BLOCK
-        out_ref[v, last : last + 1, :] = jnp.broadcast_to(count, (1, BLOCK))
+        spare = [sums[:, k * half : (k + 1) * half] for k in range(width // half)]
+        spare.append(jnp.broadcast_to(jnp.sum(alive, axis=0, keepdims=True), (1, half)))
+        out_ref[v, 0 : len(spare), half:] = jnp.concatenate(spare, axis=0)
 
 
 def total_kernel(sizes, parts, part_ref, out_ref, pair_in, mine, plane_in, share, line_in, total, *sems):
@@ -106,16 +106,18 @@
         copy.start()
         return copy
 
-    sent(part_ref.at[partner], pair_in, pair_send, pair_recv, (z, x, partner, y)).wait()
-    mine[...] = part_ref[core] + pair_in[...]
-
     starts = [sum(parts[:i]) for i in range(len(parts))]
-
-    def rows_of(index, i):
-        return pl.ds(pl.multiple_of(index * rows + starts[i], GROUP), parts[i])
 
     def within(i):
         return pl.ds(starts[i], parts[i])
+
+    swaps = [
+        sent(
+            part_ref.at[partner, :, within(i)], pair_in.at[:, within(i)],
+            pair_send.at[i], pair_recv.at[i], (z, x, partner, y),
+        )
+        for i in range(len(parts))
+    ]
 
     def summed(buffer, own, count, i):
         acc = None
@@ -126,17 +128,19 @@
 
     spread, lines, back = {}, {}, {}
     for i in range(len(parts)):
+        swaps[i].wait_recv()
+        mine[:, within(i)] = part_ref[core, :, within(i)] + pair_in[:, within(i)]
         for step in range(1, planes):
             other, device = in_plane(step)
             spread[i, step] = sent(
-                mine.at[rows_of(other, i)], plane_in.at[step, within(i)],
+                mine.at[other, within(i)], plane_in.at[step, within(i)],
                 plane_send.at[i, step], plane_recv.at[i, step], device,
             )
 
     def to_line(i):
         for step in range(1, planes):
             spread[i, step].wait_recv()
-        plane_in[0, within(i)] = mine[rows_of(me, i)]
+        plane_in[0, within(i)] = mine[me, within(i)]
         share[within(i)] = summed(plane_in, me, planes, i)
         for step in range(1, depth):
             lines[i, step] = sent(
@@ -151,10 +155,10 @@
         total[within(i)] = summed(line_in, z, depth, i)
         for step in range(1, planes):
             back[i, step] = sent(
-                total.at[within(i)], out_ref.at[rows_of(me, i)],
+                total.at[within(i)], out_ref.at[me, within(i)],
                 back_send.at[i, step], back_recv.at[i, step], in_plane(step)[1],
             )
-        out_ref[rows_of(me, i)] = total[within(i)]
+        out_ref[me, within(i)] = total[within(i)]
 
     lag = 2
     for i in range(len(parts) + lag):
@@ -164,6 +168,8 @@
             to_plane(i - lag)
     for copy in back.values():
         copy.wait_recv()
+    for copy in swaps:
+        copy.wait_send()
     for group in (spread, lines, back):
         for copy in group.values():
             copy.wait_send()
@@ -180,17 +186,17 @@
     vm = lambda *shape: pltpu.VMEM(shape, jnp.float32)
     return pl.pallas_call(
         lambda *refs: total_kernel(mesh_sizes, pieces, *refs),
-        out_shape=jax.ShapeDtypeStruct((all_rows, lanes), jnp.float32),
+        out_shape=jax.ShapeDtypeStruct((planes, rows, lanes), jnp.float32),
         in_specs=[in_vmem()],
         out_specs=in_vmem(),
         scratch_shapes=[
-            vm(all_rows, lanes),
-            vm(all_rows, lanes),
+            vm(planes, rows, lanes),
+            vm(planes, rows, lanes),
             vm(planes, rows, lanes),
             vm(rows, lanes),
             vm(depth, rows, lanes),
             vm(rows, lanes),
-            dma, dma,
+            dma((4,)), dma((4,)),
             dma((4, planes)), dma((4, planes)),
             dma((4, depth)), dma((4, depth)),
             dma((4, planes)), dma((4, planes)),
@@ -199,7 +205,7 @@
             collective_id=1, has_side_effects=True, vmem_limit_bytes=32 << 20
         ),
         name="total_moments",
-    )(parts)
+    )(parts.reshape(2, planes, rows, lanes)).reshape(all_rows, lanes)
 
 
 def splat_row(v, a):
@@ -216,70 +222,87 @@
     lane = lax.broadcasted_iota(jnp.int32, (GROUP, BLOCK), 1)
     sub = lax.broadcasted_iota(jnp.int32, (GROUP, BLOCK), 0)
     steps = range(GROUP)
+    twos = range(GROUP // 2)
     for p in range(count):
         j = GROUP * p
         v = groups[p]
         cols = [splat_lane(v, j + a) for a in steps]
         e = [[splat_row(cols[a], b) if b >= a else None for a in steps] for b in steps]
-        low = [[None] * GROUP for _ in steps]
-        rec = []
-        for a in steps:
-            rec.append(1.0 / e[a][a])
-            for b in range(a + 1, GROUP):
-                low[b][a] = e[b][a] * rec[a]
-            for b in range(a + 1, GROUP):
-                for c in range(a + 1, b + 1):
-                    e[b][c] = e[b][c] - low[b][a] * e[c][a]
         panel = (lane >= j) & (lane < j + GROUP)
-        rows = []
-        for a in steps:
-            r = jnp.where(panel, jnp.where(lane == j + a, 1.0, 0.0), splat_row(v, a))
-            for b in range(a):
-                r = r - low[a][b] * rows[b]
-            rows.append(r)
+        rows = [
+            jnp.where(panel, jnp.where(lane == j + a, 1.0, 0.0), splat_row(v, a)) for a in steps
+        ]
+        f, inv = {}, []
+        for t in twos:
+            m, n = 2 * t, 2 * t + 1
+            e00, e10, e11 = e[m][m], e[n][m], e[n][n]
+            det = e00 * e11 - e10 * e10
+            rd = 1.0 / det
+            inv.append(rd)
+            for b in range(n + 1, GROUP):
+                f0 = (e11 * e[b][m] - e10 * e[b][n]) * rd
+                f1 = (e00 * e[b][n] - e10 * e[b][m]) * rd
+                f[b, t] = (f0, f1)
+                for c in range(n + 1, b + 1):
+                    e[b][c] = e[b][c] - (f0 * e[c][m] + f1 * e[c][n])
+                rows[b] = rows[b] - (f0 * rows[m] + f1 * rows[n])
         out = None
-        for a in steps:
-            r = rows[a] * lax.rsqrt(e[a][a])
-            out = r if out is None else jnp.where(sub == a, r, out)
-        store(p, jnp.where(lane < j + GROUP, out, 0.0))
+        q = [None] * GROUP
+        for t in reversed(twos):
+            m, n = 2 * t, 2 * t + 1
+            e00, e10, e11, rd = e[m][m], e[n][m], e[n][n], inv[t]
+            q0 = (e11 * rows[m] - e10 * rows[n]) * rd
+            q1 = (e00 * rows[n] - e10 * rows[m]) * rd
+            for b in range(n + 1, GROUP):
+                q0 = q0 - f[b, t][0] * q[b]
+                q1 = q1 - f[b, t][1] * q[b]
+            q[m], q[n] = q0, q1
         for g in range(p + 1, count):
             x = groups[g]
-            w = []
-            acc = jnp.where(panel, 0.0, x)
-            for a in steps:
-                t = splat_lane(x, j + a)
-                for b in range(a):
-                    t = t - low[a][b] * w[b]
-                w.append(t)
-                acc = acc - (t * rec[a]) * rows[a]
-            groups[g] = acc
+            terms = [splat_lane(x, j + a) * q[a] for a in steps]
+            pairs = [terms[2 * t] + terms[2 * t + 1] for t in twos]
+            groups[g] = jnp.where(panel, 0.0, x) - ((pairs[0] + pairs[1]) + (pairs[2] + pairs[3]))
+        for t in twos:
+            m, n = 2 * t, 2 * t + 1
+            e00, e10, e11 = e[m][m], e[n][m], e[n][n]
+            ratio = e10 / e00
+            first = rows[m] * lax.rsqrt(e00)
+            second = (rows[n] - ratio * rows[m]) * lax.rsqrt(e11 - ratio * e10)
+            out = first if out is None else jnp.where(sub == m, first, out)
+            out = jnp.where(sub == n, second, out)
+        store(p, jnp.where(lane < j + GROUP, out, 0.0))
 
 
 def factor_kernel(total_ref, out_ref, work, m_ref):
     width = work.shape[1]
     blocks = width // BLOCK
     pairs = block_pairs(width)
-    at = len(pairs) * BLOCK
-    tail = total_ref[at : at + GROUP, :]
-    count = tail[blocks : blocks + 1, 0:1]
-    center = jnp.concatenate([tail[k : k + 1, :] for k in range(blocks)], axis=1) / count
+    half = BLOCK // 2
+    spare = total_ref[0 : 2 * GROUP, half:]
+    last = width // half
+    count = spare[last : last + 1, 0:1]
+    center = jnp.concatenate([spare[k : k + 1, :] for k in range(last)], axis=1) / count
     first = lax.broadcasted_iota(jnp.int32, (GROUP, width), 0) == 0
     center8 = jnp.where(first, jnp.broadcast_to(center, (GROUP, width)), 0.0)
     eye = lax.broadcasted_iota(jnp.int32, (BLOCK, BLOCK), 0) == lax.broadcasted_iota(
+        jnp.int32, (BLOCK, BLOCK), 1
+    )
+    lower = lax.broadcasted_iota(jnp.int32, (BLOCK, BLOCK), 0) >= lax.broadcasted_iota(
         jnp.int32, (BLOCK, BLOCK), 1
     )
     for b, (i, k) in enumerate(pairs):
         outer = dot_of(
             center8[:, i * BLOCK : (i + 1) * BLOCK], center8[:, k * BLOCK : (k + 1) * BLOCK], ((0,), (0,))
         )
-        block = total_ref[b * BLOCK : (b + 1) * BLOCK, :] / count - outer
+        raw = total_ref[b * BLOCK : (b + 1) * BLOCK, :]
+        if b == 0:
+            raw = jnp.where(lower, raw, raw.T)
+        block = raw / count - outer
         if i == k:
             block = block + jnp.where(eye, EPS_COV, 0.0)
         work[i * BLOCK : (i + 1) * BLOCK, k * BLOCK : (k + 1) * BLOCK] = block
         if i != k:
             work[k * BLOCK : (k + 1) * BLOCK, i * BLOCK : (i + 1) * BLOCK] = block.T
-    row_block = lax.broadcasted_iota(jnp.int32, (width, BLOCK), 0) // BLOCK
-    col_block = lax.broadcasted_iota(jnp.int32, (width, width), 1) // BLOCK
     strip_block = lax.broadcasted_iota(jnp.int32, (BLOCK, width), 1) // BLOCK
     strip_eye = jnp.where(
         lax.broadcasted_iota(jnp.int32, (BLOCK, width), 1) % BLOCK
@@ -299,11 +322,18 @@
 
         base_inverse(load, store)
         m = m_ref[...]
-        col = jnp.where(row_block > k, work[:, pl.ds(here, BLOCK)], 0.0)
-        left = dot_of(col, m, ((1,), (1,)))
         row = jnp.where(strip_block == k, strip_eye, work[pl.ds(here, BLOCK), :])
         across = dot_of(m, row, ((1,), (0,)))
-        work[...] = jnp.where(col_block == k, 0.0, work[...]) - dot_of(left, across, ((1,), (0,)))
+        for done in range(blocks - 1):
+
+            @pl.when(k == done)
+            def _():
+                first = (done + 1) * BLOCK
+                col_block = lax.broadcasted_iota(jnp.int32, (width - first, width), 1) // BLOCK
+                left = dot_of(work[first:, done * BLOCK : first], m, ((1,), (1,)))
+                kept = jnp.where(col_block == done, 0.0, work[first:, :])
+                work[first:, :] = kept - dot_of(left, across, ((1,), (0,)))
+
         work[pl.ds(here, BLOCK), :] = jnp.where(strip_block <= k, across, 0.0)
         return 0
 
@@ -362,7 +392,10 @@
     alive = alive_column(lengths_ref, tokens, length)
     for ref, v in ((own_ref, core), (other_ref, 1 - core)):
         centered = (emb_ref[v] - ref[width : width + 1, :]) * alive
-        out_ref[v] = dot_of(centered, ref[:width, :], ((1,), (1,)))
+        part = 2 * BLOCK
+        for first in range(0, width, part):
+            last = first + part
+            out_ref[v, :, first:last] = dot_of(centered[:, :last], ref[first:last, :last], ((1,), (1,)))
     gap = out_ref[0] - out_ref[1]
     ones = jnp.ones((GROUP, width), jnp.float32)
     sums = dot_of(ones, gap * gap, ((1,), (1,))) / width
@@ -475,6 +508,9 @@
         return (self.z, self.x, self.core, yy)
 
     def greet(self):
+        self.greeted(self.greeting())
+
+    def greeting(self):
         peers = [self.along_z(self.z_at(s)) for s in (1, -1)]
         peers += [self.along_x(self.x_at(s)) for s in (1, -1)]
         peers += [self.along_y(self.y_at(s)) for s in range(1, self.down)]
@@ -482,7 +518,10 @@
         barrier = pltpu.get_barrier_semaphore()
         for peer in peers:
             pl.semaphore_signal(barrier, inc=1, device_id=peer, device_id_type=MESH_IDS)
-        pl.semaphore_wait(barrier, len(peers))
+        return len(peers)
+
+    def greeted(self, count):
+        pl.semaphore_wait(pltpu.get_barrier_semaphore(), count)
 
 
 SITES = 64
@@ -493,15 +532,22 @@
 
 
 def gather_kernel(
-    sizes, xt_ref, raw_a, raw_b, xt_out, wa_out, wb_out, wa_ref, wb_ref,
+    sizes, xt_ref, hbm_a, hbm_b, xt_out, wa_out, wb_out, raw_a, raw_b, wa_ref, wb_ref,
     ring_send, ring_recv, pair_send, pair_recv, y_send, y_recv, local,
 ):
     here = Place(sizes)
     depth, across, down = sizes
     z, x, core, y = here.z, here.x, here.core, here.y
+    greeted = here.greeting()
+    load_a = pltpu.make_async_copy(hbm_a, raw_a, local.at[3])
+    load_b = pltpu.make_async_copy(hbm_b, raw_b, local.at[4])
+    load_a.start()
+    load_b.start()
+    load_a.wait()
+    load_b.wait()
     wa_ref[...] = jnp.concatenate([raw_a[k] for k in range(raw_a.shape[0])], axis=1)
     wb_ref[...] = jnp.concatenate([raw_b[k] for k in range(raw_b.shape[0])], axis=1)
-    here.greet()
+    here.greeted(greeted)
     half = xt_ref.shape[0] // 2
 
     def slab(zz, xx, cc):
@@ -671,15 +717,17 @@
             jax.ShapeDtypeStruct((depth, across, 2, rows_a, taps * width), wa.dtype),
             jax.ShapeDtypeStruct((down, depth * across * 2 * rows_b, taps * width), wb.dtype),
         ),
-        in_specs=[anywhere, in_vmem(), in_vmem()],
+        in_specs=[anywhere] * 3,
         out_specs=(in_vmem(), anywhere, anywhere),
         scratch_shapes=[
+            pltpu.VMEM(wa.shape, wa.dtype),
+            pltpu.VMEM(wb.shape, wb.dtype),
             pltpu.VMEM((rows_a, taps * width), wa.dtype),
             pltpu.VMEM((rows_b, taps * width), wb.dtype),
             dma((SITES,)), dma((SITES,)),
             dma((depth * across,)), dma((depth * across,)),
             dma((16,)), dma((16,)),
-            dma((3,)),
+            dma((5,)),
         ],
         compiler_params=pltpu.CompilerParams(
             collective_id=3, has_side_effects=True, vmem_limit_bytes=16 << 20
@@ -698,7 +746,8 @@
 
 
 def conv_kernel(
-    sizes, lengths_ref, xt_ref, wa_hbm, gain_ref, keep_ref, out_ref, wa_ref, n_ref, w_ref, stage, p_ref, cols, sems
+    sizes, lengths_ref, xt_ref, wa_hbm, gain_hbm, keep_hbm, out_ref,
+    wa_ref, gain_ref, keep_ref, n_ref, w_ref, stage, p_ref, cols, sems,
 ):
     sequences, length, taps = sizes
     channels, tokens = xt_ref.shape
@@ -709,7 +758,11 @@
         pltpu.make_async_copy(wa_hbm.at[pl.ds(i * each, each)], wa_ref.at[pl.ds(i * each, each)], sems.at[i])
         for i in range(loads)
     ]
-    for copy in arriving:
+    small = [
+        pltpu.make_async_copy(gain_hbm, gain_ref, sems.at[loads]),
+        pltpu.make_async_copy(keep_hbm, keep_ref, sems.at[loads + 1]),
+    ]
+    for copy in small + arriving:
         copy.start()
     eye = lax.broadcasted_iota(jnp.int32, (BLOCK, BLOCK), 0) == lax.broadcasted_iota(
         jnp.int32, (BLOCK, BLOCK), 1
@@ -719,6 +772,8 @@
         part = xt_ref[i * BLOCK : (i + 1) * BLOCK, :].astype(jnp.float32)
         squares = squares + jnp.sum(part * part, axis=0, keepdims=True)
     scale = lax.rsqrt(squares / channels + EPS_NORM)
+    for copy in small:
+        copy.wait()
     for i in range(channels // BLOCK):
         part = xt_ref[i * BLOCK : (i + 1) * BLOCK, :].astype(jnp.float32)
         gain = jnp.sum(
@@ -789,16 +844,18 @@
     return pl.pallas_call(
         lambda *refs: conv_kernel((sequences, length, taps), *refs),
         out_shape=jax.ShapeDtypeStruct((tokens, 2 * lanes // taps), bf),
-        in_specs=[in_smem(), in_vmem(), pl.BlockSpec(memory_space=pl.ANY), in_vmem(), in_vmem()],
+        in_specs=[in_smem(), in_vmem()] + [pl.BlockSpec(memory_space=pl.ANY)] * 3,
         out_specs=in_vmem(),
         scratch_shapes=[
             pltpu.VMEM(wa.shape, bf),
+            pltpu.VMEM(gain.shape, f32),
+            pltpu.VMEM(keep.shape, keep.dtype),
             pltpu.VMEM((tokens, channels), bf),
             pltpu.VMEM((channels, lanes), bf),
             pltpu.VMEM((4 * chunk_rows, lanes), f32),
             pltpu.VMEM((length + 2 * PAD, lanes), f32),
             pltpu.VMEM((taps, tokens, GROUP), f32),
-            pltpu.SemaphoreType.DMA((4,)),
+            pltpu.SemaphoreType.DMA((6,)),
         ],
         compiler_params=pltpu.CompilerParams(vmem_limit_bytes=40 << 20),
         name="first_conv",

time: 156 us -> 152 us (0.974)
  Pallas kernels: 150 us -> 146 us
    pallas_call x1, Pallas kernels: 25.7 us -> 23.1 us  [inverse_factor(): pl.pallas_call(factor_kernel, out_shape=jax.ShapeDtypeStruct((width + GRO...]
where the time goes in v4:
time: 152 us; the launch traced here: 151 us
  Pallas kernels  146 us (96%)
  local copies, waits for them, and re-layouts  4.77 us (3%)
    pallas_call x1, Pallas kernels, gathered_inputs(): pl.pallas_call(lambda *refs: gather_kernel(sizes, *refs), out_shape=(jax....  40 us
    pallas_call x1, Pallas kernels, total_moments(): pl.pallas_call(lambda *refs: total_kernel(mesh_sizes, pieces, *refs), out...  29.2 us
    pallas_call x1, Pallas kernels, spread_hidden(): pl.pallas_call(lambda *refs: spread_kernel(sizes, *refs), out_shape=(jax....  24.1 us
    pallas_call x1, Pallas kernels, inverse_factor(): pl.pallas_call(factor_kernel, out_shape=jax.ShapeDtypeStruct((width + GRO...  23.1 us
    pallas_call x1, Pallas kernels, first_conv(): pl.pallas_call(lambda *refs: conv_kernel((sequences, length, taps), *refs...  12.1 us
    pallas_call x1, Pallas kernels, embedding(): pl.pallas_call(lambda *refs: embed_kernel(taps, length, *refs), out_shape...  9.15 us
    unnamed x14, local copies, waits for them, and re-layouts  4.77 us
    pallas_call x1, Pallas kernels, from_partner(): pl.pallas_call(swap_kernel, out_shape=jax.ShapeDtypeStruct(own.shape, own...  4.19 us

profile of v4, /device:TPU:1, one launch (start us, length us, event | category | flops | bytes accessed | tf_op | source)
XLA Modules:
  0.0 151.4 jit_solution(12570723536682576509)
XLA Ops:
  0.6 0.0 copy-start
  0.6 1.1 copy-done
  1.7 0.0 copy-start.1
  1.7 0.9 copy-done.1
  2.6 0.0 copy-start.2
  2.6 0.8 copy-done.2
  3.4 40.0 %gathered_inputs.1 = (bf16[4,320,1024]{2,1,0:T(8,128)(2,1)S(1)}, bf16[8,4,2,20,1600]{4,3,2,1,0:T(8,128)(2,1)S(1)}, bf16[4,512,1600]{2,1,0:T(8,128)(2,1)S(1)}) custom-call(bf16[320,1024]{1,0:T(8,128)(2,1)S(1)} %bitcast.12, bf16[5,20,320]{2,1,0:T(8,128)(2,1)S(1)} %copy-done.1, bf16[5,8,320]{2,1,0:T(8,128)(2,1)S(1)} %bitcast.13), custom_call_target="tpu_custom_call" | custom-call | tf_op jit(solution)/shard_map/gathered_inputs/pallas_call | solution.py:713
  43.3 0.0 copy-start.3
  43.4 0.7 copy-done.3
  44.0 0.0 copy-start.4
  44.0 0.7 copy-done.4
  44.7 0.0 copy-start.5
  44.7 0.7 copy-done.5
  45.4 12.1 %first_conv.1.refs_0_ = bf16[1024,640]{1,0:T(8,128)(2,1)S(1)} custom-call(s32[2]{0:T(128)S(1)} %copy-done.5, bf16[1280,1024]{1,0:T(8,128)(2,1)S(1)} %bitcast.10, bf16[64,20,1600]{2,1,0:T(8,128)(2,1)S(1)} %bitcast.8, f32[10,128]{1,0:T(8,128)S(1)} %bitcast.14, s32[2,1024]{1,0:T(2,128)S(1)} %copy-done.4), custom_call_target="tpu_custom_call" | custom-call | tf_op jit(solution)/shard_map/first_conv/pallas_call | solution.py:844
  57.6 0.0 copy-start.6
  57.6 24.1 %spread_hidden.1 = (bf16[4,288,640]{2,1,0:T(8,128)(2,1)S(1)}, bf16[4,512,1600]{2,1,0:T(8,128)(2,1)S(1)}) custom-call(bf16[1024,640]{1,0:T(8,128)(2,1)S(1)} %first_conv.1.refs_0_, bf16[4,512,1600]{2,1,0:T(8,128)(2,1)S(1)} %get-tuple-element.13.refs_1_), custom_call_target="tpu_custom_call", output_to_operand_aliasing={{1}: (1, {})} | custom-call | tf_op jit(solution)/shard_map/spread_hidden/pallas_call | solution.py:959
  81.7 0.0 copy-done.6
  81.7 9.2 %embedding.1 = (f32[2,256,512]{2,1,0:T(8,128)S(1)}, f32[2,1280,128]{2,1,0:T(8,128)S(1)}) custom-call(s32[2]{0:T(128)S(1)} %copy-done.6, bf16[4,288,640]{2,1,0:T(8,128)(2,1)S(1)} %get-tuple-element.14.refs_1_, bf16[4,512,1600]{2,1,0:T(8,128)(2,1)S(1)} %get-tuple-element.15.refs_2_), custom_call_target="tpu_custom_call" | custom-call | tf_op jit(solution)/shard_map/embedding/pallas_call | solution.py:1015
  90.8 29.2 %total_moments.1 = f32[16,80,128]{2,1,0:T(8,128)S(1)} custom-call(f32[2,16,80,128]{3,2,1,0:T(8,128)S(1)} %bitcast.11), custom_call_target="tpu_custom_call" | custom-call | tf_op jit(solution)/shard_map/total_moments/pallas_call | solution.py:187
  120.1 23.1 %inverse_factor.1.own_ref.refs_2_ = f32[520,512]{1,0:T(8,128)S(1)} custom-call(f32[1280,128]{1,0:T(8,128)S(1)} %bitcast.9), custom_call_target="tpu_custom_call" | custom-call | tf_op jit(solution)/shard_map/inverse_factor/pallas_call | solution.py:346
  143.2 4.2 %from_partner.1.refs_3_ = f32[520,512]{1,0:T(8,128)S(1)} custom-call(f32[520,512]{1,0:T(8,128)S(1)} %inverse_factor.1.own_ref.refs_2_), custom_call_target="tpu_custom_call" | custom-call | tf_op jit(solution)/shard_map/from_partner/pallas_call | solution.py:376
  147.4 4.0 %whitened_rows.1 = (f32[2,256,512]{2,1,0:T(8,128)}, f32[2,128]{1,0:T(2,128)}) custom-call(s32[2]{0:T(128)S(1)} %copy-done.6, f32[2,256,512]{2,1,0:T(8,128)S(1)} %get-tuple-element.16.refs_1_, f32[520,512]{1,0:T(8,128)S(1)} %inverse_factor.1.own_ref.refs_2_, f32[520,512]{1,0:T(8,128)S(1)} %from_partner.1.refs_3_), custom_call_target="tpu_custom_call" | custom-call | tf_op jit(solution)/shard_map/whitened_rows/pallas_call | solution.py:408
Async XLA Ops:
  0.6 1.1 copy-start
  1.7 0.9 copy-start.1
  2.6 0.8 copy-start.2
  43.3 0.7 copy-start.3
  44.0 0.7 copy-start.4
  44.7 0.7 copy-start.5
  57.6 24.1 %copy-start.6 = (s32[2]{0:T(128)S(1)}, s32[2]{0:T(128)}, u32[]{:S(2)}) copy-start(s32[2]{0:T(128)} %refs_0_.5) | copy-start | bytes 28

commit v5 on v4

--- a/solution.py
+++ b/solution.py
@@ -253,7 +253,7 @@
             e00, e10, e11, rd = e[m][m], e[n][m], e[n][n], inv[t]
             q0 = (e11 * rows[m] - e10 * rows[n]) * rd
             q1 = (e00 * rows[n] - e10 * rows[m]) * rd
-            for b in range(n + 1, GROUP):
+            for b in reversed(range(n + 1, GROUP)):
                 q0 = q0 - f[b, t][0] * q[b]
                 q1 = q1 - f[b, t][1] * q[b]
             q[m], q[n] = q0, q1
@@ -261,7 +261,8 @@
             x = groups[g]
             terms = [splat_lane(x, j + a) * q[a] for a in steps]
             pairs = [terms[2 * t] + terms[2 * t + 1] for t in twos]
-            groups[g] = jnp.where(panel, 0.0, x) - ((pairs[0] + pairs[1]) + (pairs[2] + pairs[3]))
+            late = jnp.where(panel, 0.0, x) - ((pairs[3] + pairs[2]) + pairs[1])
+            groups[g] = late - pairs[0]
         for t in twos:
             m, n = 2 * t, 2 * t + 1
             e00, e10, e11 = e[m][m], e[n][m], e[n][n]
@@ -282,8 +283,20 @@
     last = width // half
     count = spare[last : last + 1, 0:1]
     center = jnp.concatenate([spare[k : k + 1, :] for k in range(last)], axis=1) / count
-    first = lax.broadcasted_iota(jnp.int32, (GROUP, width), 0) == 0
-    center8 = jnp.where(first, jnp.broadcast_to(center, (GROUP, width)), 0.0)
+    sub = lax.broadcasted_iota(jnp.int32, (GROUP, width), 0)
+    center8 = jnp.where(sub == 0, jnp.broadcast_to(center, (GROUP, width)), 0.0)
+    high = center.astype(jnp.bfloat16).astype(jnp.float32)
+    middle = (center - high).astype(jnp.bfloat16).astype(jnp.float32)
+    low = center - high - middle
+
+    def stacked(parts):
+        rows = jnp.zeros((GROUP, width), jnp.float32)
+        for i, part in enumerate(parts):
+            rows = jnp.where(sub == i, jnp.broadcast_to(part, (GROUP, width)), rows)
+        return rows.astype(jnp.bfloat16)
+
+    one_side = stacked((high, high, middle, high, low, middle, middle, low))
+    other_side = stacked((high, middle, high, low, high, middle, low, middle))
     eye = lax.broadcasted_iota(jnp.int32, (BLOCK, BLOCK), 0) == lax.broadcasted_iota(
         jnp.int32, (BLOCK, BLOCK), 1
     )
@@ -292,7 +305,10 @@
     )
     for b, (i, k) in enumerate(pairs):
         outer = dot_of(
-            center8[:, i * BLOCK : (i + 1) * BLOCK], center8[:, k * BLOCK : (k + 1) * BLOCK], ((0,), (0,))
+            one_side[:, i * BLOCK : (i + 1) * BLOCK],
+            other_side[:, k * BLOCK : (k + 1) * BLOCK],
+            ((0,), (0,)),
+            lax.Precision.DEFAULT,
         )
         raw = total_ref[b * BLOCK : (b + 1) * BLOCK, :]
         if b == 0:
@@ -525,6 +541,7 @@
 
 
 SITES = 64
+FEW = 4
 
 
 def rows_of_slab(zz, xx, core, across):
@@ -545,7 +562,9 @@
     load_b.start()
     load_a.wait()
     load_b.wait()
-    wa_ref[...] = jnp.concatenate([raw_a[k] for k in range(raw_a.shape[0])], axis=1)
+    rows_a = jnp.concatenate([raw_a[k] for k in range(raw_a.shape[0])], axis=1)
+    for i in range(wa_ref.shape[0]):
+        wa_ref[i] = rows_a[i * FEW : (i + 1) * FEW, :]
     wb_ref[...] = jnp.concatenate([raw_b[k] for k in range(raw_b.shape[0])], axis=1)
     here.greeted(greeted)
     half = xt_ref.shape[0] // 2
@@ -714,7 +733,7 @@
         lambda *refs: gather_kernel(sizes, *refs),
         out_shape=(
             jax.ShapeDtypeStruct((down, *xt.shape), xt.dtype),
-            jax.ShapeDtypeStruct((depth, across, 2, rows_a, taps * width), wa.dtype),
+            jax.ShapeDtypeStruct((depth, across, 2, rows_a // FEW, FEW, taps * width), wa.dtype),
             jax.ShapeDtypeStruct((down, depth * across * 2 * rows_b, taps * width), wb.dtype),
         ),
         in_specs=[anywhere] * 3,
@@ -722,7 +741,7 @@
         scratch_shapes=[
             pltpu.VMEM(wa.shape, wa.dtype),
             pltpu.VMEM(wb.shape, wb.dtype),
-            pltpu.VMEM((rows_a, taps * width), wa.dtype),
+            pltpu.VMEM((rows_a // FEW, FEW, taps * width), wa.dtype),
             pltpu.VMEM((rows_b, taps * width), wb.dtype),
             dma((SITES,)), dma((SITES,)),
             dma((depth * across,)), dma((depth * across,)),
@@ -732,6 +751,7 @@
         compiler_params=pltpu.CompilerParams(
             collective_id=3, has_side_effects=True, vmem_limit_bytes=16 << 20
         ),
+        cost_estimate=pl.CostEstimate(flops=20_000_000_000, bytes_accessed=80_000_000, transcendentals=0),
         name="gathered_inputs",
     )(xt, wa, wb)
 
@@ -751,7 +771,8 @@
 ):
     sequences, length, taps = sizes
     channels, tokens = xt_ref.shape
-    chunks, chunk_rows, lanes = wa_ref.shape
+    chunks, few_count, _, lanes = wa_ref.shape
+    chunk_rows = few_count * FEW
     loads = 4
     each = chunks // loads
     arriving = [
@@ -800,7 +821,9 @@
 
     def relay(q, _):
         for i in range(group):
-            stage[i * chunk_rows : (i + 1) * chunk_rows, :] = wa_ref[q * group + i].astype(jnp.float32)
+            for r in range(few_count):
+                first = i * chunk_rows + r * FEW
+                stage[first : first + FEW, :] = wa_ref[q * group + i, r].astype(jnp.float32)
         at = pl.multiple_of(q * group * chunk_rows, group * chunk_rows)
         w_ref[pl.ds(at, group * chunk_rows), :] = stage[...].astype(jnp.bfloat16)
         return 0
@@ -837,7 +860,8 @@
 
 def first_conv(lengths, xt, wa, gain, keep, taps):
     channels, tokens = xt.shape
-    chunks, chunk_rows, lanes = wa.shape
+    chunks, few_count, _, lanes = wa.shape
+    chunk_rows = few_count * FEW
     sequences = lengths.shape[0]
     length = tokens // sequences
     bf, f32 = jnp.bfloat16, jnp.float32
@@ -974,6 +998,7 @@
         compiler_params=pltpu.CompilerParams(
             collective_id=4, has_side_effects=True, vmem_limit_bytes=16 << 20
         ),
+        cost_estimate=pl.CostEstimate(flops=10_000_000_000, bytes_accessed=40_000_000, transcendentals=0),
         name="spread_hidden",
     )(hidden, wb)
 

time: 152 us -> 148 us (0.974)
  local copies, waits for them, and re-layouts: 4.77 us -> 2.73 us
  Pallas kernels: 146 us -> 144 us
    unnamed x14 -> x12, local copies, waits for them, and re-layouts: 4.77 us -> 2.73 us
where the time goes in v5:
time: 148 us
  Pallas kernels  144 us (97%)
  local copies, waits for them, and re-layouts  2.73 us (2%)
    pallas_call x1, Pallas kernels, gathered_inputs(): pl.pallas_call(lambda *refs: gather_kernel(sizes, *refs), out_shape=(jax....  39.1 us
    pallas_call x1, Pallas kernels, total_moments(): pl.pallas_call(lambda *refs: total_kernel(mesh_sizes, pieces, *refs), out...  28.8 us
    pallas_call x1, Pallas kernels, spread_hidden(): pl.pallas_call(lambda *refs: spread_kernel(sizes, *refs), out_shape=(jax....  24.2 us
    pallas_call x1, Pallas kernels, inverse_factor(): pl.pallas_call(factor_kernel, out_shape=jax.ShapeDtypeStruct((width + GRO...  22.5 us
    pallas_call x1, Pallas kernels, first_conv(): pl.pallas_call(lambda *refs: conv_kernel((sequences, length, taps), *refs...  11.7 us
    pallas_call x1, Pallas kernels, embedding(): pl.pallas_call(lambda *refs: embed_kernel(taps, length, *refs), out_shape...  9.2 us
    pallas_call x1, Pallas kernels, from_partner(): pl.pallas_call(swap_kernel, out_shape=jax.ShapeDtypeStruct(own.shape, own...  4.49 us
    pallas_call x1, Pallas kernels, whitened_rows(): pl.pallas_call(lambda *refs: whiten_kernel(length, *refs), out_shape=(jax...  4 us

profile of v5, /device:TPU:1, one launch (start us, length us, event | category | flops | bytes accessed | tf_op | source)
XLA Modules:
  0.0 147.6 jit_solution(7498936806209468628)
XLA Ops:
  0.6 0.0 copy-start.3
  0.6 1.1 copy-done.3
  1.7 0.0 copy-start.4
  1.7 0.9 copy-done.4
  2.6 0.0 copy-start.5
  2.6 0.8 copy-done.5
  3.4 0.0 copy-start
  3.4 0.0 copy-start.1
  3.4 0.0 copy-start.2
  3.4 39.1 %gathered_inputs.1 = (bf16[4,320,1024]{2,1,0:T(8,128)(2,1)S(1)}, bf16[8,4,2,5,4,1600]{5,4,3,2,1,0:T(4,128)(2,1)S(1)}, bf16[4,512,1600]{2,1,0:T(8,128)(2,1)S(1)}) custom-call(bf16[320,1024]{1,0:T(8,128)(2,1)S(1)} %bitcast.13, bf16[5,20,320]{2,1,0:T(8,128)(2,1)S(1)} %copy-done.4, bf16[5,8,320]{2,1,0:T(8,128)(2,1)S(1)} %bitcast.14), custom_call_target="tpu_custom_call" | custom-call | flops 20000000000 | bytes 80000000 | tf_op jit(solution)/shard_map/gathered_inputs/pallas_call | solution.py:732
  42.5 0.0 copy-done
  42.5 0.0 copy-done.1
  42.5 0.0 copy-done.2
  42.5 11.7 %first_conv.1.refs_0_ = bf16[1024,640]{1,0:T(8,128)(2,1)S(1)} custom-call(s32[2]{0:T(128)S(1)} %copy-done.2, bf16[1280,1024]{1,0:T(8,128)(2,1)S(1)} %bitcast.9, bf16[64,5,4,1600]{3,2,1,0:T(4,128)(2,1)S(1)} %bitcast.8, f32[10,128]{1,0:T(8,128)S(1)} %bitcast.12, s32[2,1024]{1,0:T(2,128)S(1)} %copy-done.1), custom_call_target="tpu_custom_call" | custom-call | tf_op jit(solution)/shard_map/first_conv/pallas_call | solution.py:868
  54.2 24.2 %spread_hidden.1 = (bf16[4,288,640]{2,1,0:T(8,128)(2,1)S(1)}, bf16[4,512,1600]{2,1,0:T(8,128)(2,1)S(1)}) custom-call(bf16[1024,640]{1,0:T(8,128)(2,1)S(1)} %first_conv.1.refs_0_, bf16[4,512,1600]{2,1,0:T(8,128)(2,1)S(1)} %get-tuple-element.13.refs_1_), custom_call_target="tpu_custom_call", output_to_operand_aliasing={{1}: (1, {})} | custom-call | flops 10000000000 | bytes 40000000 | tf_op jit(solution)/shard_map/spread_hidden/pallas_call | solution.py:983
  78.5 9.2 %embedding.1 = (f32[2,256,512]{2,1,0:T(8,128)S(1)}, f32[2,1280,128]{2,1,0:T(8,128)S(1)}) custom-call(s32[2]{0:T(128)S(1)} %copy-done.2, bf16[4,288,640]{2,1,0:T(8,128)(2,1)S(1)} %get-tuple-element.14.refs_1_, bf16[4,512,1600]{2,1,0:T(8,128)(2,1)S(1)} %get-tuple-element.15.refs_2_), custom_call_target="tpu_custom_call" | custom-call | tf_op jit(solution)/shard_map/embedding/pallas_call | solution.py:1040
  87.7 28.8 %total_moments.1 = f32[16,80,128]{2,1,0:T(8,128)S(1)} custom-call(f32[2,16,80,128]{3,2,1,0:T(8,128)S(1)} %bitcast.11), custom_call_target="tpu_custom_call" | custom-call | tf_op jit(solution)/shard_map/total_moments/pallas_call | solution.py:187
  116.5 22.5 %inverse_factor.1.own_ref.refs_2_ = f32[520,512]{1,0:T(8,128)S(1)} custom-call(f32[1280,128]{1,0:T(8,128)S(1)} %bitcast.10), custom_call_target="tpu_custom_call" | custom-call | tf_op jit(solution)/shard_map/inverse_factor/pallas_call | solution.py:362
  139.0 4.5 %from_partner.1.refs_3_ = f32[520,512]{1,0:T(8,128)S(1)} custom-call(f32[520,512]{1,0:T(8,128)S(1)} %inverse_factor.1.own_ref.refs_2_), custom_call_target="tpu_custom_call" | custom-call | tf_op jit(solution)/shard_map/from_partner/pallas_call | solution.py:392
  143.5 4.0 %whitened_rows.1 = (f32[2,256,512]{2,1,0:T(8,128)}, f32[2,128]{1,0:T(2,128)}) custom-call(s32[2]{0:T(128)S(1)} %copy-done.2, f32[2,256,512]{2,1,0:T(8,128)S(1)} %get-tuple-element.16.refs_1_, f32[520,512]{1,0:T(8,128)S(1)} %inverse_factor.1.own_ref.refs_2_, f32[520,512]{1,0:T(8,128)S(1)} %from_partner.1.refs_3_), custom_call_target="tpu_custom_call" | custom-call | tf_op jit(solution)/shard_map/whitened_rows/pallas_call | solution.py:424
Async XLA Ops:
  0.6 1.1 copy-start.3
  1.7 0.9 copy-start.4
  2.6 0.8 copy-start.5
  3.4 39.1 %copy-start = (f32[1280]{0:T(1024)S(1)}, f32[1280]{0:T(1024)}, u32[]{:S(2)}) copy-start(f32[1280]{0:T(1024)} %param.9) | copy-start | bytes 15364
  3.4 39.1 %copy-start.1 = (s32[2,1024]{1,0:T(2,128)S(1)}, s32[2,1024]{1,0:T(2,128)}, u32[]{:S(2)}) copy-start(s32[2,1024]{1,0:T(2,128)} %refs_4_.1) | copy-start | bytes 24580
  3.4 39.1 %copy-start.2 = (s32[2]{0:T(128)S(1)}, s32[2]{0:T(128)}, u32[]{:S(2)}) copy-start(s32[2]{0:T(128)} %refs_0_.5) | copy-start | bytes 28

commit v6 on v5

--- a/solution.py
+++ b/solution.py
@@ -18,6 +18,7 @@
 AXES = (Z, X, CORE, Y)
 BLOCK = 128
 GROUP = 8
+LOWEST = -3.0e38
 
 
 def dot_of(a, b, dims, precision=HI):
@@ -226,7 +227,7 @@
     for p in range(count):
         j = GROUP * p
         v = groups[p]
-        cols = [splat_lane(v, j + a) for a in steps]
+        cols = [jnp.maximum(splat_lane(v, j + a), LOWEST) for a in steps]
         e = [[splat_row(cols[a], b) if b >= a else None for a in steps] for b in steps]
         panel = (lane >= j) & (lane < j + GROUP)
         rows = [
@@ -767,7 +768,7 @@
 
 def conv_kernel(
     sizes, lengths_ref, xt_ref, wa_hbm, gain_hbm, keep_hbm, out_ref,
-    wa_ref, gain_ref, keep_ref, n_ref, w_ref, stage, p_ref, cols, sems,
+    wa_ref, gain_ref, keep_ref, n_ref, w_ref, p_ref, cols, sems,
 ):
     sequences, length, taps = sizes
     channels, tokens = xt_ref.shape
@@ -811,21 +812,27 @@
     view = lax.broadcasted_iota(jnp.int32, (GROUP, tokens), 0)
     keep = jnp.where(view == 0, keep_ref[0:1, :], jnp.where(view == 1, keep_ref[1:2, :], 0))
     kept = jnp.where(position < limit, keep, 0).astype(jnp.float32)
+    stacked = [jnp.zeros((GROUP, tokens), jnp.float32) for _ in range(cols.shape[0])]
+    per = GROUP // 2
     for k in range(taps):
         move = k - taps // 2
         rolled = kept if move == 0 else pltpu.roll(kept, (-move) % tokens, 1)
         inside = (position + move >= 0) & (position + move < length)
-        cols[k] = jnp.where(inside, rolled, 0.0).T
+        rolled = jnp.where(inside, rolled, 0.0)
+        down = 2 * (k % per)
+        rolled = rolled if down == 0 else pltpu.roll(rolled, down, 0)
+        stacked[k // per] = jnp.where(view // 2 == k % per, rolled, stacked[k // per])
+    for i in range(cols.shape[0]):
+        cols[i] = stacked[i].T
 
     group = 4
 
     def relay(q, _):
-        for i in range(group):
-            for r in range(few_count):
-                first = i * chunk_rows + r * FEW
-                stage[first : first + FEW, :] = wa_ref[q * group + i, r].astype(jnp.float32)
+        pieces = [
+            wa_ref[q * group + i, r].astype(jnp.float32) for i in range(group) for r in range(few_count)
+        ]
         at = pl.multiple_of(q * group * chunk_rows, group * chunk_rows)
-        w_ref[pl.ds(at, group * chunk_rows), :] = stage[...].astype(jnp.bfloat16)
+        w_ref[pl.ds(at, group * chunk_rows), :] = jnp.concatenate(pieces, axis=0).astype(jnp.bfloat16)
         return 0
 
     for i in range(loads):
@@ -849,7 +856,8 @@
                 for k in range(taps):
                     first = PAD + r * ROWS + k - taps // 2
                     piece = p_ref[first : first + ROWS, k * width : (k + 1) * width]
-                    piece = piece * cols[k, pl.ds(start + r * ROWS, ROWS), v : v + 1]
+                    at = 2 * (k % per) + v
+                    piece = piece * cols[k // per, pl.ds(start + r * ROWS, ROWS), at : at + 1]
                     acc = piece if acc is None else acc + piece
                 hidden.append(gate(acc))
             out_ref[pl.ds(start + r * ROWS, ROWS), :] = jnp.concatenate(hidden, axis=1).astype(jnp.bfloat16)
@@ -876,9 +884,8 @@
             pltpu.VMEM(keep.shape, keep.dtype),
             pltpu.VMEM((tokens, channels), bf),
             pltpu.VMEM((channels, lanes), bf),
-            pltpu.VMEM((4 * chunk_rows, lanes), f32),
             pltpu.VMEM((length + 2 * PAD, lanes), f32),
-            pltpu.VMEM((taps, tokens, GROUP), f32),
+            pltpu.VMEM((-(-taps // (GROUP // 2)), tokens, GROUP), f32),
             pltpu.SemaphoreType.DMA((6,)),
         ],
         compiler_params=pltpu.CompilerParams(vmem_limit_bytes=40 << 20),

time: 148 us -> 143 us (0.966)
  Pallas kernels: 144 us -> 139 us
    pallas_call x1, Pallas kernels: 22.5 us -> 17.6 us  [inverse_factor(): pl.pallas_call(factor_kernel, out_shape=jax.ShapeDtypeStruct((width + GRO...]
where the time goes in v6:
time: 143 us; the launch traced here: 142 us
  Pallas kernels  139 us (97%)
  local copies, waits for them, and re-layouts  2.73 us (2%)
    pallas_call x1, Pallas kernels, gathered_inputs(): pl.pallas_call(lambda *refs: gather_kernel(sizes, *refs), out_shape=(jax....  39.1 us
    pallas_call x1, Pallas kernels, total_moments(): pl.pallas_call(lambda *refs: total_kernel(mesh_sizes, pieces, *refs), out...  28.9 us
    pallas_call x1, Pallas kernels, spread_hidden(): pl.pallas_call(lambda *refs: spread_kernel(sizes, *refs), out_shape=(jax....  24.2 us
    pallas_call x1, Pallas kernels, inverse_factor(): pl.pallas_call(factor_kernel, out_shape=jax.ShapeDtypeStruct((width + GRO...  17.6 us
    pallas_call x1, Pallas kernels, first_conv(): pl.pallas_call(lambda *refs: conv_kernel((sequences, length, taps), *refs...  11.2 us
    pallas_call x1, Pallas kernels, embedding(): pl.pallas_call(lambda *refs: embed_kernel(taps, length, *refs), out_shape...  9.21 us
    pallas_call x1, Pallas kernels, from_partner(): pl.pallas_call(swap_kernel, out_shape=jax.ShapeDtypeStruct(own.shape, own...  4.5 us
    pallas_call x1, Pallas kernels, whitened_rows(): pl.pallas_call(lambda *refs: whiten_kernel(length, *refs), out_shape=(jax...  4 us

profile of v6, /device:TPU:1, one launch (start us, length us, event | category | flops | bytes accessed | tf_op | source)
XLA Modules:
  0.0 142.3 jit_solution(14164365477856647809)
XLA Ops:
  0.6 0.0 copy-start.3
  0.6 1.1 copy-done.3
  1.7 0.0 copy-start.4
  1.7 0.9 copy-done.4
  2.6 0.0 copy-start.5
  2.6 0.8 copy-done.5
  3.4 0.0 copy-start
  3.4 0.0 copy-start.1
  3.4 0.0 copy-start.2
  3.4 39.1 %gathered_inputs.1 = (bf16[4,320,1024]{2,1,0:T(8,128)(2,1)S(1)}, bf16[8,4,2,5,4,1600]{5,4,3,2,1,0:T(4,128)(2,1)S(1)}, bf16[4,512,1600]{2,1,0:T(8,128)(2,1)S(1)}) custom-call(bf16[320,1024]{1,0:T(8,128)(2,1)S(1)} %bitcast.13, bf16[5,20,320]{2,1,0:T(8,128)(2,1)S(1)} %copy-done.4, bf16[5,8,320]{2,1,0:T(8,128)(2,1)S(1)} %bitcast.14), custom_call_target="tpu_custom_call" | custom-call | flops 20000000000 | bytes 80000000 | tf_op jit(solution)/shard_map/gathered_inputs/pallas_call | solution.py:733
  42.5 0.0 copy-done
  42.5 0.0 copy-done.1
  42.5 0.0 copy-done.2
  42.5 11.2 %first_conv.1.refs_0_ = bf16[1024,640]{1,0:T(8,128)(2,1)S(1)} custom-call(s32[2]{0:T(128)S(1)} %copy-done.2, bf16[1280,1024]{1,0:T(8,128)(2,1)S(1)} %bitcast.9, bf16[64,5,4,1600]{3,2,1,0:T(4,128)(2,1)S(1)} %bitcast.8, f32[10,128]{1,0:T(8,128)S(1)} %bitcast.12, s32[2,1024]{1,0:T(2,128)S(1)} %copy-done.1), custom_call_target="tpu_custom_call" | custom-call | tf_op jit(solution)/shard_map/first_conv/pallas_call | solution.py:876
  53.8 24.2 %spread_hidden.1 = (bf16[4,288,640]{2,1,0:T(8,128)(2,1)S(1)}, bf16[4,512,1600]{2,1,0:T(8,128)(2,1)S(1)}) custom-call(bf16[1024,640]{1,0:T(8,128)(2,1)S(1)} %first_conv.1.refs_0_, bf16[4,512,1600]{2,1,0:T(8,128)(2,1)S(1)} %get-tuple-element.13.refs_1_), custom_call_target="tpu_custom_call", output_to_operand_aliasing={{1}: (1, {})} | custom-call | flops 10000000000 | bytes 40000000 | tf_op jit(solution)/shard_map/spread_hidden/pallas_call | solution.py:990
  78.0 9.2 %embedding.1 = (f32[2,256,512]{2,1,0:T(8,128)S(1)}, f32[2,1280,128]{2,1,0:T(8,128)S(1)}) custom-call(s32[2]{0:T(128)S(1)} %copy-done.2, bf16[4,288,640]{2,1,0:T(8,128)(2,1)S(1)} %get-tuple-element.14.refs_1_, bf16[4,512,1600]{2,1,0:T(8,128)(2,1)S(1)} %get-tuple-element.15.refs_2_), custom_call_target="tpu_custom_call" | custom-call | tf_op jit(solution)/shard_map/embedding/pallas_call | solution.py:1047
  87.2 28.9 %total_moments.1 = f32[16,80,128]{2,1,0:T(8,128)S(1)} custom-call(f32[2,16,80,128]{3,2,1,0:T(8,128)S(1)} %bitcast.11), custom_call_target="tpu_custom_call" | custom-call | tf_op jit(solution)/shard_map/total_moments/pallas_call | solution.py:188
  116.2 17.6 %inverse_factor.1.own_ref.refs_2_ = f32[520,512]{1,0:T(8,128)S(1)} custom-call(f32[1280,128]{1,0:T(8,128)S(1)} %bitcast.10), custom_call_target="tpu_custom_call" | custom-call | tf_op jit(solution)/shard_map/inverse_factor/pallas_call | solution.py:363
  133.8 4.5 %from_partner.1.refs_3_ = f32[520,512]{1,0:T(8,128)S(1)} custom-call(f32[520,512]{1,0:T(8,128)S(1)} %inverse_factor.1.own_ref.refs_2_), custom_call_target="tpu_custom_call" | custom-call | tf_op jit(solution)/shard_map/from_partner/pallas_call | solution.py:393
  138.3 4.0 %whitened_rows.1 = (f32[2,256,512]{2,1,0:T(8,128)}, f32[2,128]{1,0:T(2,128)}) custom-call(s32[2]{0:T(128)S(1)} %copy-done.2, f32[2,256,512]{2,1,0:T(8,128)S(1)} %get-tuple-element.16.refs_1_, f32[520,512]{1,0:T(8,128)S(1)} %inverse_factor.1.own_ref.refs_2_, f32[520,512]{1,0:T(8,128)S(1)} %from_partner.1.refs_3_), custom_call_target="tpu_custom_call" | custom-call | tf_op jit(solution)/shard_map/whitened_rows/pallas_call | solution.py:425
Async XLA Ops:
  0.6 1.1 copy-start.3
  1.7 0.9 copy-start.4
  2.6 0.8 copy-start.5
  3.4 39.1 %copy-start = (f32[1280]{0:T(1024)S(1)}, f32[1280]{0:T(1024)}, u32[]{:S(2)}) copy-start(f32[1280]{0:T(1024)} %param.9) | copy-start | bytes 15364
  3.4 39.1 %copy-start.1 = (s32[2,1024]{1,0:T(2,128)S(1)}, s32[2,1024]{1,0:T(2,128)}, u32[]{:S(2)}) copy-start(s32[2,1024]{1,0:T(2,128)} %refs_4_.1) | copy-start | bytes 24580
  3.4 39.1 %copy-start.2 = (s32[2]{0:T(128)S(1)}, s32[2]{0:T(128)}, u32[]{:S(2)}) copy-start(s32[2]{0:T(128)} %refs_0_.5) | copy-start | bytes 28

commit v7 on v6

--- a/solution.py
+++ b/solution.py
@@ -19,6 +19,7 @@
 BLOCK = 128
 GROUP = 8
 LOWEST = -3.0e38
+PARTS = 5
 
 
 def dot_of(a, b, dims, precision=HI):
@@ -57,14 +58,17 @@
     half = BLOCK // 2
     for v in range(views):
         masked = emb_ref[v] * alive
-        for i in range(width // BLOCK):
-            wide = (i + 1) * BLOCK
-            strip = dot_of(
-                masked[:, i * BLOCK : wide], masked[:, :wide], ((0,), (0,))
-            )
-            for k in range(i + 1):
-                b = pairs.index((i, k))
-                out_ref[v, b * BLOCK : (b + 1) * BLOCK, :] = strip[:, k * BLOCK : (k + 1) * BLOCK]
+        side = 2 * BLOCK
+        for j in range(width // side):
+            wide = (j + 1) * side
+            strip = dot_of(masked[:, j * side : wide], masked[:, :wide], ((0,), (0,)))
+            for i in (2 * j, 2 * j + 1):
+                first = (i - 2 * j) * BLOCK
+                for k in range(i + 1):
+                    b = pairs.index((i, k))
+                    out_ref[v, b * BLOCK : (b + 1) * BLOCK, :] = strip[
+                        first : first + BLOCK, k * BLOCK : (k + 1) * BLOCK
+                    ]
         if out_ref.shape[1] > at:
             out_ref[v, at:, :] = jnp.zeros((out_ref.shape[1] - at, BLOCK), jnp.float32)
         sums = jnp.sum(masked, axis=0, keepdims=True)
@@ -182,7 +186,7 @@
     _, all_rows, lanes = parts.shape
     rows = all_rows // planes
     tiles = rows // GROUP
-    pieces = tuple(GROUP * (tiles // 4 + (1 if i < tiles % 4 else 0)) for i in range(4))
+    pieces = tuple(GROUP * (tiles // PARTS + (1 if i < tiles % PARTS else 0)) for i in range(PARTS))
     dma = pltpu.SemaphoreType.DMA
     vm = lambda *shape: pltpu.VMEM(shape, jnp.float32)
     return pl.pallas_call(
@@ -197,10 +201,10 @@
             vm(rows, lanes),
             vm(depth, rows, lanes),
             vm(rows, lanes),
-            dma((4,)), dma((4,)),
-            dma((4, planes)), dma((4, planes)),
-            dma((4, depth)), dma((4, depth)),
-            dma((4, planes)), dma((4, planes)),
+            dma((PARTS,)), dma((PARTS,)),
+            dma((PARTS, planes)), dma((PARTS, planes)),
+            dma((PARTS, depth)), dma((PARTS, depth)),
+            dma((PARTS, planes)), dma((PARTS, planes)),
         ],
         compiler_params=pltpu.CompilerParams(
             collective_id=1, has_side_effects=True, vmem_limit_bytes=32 << 20
@@ -381,12 +385,19 @@
     barrier = pltpu.get_barrier_semaphore()
     pl.semaphore_signal(barrier, inc=1, device_id=other, device_id_type=MESH_IDS)
     pl.semaphore_wait(barrier, 1)
-    copy = pltpu.make_async_remote_copy(
-        src_ref=own_ref, dst_ref=out_ref, send_sem=send, recv_sem=recv,
-        device_id=other, device_id_type=MESH_IDS,
-    )
-    copy.start()
-    copy.wait()
+    rows, width = own_ref.shape
+    side = width // 2
+    copies = []
+    for i, (first, last, wide) in enumerate(((0, side, side), (side, rows, width))):
+        part = (pl.ds(first, last - first), pl.ds(0, wide))
+        copy = pltpu.make_async_remote_copy(
+            src_ref=own_ref.at[part], dst_ref=out_ref.at[part], send_sem=send.at[i], recv_sem=recv.at[i],
+            device_id=other, device_id_type=MESH_IDS,
+        )
+        copy.start()
+        copies.append(copy)
+    for copy in copies:
+        copy.wait()
 
 
 def from_partner(own):
@@ -395,7 +406,7 @@
         out_shape=jax.ShapeDtypeStruct(own.shape, own.dtype),
         in_specs=[in_vmem()],
         out_specs=in_vmem(),
-        scratch_shapes=[pltpu.SemaphoreType.DMA, pltpu.SemaphoreType.DMA],
+        scratch_shapes=[pltpu.SemaphoreType.DMA((2,)), pltpu.SemaphoreType.DMA((2,))],
         compiler_params=pltpu.CompilerParams(
             collective_id=2, has_side_effects=True, vmem_limit_bytes=16 << 20
         ),

time: 143 us -> 143 us (level)
  no operation moved by 1% of the time
where the time goes in v7:
time: 143 us
  Pallas kernels  139 us (97%)
  local copies, waits for them, and re-layouts  2.73 us (2%)
    pallas_call x1, Pallas kernels, gathered_inputs(): pl.pallas_call(lambda *refs: gather_kernel(sizes, *refs), out_shape=(jax....  39.1 us
    pallas_call x1, Pallas kernels, total_moments(): pl.pallas_call(lambda *refs: total_kernel(mesh_sizes, pieces, *refs), out...  29.2 us
    pallas_call x1, Pallas kernels, spread_hidden(): pl.pallas_call(lambda *refs: spread_kernel(sizes, *refs), out_shape=(jax....  24.2 us
    pallas_call x1, Pallas kernels, inverse_factor(): pl.pallas_call(factor_kernel, out_shape=jax.ShapeDtypeStruct((width + GRO...  17.6 us
    pallas_call x1, Pallas kernels, first_conv(): pl.pallas_call(lambda *refs: conv_kernel((sequences, length, taps), *refs...  11.2 us
    pallas_call x1, Pallas kernels, embedding(): pl.pallas_call(lambda *refs: embed_kernel(taps, length, *refs), out_shape...  9.15 us
    pallas_call x1, Pallas kernels, from_partner(): pl.pallas_call(swap_kernel, out_shape=jax.ShapeDtypeStruct(own.shape, own...  4.68 us
    pallas_call x1, Pallas kernels, whitened_rows(): pl.pallas_call(lambda *refs: whiten_kernel(length, *refs), out_shape=(jax...  4 us

profile of v7, /device:TPU:1, one launch (start us, length us, event | category | flops | bytes accessed | tf_op | source)
XLA Modules:
  0.0 142.7 jit_solution(13639121038246410556)
XLA Ops:
  0.6 0.0 copy-start.3
  0.6 1.1 copy-done.3
  1.7 0.0 copy-start.4
  1.7 0.9 copy-done.4
  2.6 0.0 copy-start.5
  2.6 0.8 copy-done.5
  3.4 0.0 copy-start
  3.4 0.0 copy-start.1
  3.4 0.0 copy-start.2
  3.4 39.1 %gathered_inputs.1 = (bf16[4,320,1024]{2,1,0:T(8,128)(2,1)S(1)}, bf16[8,4,2,5,4,1600]{5,4,3,2,1,0:T(4,128)(2,1)S(1)}, bf16[4,512,1600]{2,1,0:T(8,128)(2,1)S(1)}) custom-call(bf16[320,1024]{1,0:T(8,128)(2,1)S(1)} %bitcast.13, bf16[5,20,320]{2,1,0:T(8,128)(2,1)S(1)} %copy-done.4, bf16[5,8,320]{2,1,0:T(8,128)(2,1)S(1)} %bitcast.14), custom_call_target="tpu_custom_call" | custom-call | flops 20000000000 | bytes 80000000 | tf_op jit(solution)/shard_map/gathered_inputs/pallas_call | solution.py:744
  42.5 0.0 copy-done
  42.5 0.0 copy-done.1
  42.5 0.0 copy-done.2
  42.5 11.2 %first_conv.1.refs_0_ = bf16[1024,640]{1,0:T(8,128)(2,1)S(1)} custom-call(s32[2]{0:T(128)S(1)} %copy-done.2, bf16[1280,1024]{1,0:T(8,128)(2,1)S(1)} %bitcast.9, bf16[64,5,4,1600]{3,2,1,0:T(4,128)(2,1)S(1)} %bitcast.8, f32[10,128]{1,0:T(8,128)S(1)} %bitcast.12, s32[2,1024]{1,0:T(2,128)S(1)} %copy-done.1), custom_call_target="tpu_custom_call" | custom-call | tf_op jit(solution)/shard_map/first_conv/pallas_call | solution.py:887
  53.8 24.2 %spread_hidden.1 = (bf16[4,288,640]{2,1,0:T(8,128)(2,1)S(1)}, bf16[4,512,1600]{2,1,0:T(8,128)(2,1)S(1)}) custom-call(bf16[1024,640]{1,0:T(8,128)(2,1)S(1)} %first_conv.1.refs_0_, bf16[4,512,1600]{2,1,0:T(8,128)(2,1)S(1)} %get-tuple-element.13.refs_1_), custom_call_target="tpu_custom_call", output_to_operand_aliasing={{1}: (1, {})} | custom-call | flops 10000000000 | bytes 40000000 | tf_op jit(solution)/shard_map/spread_hidden/pallas_call | solution.py:1001
  78.0 9.1 %embedding.1 = (f32[2,256,512]{2,1,0:T(8,128)S(1)}, f32[2,1280,128]{2,1,0:T(8,128)S(1)}) custom-call(s32[2]{0:T(128)S(1)} %copy-done.2, bf16[4,288,640]{2,1,0:T(8,128)(2,1)S(1)} %get-tuple-element.14.refs_1_, bf16[4,512,1600]{2,1,0:T(8,128)(2,1)S(1)} %get-tuple-element.15.refs_2_), custom_call_target="tpu_custom_call" | custom-call | tf_op jit(solution)/shard_map/embedding/pallas_call | solution.py:1058
  87.2 29.2 %total_moments.1 = f32[16,80,128]{2,1,0:T(8,128)S(1)} custom-call(f32[2,16,80,128]{3,2,1,0:T(8,128)S(1)} %bitcast.11), custom_call_target="tpu_custom_call" | custom-call | tf_op jit(solution)/shard_map/total_moments/pallas_call | solution.py:192
  116.4 17.6 %inverse_factor.1.own_ref.refs_2_ = f32[520,512]{1,0:T(8,128)S(1)} custom-call(f32[1280,128]{1,0:T(8,128)S(1)} %bitcast.10), custom_call_target="tpu_custom_call" | custom-call | tf_op jit(solution)/shard_map/inverse_factor/pallas_call | solution.py:367
  134.0 4.7 %from_partner.1.refs_3_ = f32[520,512]{1,0:T(8,128)S(1)} custom-call(f32[520,512]{1,0:T(8,128)S(1)} %inverse_factor.1.own_ref.refs_2_), custom_call_target="tpu_custom_call" | custom-call | tf_op jit(solution)/shard_map/from_partner/pallas_call | solution.py:404
  138.7 4.0 %whitened_rows.1 = (f32[2,256,512]{2,1,0:T(8,128)}, f32[2,128]{1,0:T(2,128)}) custom-call(s32[2]{0:T(128)S(1)} %copy-done.2, f32[2,256,512]{2,1,0:T(8,128)S(1)} %get-tuple-element.16.refs_1_, f32[520,512]{1,0:T(8,128)S(1)} %inverse_factor.1.own_ref.refs_2_, f32[520,512]{1,0:T(8,128)S(1)} %from_partner.1.refs_3_), custom_call_target="tpu_custom_call" | custom-call | tf_op jit(solution)/shard_map/whitened_rows/pallas_call | solution.py:436
Async XLA Ops:
  0.6 1.1 copy-start.3
  1.7 0.9 copy-start.4
  2.6 0.8 copy-start.5
  3.4 39.1 %copy-start = (f32[1280]{0:T(1024)S(1)}, f32[1280]{0:T(1024)}, u32[]{:S(2)}) copy-start(f32[1280]{0:T(1024)} %param.9) | copy-start | bytes 15364
  3.4 39.1 %copy-start.1 = (s32[2,1024]{1,0:T(2,128)S(1)}, s32[2,1024]{1,0:T(2,128)}, u32[]{:S(2)}) copy-start(s32[2,1024]{1,0:T(2,128)} %refs_4_.1) | copy-start | bytes 24580
  3.4 39.1 %copy-start.2 = (s32[2]{0:T(128)S(1)}, s32[2]{0:T(128)}, u32[]{:S(2)}) copy-start(s32[2]{0:T(128)} %refs_0_.5) | copy-start | bytes 28
